TPU v7x, 32 devices: a whole 2x2x4 slice. The times are simulated.
32 devices in a mesh: groups: 2 (over y), expert: 4 (over z), dp: 2 (over x), head: 2 (over core).
Axes of the slice: x: 2, y: 2, z: 4, core: 2. Of those that a mesh axis runs over, the one named last changes fastest.
Arguments:
- hidden: bfloat16 [4, 1024, 1536], P(('groups', 'dp'), ('expert', 'head')), parts along dimension 0, may hold values from -6 to 6
- modulation: float32 [4, 3, 1536], P(('groups', 'dp')), parts along dimension 0, may hold values from -3 to 3
- router_weight: float32 [1536, 16], replicated, may hold values from -0.15625 to 0.15625
- route_ids: int32 [4, 1024, 2], P(('groups', 'dp'), ('expert', 'head')), parts along dimension 0, may hold values from 0 to 15, all different within a row; in each aligned block of 128 rows (0 to 127, 128 to 255, ..., all dimensions but the last counted through in order) at most 32 rows name the same one
- gate_weight: bfloat16 [1536, 98304], P(None, ('expert', 'dp', 'head')), may hold values from -0.15625 to 0.15625
- up_weight: bfloat16 [1536, 98304], P(None, ('expert', 'dp', 'head')), may hold values from -0.15625 to 0.15625
- down_weight: bfloat16 [98304, 1536], P(('expert', 'dp', 'head')), may hold values from -0.078125 to 0.078125
- main_final: bfloat16 [1536, 16], replicated, may hold values from -0.15625 to 0.15625
- guide_qkv: bfloat16 [4, 1024, 6, 192], P(('groups', 'dp'), 'expert', 'head'), parts along dimension 0, may hold values from -6 to 6
- guide_out: bfloat16 [6, 64, 384], P('head'), may hold values from -0.3125 to 0.3125
- guide_final: bfloat16 [384, 16], replicated, may hold values from -0.3125 to 0.3125
- latent: float32 [4, 1024, 16], P(('groups', 'dp'), ('expert', 'head')), parts along dimension 0, may hold values from -6 to 6
- guidance: float32 [4], P(('groups', 'dp')), parts along dimension 0, may hold values from 1.5 to 3
- step_size: float32 [4], P(('groups', 'dp')), parts along dimension 0, may hold values from 0.1 to 0.5
Outputs:
- next_latent: float32 [4, 1024, 16], P(('groups', 'dp'), ('expert', 'head')), parts along dimension 0
There are 2 independent parts, one for each index of `groups`. A program takes and returns all parts, laid end to end along the dimension named above; an argument that names none is the same for every part. Nothing has to cross between parts.
Inputs may be any that keep to these rules, and one draw needn't show every extreme that they name: `route_ids`: each token names 2 different experts. In each aligned block of 128 tokens of a latent (tokens 128 j to 128 (j + 1) - 1), no expert is named by more than 32 routes, a bound that some block reaches.
All inputs are finite; a program needn't handle non-finite values.
Results may differ from a plain program's by a relative error of at most 0.0065.
Values may be sent and summed in bfloat16 or wider, within the bound.
No kernel may reach another device: no remote copies, remote signals or barrier semaphores. Data moves between devices by JAX's collectives and lax.ppermute only.
A program may use at most 192 MiB of HBM per device.

v0:
```python
import jax
import jax.numpy as jnp
from jax import lax
from jax.sharding import PartitionSpec as P

FF = 6144
EXPERTS = 16
TOP = 2
HD = 64
P_SIZE = 16


epsilon = 1e-06
score_scale = 8.0


def layer_norm(values):
    average = jnp.mean(values, axis=-1, keepdims=True)
    centered = values - average
    return centered / jnp.sqrt(jnp.mean(centered * centered, axis=-1, keepdims=True) + epsilon)


def unit_rows(values):
    return values / jnp.sqrt(jnp.mean(values * values, axis=-1, keepdims=True) + epsilon)


def route_slots(flat_ids, block_slots, per_index, copies):
    route_flat = flat_ids.reshape(-1)
    one_hot = (route_flat[:, None] == jnp.arange(EXPERTS, dtype=jnp.int32)[None, :]).astype(
        jnp.int32
    )
    earlier = jnp.cumsum(one_hot, axis=0) - one_hot
    earlier_count = jnp.sum(earlier * one_hot, axis=1)
    slot_pos = route_flat % per_index * block_slots + earlier_count
    targets = (
        route_flat[:, None] * copies + jnp.arange(copies, dtype=jnp.int32)[None, :]
    ) // per_index
    return (targets, slot_pos)


def expert_hidden(
    rows, positions, gate_weight, up_weight, my_expert, index_first, block_slots, copies
):
    owner_expert = (index_first + positions // block_slots) // copies
    keep_mask = (owner_expert == my_expert).astype(jnp.float32)[:, None]
    gate_vals = jnp.dot(rows, gate_weight, preferred_element_type=jnp.float32)
    up_vals = jnp.dot(rows, up_weight, preferred_element_type=jnp.float32)
    return (jax.nn.silu(gate_vals) * up_vals * keep_mask).astype(jnp.bfloat16)


def body(
    hidden,
    modulation,
    router_weight,
    route_ids,
    gate_weight,
    up_weight,
    down_weight,
    main_final,
    guide_qkv,
    guide_out,
    guide_final,
    latent,
    guidance,
    step_size,
):
    lat_dev, tok_dev, width = hidden.shape
    experts_axis = lax.axis_size("expert")
    group_size = lax.axis_size(("dp", "head"))
    slice_units = gate_weight.shape[1]
    index_units = slice_units * group_size
    if EXPERTS >= experts_axis:
        per_index = EXPERTS // experts_axis
        copies = 1
    else:
        per_index = 1
        copies = experts_axis // EXPERTS
    capacity = max(2, 2 * tok_dev * TOP // EXPERTS)
    block_slots = lat_dev * capacity
    slot_count = per_index * block_slots
    my_index = lax.axis_index("expert")
    my_member = lax.axis_index(("dp", "head"))
    my_expert = (my_index * index_units + my_member * slice_units) // FF
    index_first = my_index * per_index
    hidden_float = hidden.astype(jnp.float32)
    modulated = (
        layer_norm(hidden_float) * (1.0 + modulation[:, 1][:, None, :])
        + modulation[:, 0][:, None, :]
    ).astype(jnp.bfloat16)
    row_count = lat_dev * tok_dev
    flat_rows = modulated.reshape(row_count, width)
    logits = jnp.dot(flat_rows.astype(jnp.float32), router_weight, precision=lax.Precision.HIGHEST)
    flat_ids = route_ids.reshape(row_count, TOP)
    picked = jnp.take_along_axis(logits, flat_ids, axis=1)
    first_weight = jax.nn.sigmoid(picked[:, 0] - picked[:, 1])
    route_weight = jnp.stack([first_weight, 1.0 - first_weight], axis=1)
    route_count = row_count * TOP
    route_token = jnp.arange(route_count, dtype=jnp.int32) // TOP
    targets, slot_pos = route_slots(flat_ids, block_slots, per_index, copies)
    outgoing = jnp.zeros((experts_axis, slot_count, width), jnp.bfloat16)
    payload = jnp.broadcast_to(flat_rows[route_token][:, None, :], (route_count, copies, width))
    outgoing = outgoing.at[targets, slot_pos[:, None]].set(payload)
    received = lax.all_to_all(outgoing, "expert", split_axis=0, concat_axis=0, tiled=True)
    received_rows = received.reshape(experts_axis * slot_count, width)
    piece = lax.all_gather(received_rows, ("dp", "head"), axis=0, tiled=True)
    positions = jnp.arange(piece.shape[0], dtype=jnp.int32) % slot_count
    activated = expert_hidden(
        piece, positions, gate_weight, up_weight, my_expert, index_first, block_slots, copies
    )
    term = jnp.dot(activated, down_weight, preferred_element_type=jnp.float32)
    row_sums = lax.psum_scatter(
        lax.optimization_barrier(term.astype(jnp.bfloat16))
        .astype(jnp.float32)
        .astype(jnp.bfloat16),
        ("dp", "head"),
        scatter_dimension=0,
        tiled=True,
    ).astype(jnp.float32)
    returned = lax.all_to_all(
        row_sums.reshape(experts_axis, slot_count, width).astype(jnp.bfloat16),
        "expert",
        split_axis=0,
        concat_axis=0,
        tiled=True,
    ).astype(jnp.float32)
    gathered_back = returned[targets, slot_pos[:, None]]
    per_route = jnp.sum(gathered_back, axis=1).reshape(row_count, TOP, width)
    moe_out = jnp.sum(per_route * route_weight[:, :, None], axis=1)
    updated = hidden_float + modulation[:, 2][:, None, :] * moe_out.reshape(lat_dev, tok_dev, width)
    main_norm = layer_norm(updated).astype(jnp.bfloat16)
    main_velocity = jnp.dot(
        main_norm.reshape(row_count, width), main_final, preferred_element_type=jnp.float32
    ).reshape(lat_dev, tok_dev, P_SIZE)
    queries = unit_rows(guide_qkv[..., :HD].astype(jnp.float32)).astype(jnp.bfloat16)
    unit_keys = unit_rows(guide_qkv[..., HD : 2 * HD].astype(jnp.float32)).astype(jnp.bfloat16)
    key_value = jnp.concatenate([unit_keys, guide_qkv[..., 2 * HD :]], axis=-1)
    piece = lax.all_gather(key_value, "expert", axis=1, tiled=True)
    key_piece = piece[..., :HD]
    value_piece = piece[..., HD:]
    scores = jnp.einsum(
        "lqhc,lkhc->lhqk", queries, key_piece, preferred_element_type=jnp.float32
    ) * (score_scale / HD)
    weights = jnp.exp(scores - score_scale)
    weighted_sum = jnp.einsum(
        "lhqk,lkhc->lqhc",
        weights.astype(jnp.bfloat16),
        value_piece,
        preferred_element_type=jnp.float32,
    )
    weight_total = jnp.transpose(jnp.sum(weights, axis=-1), (0, 2, 1))
    weighted_sum, weight_total = (weighted_sum, weight_total)
    attended = (weighted_sum / weight_total[..., None]).astype(jnp.bfloat16)
    partial_mix = jnp.einsum(
        "lqhc,hcd->lqd", attended, guide_out, preferred_element_type=jnp.float32
    )
    guide_mix = lax.psum_scatter(
        partial_mix.astype(jnp.bfloat16), "head", scatter_dimension=1, tiled=True
    ).astype(jnp.float32)
    guide_norm = layer_norm(guide_mix).astype(jnp.bfloat16)
    guide_width = guide_norm.shape[-1]
    guide_velocity = jnp.dot(
        guide_norm.reshape(row_count, guide_width), guide_final, preferred_element_type=jnp.float32
    ).reshape(lat_dev, tok_dev, P_SIZE)
    guided = guide_velocity + guidance[:, None, None] * (main_velocity - guide_velocity)
    return latent + step_size[:, None, None] * guided


def solution(mesh):
    in_specs = (
        P(("groups", "dp"), ("expert", "head"), None),
        P(("groups", "dp"), None, None),
        P(),
        P(("groups", "dp"), ("expert", "head"), None),
        P(None, ("expert", "dp", "head")),
        P(None, ("expert", "dp", "head")),
        P(("expert", "dp", "head"), None),
        P(),
        P(("groups", "dp"), "expert", "head", None),
        P("head", None, None),
        P(),
        P(("groups", "dp"), ("expert", "head"), None),
        P(("groups", "dp")),
        P(("groups", "dp")),
    )
    out_specs = P(("groups", "dp"), ("expert", "head"), None)
    return jax.shard_map(body, mesh=mesh, in_specs=in_specs, out_specs=out_specs, check_vma=False)
```

profile of v0, /device:TPU:0, one launch (start us, length us, event | category | flops | bytes accessed | tf_op | source)
XLA Modules:
  0.0 396.7 jit_solution(16349027691568316379)
XLA Ops:
  8.6 1.1 convert_reduce_fusion
  9.8 1.2 fusion.27
  11.0 1.4 slice_reduce_fusion.2
  13.9 1.2 fusion.33
  15.2 1.3 gather_fusion
  16.6 19.7 %scatter_fusion = bf16[4,128,1536]{2,1,0:T(8,128)(2,1)S(1)} fusion(bf16[4,128,1536]{2,1,0:T(8,128)(2,1)S(1)} %broadcast_in_dim.8, s32[256]{0:T(256)S(1)} %bitcast.123, bf16[256,1536]{1,0:T(8,128)(2,1)S(1)} %gather_fusion), kind=kCustom, calls=%fused_computation.3 | custom fusion | bytes 2361344 | tf_op jit(solution)/shard_map/scatter | solution.py:102
  36.3 43.2 %all_to_all.10 = bf16[4,128,1536]{2,1,0:T(8,128)(2,1)} all-to-all(bf16[4,128,1536]{2,1,0:T(8,128)(2,1)S(1)} %scatter_fusion), channel_id=1, replica_groups=mesh['groups'=2,'expert'=4,'dp'=2,'head'=2] {'expert'}, dimensions={0} | all-to-all | bytes 3145728 | tf_op jit(solution)/shard_map/all_to_all | solution.py:103
  79.6 45.6 %all-gather.2.cloned.1.call-done = bf16[2048,1536]{1,0:T(8,128)(2,1)} async-done(((bf16[512,1536]{1,0:T(8,128)(2,1)}), bf16[2048,1536]{1,0:T(8,128)(2,1)}) %all-gather.2.cloned.1.call-update) | async-done | bytes 6291472 | tf_op jit(solution)/shard_map/all_gather | solution.py:105
  125.2 47.6 %fusion.78 = f32[2048,6144]{1,0:T(8,128)} fusion(bf16[2048,1536]{1,0:T(8,128)(2,1)} %all-gather.2.cloned.1.call-done, bf16[1536,6144]{1,0:T(8,128)(2,1)} %param.18), kind=kOutput, calls=%fused_computation.133 | convolution fusion | flops 38654705664 | bytes 75497472 | tf_op jit(solution)/shard_map/dot_general | solution.py:46
  172.7 55.4 %multiply_convert_fusion.clone.4 = bf16[2048,6144]{1,0:T(8,128)(2,1)} fusion(f32[2048,6144]{1,0:T(8,128)} %fusion.78, bf16[2048,1536]{1,0:T(8,128)(2,1)} %all-gather.2.cloned.1.call-done, bf16[1536,6144]{1,0:T(8,128)(2,1)} %param.19, f32[2048]{0:T(1024)S(1)} %fusion.63), kind=kOutput, calls=%fused_computation.4.clone.clone.clone.1 | convolution fusion | flops 38742786048 | bytes 100671488 | tf_op jit(solution)/shard_map/dot_general | solution.py:47
  228.1 48.0 %convolution_convert_fusion = bf16[2048,1536]{1,0:T(8,128)(2,1)} fusion(bf16[6144,1536]{1,0:T(8,128)(2,1)} %param.20, bf16[2048,6144]{1,0:T(8,128)(2,1)} %multiply_convert_fusion.clone.4), kind=kOutput, calls=%fused_computation.5 | convolution fusion | flops 38657851392 | bytes 50331648 | tf_op jit(solution)/shard_map/dot_general | solution.py:110
  277.3 19.7 %all_gather.6 = bf16[1,1024,3,128]{1,3,2,0:T(8,128)(2,1)S(1)} all-gather(bf16[1,256,3,128]{1,3,2,0:T(8,128)(2,1)S(1)} %pad_maximum_fusion), channel_id=1, replica_groups=mesh['groups'=2,'expert'=4,'dp'=2,'head'=2] {'expert'}, dimensions={1}, use_global_device_ids=true | all-gather | bytes 983040 | tf_op jit(solution)/shard_map/all_gather | solution.py:137
  297.0 38.2 %reduce-scatter.5.cloned.1.call-done = bf16[512,1536]{1,0:T(8,128)(2,1)} async-done(((bf16[2048,1536]{1,0:T(8,128)(2,1)}), bf16[512,1536]{1,0:T(8,128)(2,1)}) %reduce-scatter.5.cloned.1.call-update) | async-done | bytes 1572880 | tf_op jit(solution)/shard_map/reduce_scatter | solution.py:111
  335.2 4.6 %all-to-all-start.1 = ((bf16[4,128,1536]{2,1,0:T(8,128)(2,1)}), bf16[4,128,1536]{2,1,0:T(8,128)(2,1)}, u32[]{:S(2)}, u32[]{:S(2)}) async-start(bf16[4,128,1536]{2,1,0:T(8,128)(2,1)} %bitcast.125), calls=%async_computation.3 | async-start | bytes 3145728 | tf_op jit(solution)/shard_map/all_to_all | solution.py:119
  339.8 2.4 fusion
  342.2 3.6 fusion.7
  346.5 2.3 gather_fusion.2
  350.4 3.6 reduce-scatter.3.cloned.1.call-done
  357.2 19.5 %all-to-all-done.1 = bf16[4,128,1536]{2,1,0:T(8,128)(2,1)} async-done(((bf16[4,128,1536]{2,1,0:T(8,128)(2,1)}), bf16[4,128,1536]{2,1,0:T(8,128)(2,1)}, u32[]{:S(2)}, u32[]{:S(2)}) %all-to-all-start.1) | async-done | bytes 1572896 | tf_op jit(solution)/shard_map/all_to_all | solution.py:119
  376.7 1.8 convert_element_type.89
  378.5 4.0 gather_fusion.1
  382.4 2.3 reshape.505
  384.7 2.2 multiply_reduce_fusion
  386.9 1.2 fusion.38
  (75 shorter events, 9.5 us)
Async XLA Ops:
  7.4 334.8 %copy-start = (bf16[3,64,384]{2,1,0:T(8,128)(2,1)S(1)}, bf16[3,64,384]{2,1,0:T(8,128)(2,1)}, u32[]{:S(2)}) copy-start(bf16[3,64,384]{2,1,0:T(8,128)(2,1)} %param.23) | copy-start | bytes 442372
  7.4 117.8 %all-gather.2.cloned.1.call-start = ((), (), s32[]{:S(2)}) async-start(), calls=%async_computation.5 | async-start | bytes 7864320 | tf_op jit(solution)/shard_map/all_gather | solution.py:105
  15.2 21.1 %copy-start.1 = (bf16[128,1536]{1,0:T(8,128)(2,1)}, bf16[128,1536]{1,0:T(8,128)(2,1)S(1)}, u32[]{:S(2)}) copy-start(bf16[128,1536]{1,0:T(8,128)(2,1)S(1)} %fusion.33) | copy-start | bytes 1179652
  79.5 255.6 %reduce-scatter.5.cloned.1.call-start = ((), (), s32[]{:S(2)}) async-start(), calls=%async_computation.6 | async-start | bytes 7864320 | tf_op jit(solution)/shard_map/reduce_scatter | solution.py:111
  276.1 1.0 copy-start.5
  276.1 1.1 slice-start
  277.2 68.5 %copy-start.8 = (s32[1,128,2]{1,2,0:T(2,128)S(1)}, s32[1,128,2]{1,2,0:T(2,128)}, u32[]{:S(2)}) copy-start(s32[1,128,2]{1,2,0:T(2,128)} %param.17) | copy-start | bytes 3076
  277.3 68.8 %copy-start.2 = (bf16[128,1536]{1,0:T(8,128)(2,1)S(1)}, bf16[128,1536]{1,0:T(8,128)(2,1)}, u32[]{:S(2)}) copy-start(bf16[128,1536]{1,0:T(8,128)(2,1)} %copy-done.1) | copy-start | bytes 1179652
  277.3 68.8 %copy-start.6 = (f32[1536,16]{0,1:T(8,128)S(1)}, f32[1536,16]{0,1:T(8,128)}, u32[]{:S(2)}) copy-start(f32[1536,16]{0,1:T(8,128)} %param.16) | copy-start | bytes 294916
  335.2 41.5 %all-to-all-start.1 = ((bf16[4,128,1536]{2,1,0:T(8,128)(2,1)}), bf16[4,128,1536]{2,1,0:T(8,128)(2,1)}, u32[]{:S(2)}, u32[]{:S(2)}) async-start(bf16[4,128,1536]{2,1,0:T(8,128)(2,1)} %bitcast.125), calls=%async_computation.3 | async-start | bytes 3145728 | tf_op jit(solution)/shard_map/all_to_all | solution.py:119
  339.8 14.2 %reduce-scatter.3.cloned.1.call-start = ((), (), s32[]{:S(2)}) async-start(), calls=%async_computation.4 | async-start | bytes 294912 | tf_op jit(solution)/shard_map/reduce_scatter | solution.py:156
  346.5 9.6 %copy-start.10 = (bf16[384,16]{0,1:T(8,128)(2,1)S(1)}, bf16[384,16]{0,1:T(8,128)(2,1)}, u32[]{:S(2)}) copy-start(bf16[384,16]{0,1:T(8,128)(2,1)} %param.24) | copy-start | bytes 36868
  346.5 32.0 %copy-start.3 = (s32[256,1]{0,1:T(1,128)S(1)}, s32[256,1]{0,1:T(1,128)}, u32[]{:S(2)}) copy-start(s32[256,1]{0,1:T(1,128)} %get-tuple-element.13) | copy-start | bytes 3076
  378.5 8.4 %copy-start.7 = (f32[1536]{0:T(1024)S(1)}, f32[1536]{0:T(1024)}, u32[]{:S(2)}) copy-start(f32[1536]{0:T(1024)} %get-tuple-element.7) | copy-start | bytes 18436
  382.4 5.7 %copy-start.4 = (bf16[1,128,1536]{2,1,0:T(8,128)(2,1)S(1)}, bf16[1,128,1536]{2,1,0:T(8,128)(2,1)}, u32[]{:S(2)}) copy-start(bf16[1,128,1536]{2,1,0:T(8,128)(2,1)} %param.14) | copy-start | bytes 1179652
  382.4 5.9 %copy-start.9 = (bf16[1536,16]{0,1:T(8,128)(2,1)S(1)}, bf16[1536,16]{0,1:T(8,128)(2,1)}, u32[]{:S(2)}) copy-start(bf16[1536,16]{0,1:T(8,128)(2,1)} %param.21) | copy-start | bytes 147460
  382.4 5.9 %copy-start.11 = (f32[1,128,16]{1,2,0:T(8,128)S(1)}, f32[1,128,16]{1,2,0:T(8,128)}, u32[]{:S(2)}) copy-start(f32[1,128,16]{1,2,0:T(8,128)} %param.25) | copy-start | bytes 24580
Sparse Core Ops, SparseCore 0:
  79.6 45.4 all-gather.1
  276.3 58.8 reduce-scatter.4
Sparse Core Ops, SparseCore 1:
  345.8 8.1 reduce-scatter.2
where the time goes:
time: 397 us
  matrix products  159 us (40%)
  waiting for transfers between devices  107 us (27%)
  blocking collectives  62.9 us (16%)
  local copies, waits for them, and re-layouts  32.5 us (8%)
  between operations  16.5 us (4%)
  other arithmetic  14 us (4%)
  starting transfers between devices  4.64 us (1%)
    dot_general x1, matrix products, expert_hidden(): up_vals = jnp.dot(rows, up_weight, preferred_element_type=jnp.float32)  55.4 us
    dot_general x1, matrix products, body(): term = jnp.dot(activated, down_weight, preferred_element_type=jnp.float32)  48 us
    dot_general x1, matrix products, expert_hidden(): gate_vals = jnp.dot(rows, gate_weight, preferred_element_type=jnp.float32)  47.6 us
    all_gather x1, waiting for transfers between devices, body(): piece = lax.all_gather(received_rows, ('dp', 'head'), axis=0, tiled=True)  45.6 us
    all_to_all x1, blocking collectives, body(): lax.all_to_all(outgoing, 'expert', split_axis=0, concat_axis=0, tiled=True)  43.2 us
    reduce_scatter x1, waiting for transfers between devices, body(): lax.psum_scatter(lax.optimization_barrier(term.astype(jnp.bfloat16)).asty...  38.2 us
    all_gather x1, blocking collectives, body(): piece = lax.all_gather(key_value, 'expert', axis=1, tiled=True)  19.7 us
    scatter x1, local copies, waits for them, and re-layouts, body(): outgoing = outgoing.at[targets, slot_pos[:, None]].set(payload)  19.7 us
  transfers between devices with their start and end apart: 4, of which 4 were waited for; matrix products, arithmetic and copies ran while one was open for 3% of the time, Pallas kernels for 0%

commit v1 on v0

--- a/solution.py
+++ b/solution.py
@@ -1,7 +1,12 @@
+import functools
+
 import jax
 import jax.numpy as jnp
 from jax import lax
+from jax.experimental import pallas as pl
+from jax.experimental.pallas import tpu as pltpu
 from jax.sharding import PartitionSpec as P
+
 
 FF = 6144
 EXPERTS = 16
@@ -12,6 +17,10 @@
 
 epsilon = 1e-06
 score_scale = 8.0
+MIB = 1024 * 1024
+MEMBERS = ("expert", "dp", "head")
+CHUNK_A = [8, 12, 4, 0]
+CHUNK_B = [10, 14, 6, 2]
 
 
 def layer_norm(values):
@@ -22,6 +31,335 @@
 
 def unit_rows(values):
     return values / jnp.sqrt(jnp.mean(values * values, axis=-1, keepdims=True) + epsilon)
+
+
+def prep_kernel(chips, capacity, me_ref, ids_ref, own_ref, other_ref, mod_ref, rows_ref, code_ref, *out_refs):
+    tokens = own_ref.shape[1]
+    both = 2 * tokens
+    for i, ref in enumerate((own_ref, other_ref)):
+        rows_ref[i * tokens : (i + 1) * tokens, :] = (
+            layer_norm(ref[0].astype(jnp.float32)) * (1.0 + mod_ref[0, 1:2, :]) + mod_ref[0, 0:1, :]
+        ).astype(jnp.bfloat16)
+    me = me_ref[0]
+    experts = lax.broadcasted_iota(jnp.int32, (EXPERTS, both), 0)
+    named = [experts == ids_ref[j : j + 1, :] for j in range(TOP)]
+    tally = functools.reduce(jnp.logical_or, named).astype(jnp.float32).astype(jnp.bfloat16)
+    earlier = lax.broadcasted_iota(jnp.int32, (both, both), 0)
+    later = lax.broadcasted_iota(jnp.int32, (both, both), 1)
+    before = jnp.logical_and(earlier < later, jnp.logical_or(later < tokens, earlier >= tokens))
+    rank = jnp.dot(
+        tally, before.astype(jnp.float32).astype(jnp.bfloat16), preferred_element_type=jnp.float32
+    )
+    second = jnp.where(lax.broadcasted_iota(jnp.int32, (1, both), 1) >= tokens, capacity, 0)
+    slots = lax.broadcasted_iota(jnp.int32, (2 * chips * capacity, both), 0)
+    hit = None
+    for j in range(TOP):
+        own_rank = jnp.sum(jnp.where(named[j], rank, 0.0), axis=0, keepdims=True).astype(jnp.int32)
+        away = jnp.bitwise_xor(ids_ref[j : j + 1, :], me)
+        code = lax.shift_right_logical(away, 1) * (2 * capacity) + second + own_rank
+        code = jnp.where(jnp.bitwise_and(away, 1) == 0, code, -1)
+        code_ref[j : j + 1, :] = code
+        hit = slots == code if hit is None else jnp.logical_or(hit, slots == code)
+    select = hit.astype(jnp.float32).astype(jnp.bfloat16)
+    for p, out_ref in enumerate(out_refs):
+        out_ref[...] = jnp.dot(
+            select[2 * p * capacity : 2 * (p + 1) * capacity, :],
+            rows_ref[...],
+            preferred_element_type=jnp.float32,
+        ).astype(jnp.bfloat16)
+
+
+def prep(me, ids, own, other, modulation, chips, capacity):
+    tokens, width = own.shape[1:]
+    vmem = pl.BlockSpec(memory_space=pltpu.VMEM)
+    return pl.pallas_call(
+        functools.partial(prep_kernel, chips, capacity),
+        in_specs=[pl.BlockSpec(memory_space=pltpu.SMEM)] + [vmem] * 4,
+        out_specs=[vmem] * (2 + chips),
+        out_shape=[
+            jax.ShapeDtypeStruct((2 * tokens, width), jnp.bfloat16),
+            jax.ShapeDtypeStruct((TOP, 2 * tokens), jnp.int32),
+        ]
+        + [jax.ShapeDtypeStruct((2 * capacity, width), jnp.bfloat16)] * chips,
+        compiler_params=pltpu.CompilerParams(vmem_limit_bytes=24 * MIB),
+        cost_estimate=pl.CostEstimate(
+            flops=8 * chips * capacity * tokens * width,
+            bytes_accessed=4 * chips * capacity * width,
+            transcendentals=0,
+        ),
+        name="prep",
+    )(me, ids, own, other, modulation)
+
+
+def ffn_kernel(blocks, *refs):
+    row_refs = refs[:blocks]
+    gate_ref, up_ref, down_ref = refs[blocks : blocks + 3]
+    out_refs = refs[blocks + 3 : 2 * blocks + 3]
+    rows, total = refs[2 * blocks + 3 :]
+    step, last = pl.program_id(0), pl.num_programs(0) - 1
+    capacity = row_refs[0].shape[0]
+
+    @pl.when(step == 0)
+    def _():
+        for i in range(blocks):
+            rows[i * capacity : (i + 1) * capacity, :] = row_refs[i][...]
+
+    gate_vals = jnp.dot(rows[...], gate_ref[...], preferred_element_type=jnp.float32)
+    up_vals = jnp.dot(rows[...], up_ref[...], preferred_element_type=jnp.float32)
+    activated = (gate_vals / (1.0 + jnp.exp(-gate_vals)) * up_vals).astype(jnp.bfloat16)
+    term = jnp.dot(activated, down_ref[...], preferred_element_type=jnp.float32)
+
+    @pl.when(step == 0)
+    def _():
+        total[...] = term
+
+    @pl.when(jnp.logical_and(step > 0, step < last))
+    def _():
+        total[...] += term
+
+    @pl.when(step == last)
+    def _():
+        done = (total[...] + term).astype(jnp.bfloat16)
+        for i in range(blocks):
+            out_refs[i][...] = done[i * capacity : (i + 1) * capacity, :]
+
+
+def ffn(row_blocks, gate_weight, up_weight, down_weight):
+    blocks = len(row_blocks)
+    capacity, width = row_blocks[0].shape
+    units = gate_weight.shape[1]
+    tile = 1024 if units % 1024 == 0 else units
+    rows = blocks * capacity
+    whole = pl.BlockSpec((capacity, width), lambda s: (0, 0))
+    return pl.pallas_call(
+        functools.partial(ffn_kernel, blocks),
+        grid=(units // tile,),
+        in_specs=[whole] * blocks
+        + [
+            pl.BlockSpec((width, tile), lambda s: (0, s)),
+            pl.BlockSpec((width, tile), lambda s: (0, s)),
+            pl.BlockSpec((tile, width), lambda s: (s, 0)),
+        ],
+        out_specs=[whole] * blocks,
+        out_shape=[jax.ShapeDtypeStruct((capacity, width), jnp.bfloat16)] * blocks,
+        scratch_shapes=[pltpu.VMEM((rows, width), jnp.bfloat16), pltpu.VMEM((rows, width), jnp.float32)],
+        compiler_params=pltpu.CompilerParams(vmem_limit_bytes=56 * MIB),
+        cost_estimate=pl.CostEstimate(
+            flops=6 * rows * width * units,
+            bytes_accessed=6 * width * units,
+            transcendentals=rows * units,
+        ),
+        name="ffn",
+    )(*row_blocks, gate_weight, up_weight, down_weight)
+
+
+def attend_kernel(pieces, head_ref, q_ref, *refs):
+    kv_refs = refs[:pieces]
+    out_ref, keep_ref, send_ref, mix = refs[pieces:]
+    heads, queries = q_ref.shape[:2]
+    acc = None
+    for h in range(heads):
+        q = q_ref[h]
+        sums, weighted = None, None
+        for kv_ref in kv_refs:
+            scores = lax.dot_general(
+                q, kv_ref[h, :, :HD], (((1,), (1,)), ((), ())), preferred_element_type=jnp.float32
+            ) * (score_scale / HD)
+            weights = jnp.exp(scores - score_scale)
+            part = jnp.sum(weights, axis=-1, keepdims=True)
+            value = jnp.dot(
+                weights.astype(jnp.bfloat16), kv_ref[h, :, HD:], preferred_element_type=jnp.float32
+            )
+            sums = part if sums is None else sums + part
+            weighted = value if weighted is None else weighted + value
+        attended = (weighted / sums).astype(jnp.bfloat16)
+        term = jnp.dot(attended, out_ref[h], preferred_element_type=jnp.float32)
+        acc = term if acc is None else acc + term
+    mix[...] = acc
+    half = queries // 2
+    mine = head_ref[0]
+    keep_ref[...] = mix[pl.ds(pl.multiple_of(mine * half, half), half), :]
+    send_ref[...] = mix[pl.ds(pl.multiple_of((1 - mine) * half, half), half), :].astype(jnp.bfloat16)
+
+
+def attend(head, queries, kv_pieces, guide_out):
+    heads, count, _ = queries.shape
+    keys = sum(piece.shape[1] for piece in kv_pieces)
+    wide = guide_out.shape[-1]
+    vmem = pl.BlockSpec(memory_space=pltpu.VMEM)
+    return pl.pallas_call(
+        functools.partial(attend_kernel, len(kv_pieces)),
+        in_specs=[pl.BlockSpec(memory_space=pltpu.SMEM)] + [vmem] * (2 + len(kv_pieces)),
+        out_specs=[vmem, vmem],
+        out_shape=[
+            jax.ShapeDtypeStruct((count // 2, wide), jnp.float32),
+            jax.ShapeDtypeStruct((count // 2, wide), jnp.bfloat16),
+        ],
+        scratch_shapes=[pltpu.VMEM((count, wide), jnp.float32)],
+        compiler_params=pltpu.CompilerParams(vmem_limit_bytes=32 * MIB),
+        cost_estimate=pl.CostEstimate(
+            flops=4 * heads * count * keys * HD,
+            bytes_accessed=4 * heads * keys * HD,
+            transcendentals=heads * count * keys,
+        ),
+        name="attend",
+    )(head, queries, *kv_pieces, guide_out)
+
+
+def combine_kernel(blocks, code_ref, first_ref, *refs):
+    row_refs, (keep_ref, send_ref, rows) = refs[:blocks], refs[blocks:]
+    size = row_refs[0].shape[0]
+    for i in range(blocks):
+        rows[i * size : (i + 1) * size, :] = row_refs[i][...]
+    both = code_ref.shape[0]
+    tokens = both // 2
+    slots = lax.broadcasted_iota(jnp.int32, (tokens, blocks * size), 1)
+    for i, out_ref in enumerate((keep_ref, send_ref)):
+        part = slice(i * tokens, (i + 1) * tokens)
+        first = first_ref[part, :]
+        total = None
+        for j, weight in enumerate((first, 1.0 - first)):
+            pick = (slots == code_ref[part, j : j + 1]).astype(jnp.float32).astype(jnp.bfloat16)
+            term = weight * jnp.dot(pick, rows[...], preferred_element_type=jnp.float32)
+            total = term if total is None else total + term
+        out_ref[...] = total.astype(out_ref.dtype)
+
+
+def combine(row_blocks, code, first):
+    blocks = len(row_blocks)
+    size, width = row_blocks[0].shape
+    tokens = code.shape[0] // 2
+    vmem = pl.BlockSpec(memory_space=pltpu.VMEM)
+    return pl.pallas_call(
+        functools.partial(combine_kernel, blocks),
+        in_specs=[vmem] * (2 + blocks),
+        out_specs=[vmem] * 2,
+        out_shape=[
+            jax.ShapeDtypeStruct((tokens, width), jnp.float32),
+            jax.ShapeDtypeStruct((tokens, width), jnp.bfloat16),
+        ],
+        scratch_shapes=[pltpu.VMEM((blocks * size, width), jnp.bfloat16)],
+        compiler_params=pltpu.CompilerParams(vmem_limit_bytes=24 * MIB),
+        cost_estimate=pl.CostEstimate(
+            flops=8 * tokens * blocks * size * width,
+            bytes_accessed=2 * blocks * size * width,
+            transcendentals=0,
+        ),
+        name="combine",
+    )(code, first, *row_blocks)
+
+
+def finish_kernel(
+    keep_moe_ref, got_moe_ref, hidden_ref, mod_ref, final_ref, keep_ref, got_ref, guide_final_ref, latent_ref,
+    guidance_ref, step_ref, out_ref
+):
+    moe_out = keep_moe_ref[...] + got_moe_ref[...].astype(jnp.float32)
+    updated = hidden_ref[0].astype(jnp.float32) + mod_ref[0, 2:3, :] * moe_out
+    main_velocity = jnp.dot(
+        layer_norm(updated).astype(jnp.bfloat16), final_ref[...], preferred_element_type=jnp.float32
+    )
+    guide_mix = keep_ref[...] + got_ref[...].astype(jnp.float32)
+    guide_velocity = jnp.dot(
+        layer_norm(guide_mix).astype(jnp.bfloat16), guide_final_ref[...], preferred_element_type=jnp.float32
+    )
+    guided = guide_velocity + guidance_ref[0] * (main_velocity - guide_velocity)
+    out_ref[0] = latent_ref[0] + step_ref[0] * guided
+
+
+def finish(keep_moe, got_moe, hidden, modulation, main_final, keep, got, guide_final, latent, guidance, step_size):
+    vmem = pl.BlockSpec(memory_space=pltpu.VMEM)
+    smem = pl.BlockSpec(memory_space=pltpu.SMEM)
+    return pl.pallas_call(
+        finish_kernel,
+        in_specs=[vmem] * 9 + [smem] * 2,
+        out_specs=vmem,
+        out_shape=jax.ShapeDtypeStruct(latent.shape, latent.dtype),
+        compiler_params=pltpu.CompilerParams(vmem_limit_bytes=16 * MIB),
+        cost_estimate=pl.CostEstimate(flops=hidden.size * 64, bytes_accessed=hidden.size * 8, transcendentals=0),
+        name="finish",
+    )(keep_moe, got_moe, hidden, modulation, main_final, keep, got, guide_final, latent, guidance, step_size)
+
+
+def direct_body(
+    hidden,
+    modulation,
+    router_weight,
+    route_ids,
+    gate_weight,
+    up_weight,
+    down_weight,
+    main_final,
+    guide_qkv,
+    guide_out,
+    guide_final,
+    latent,
+    guidance,
+    step_size,
+):
+    return direct_step(
+        hidden, modulation, router_weight, route_ids, gate_weight, up_weight, down_weight, main_final,
+        guide_qkv, guide_out, guide_final, latent, guidance, step_size,
+    )
+
+
+def direct_step(
+    hidden, modulation, router_weight, route_ids, gate_weight, up_weight, down_weight, main_final, guide_qkv,
+    guide_out, guide_final, latent, guidance, step_size,
+):
+    tokens = hidden.shape[1]
+    devices = lax.axis_size(MEMBERS)
+    capacity = max(2, 2 * tokens * TOP // EXPERTS)
+    me = lax.axis_index(MEMBERS).astype(jnp.int32)[None]
+    head = lax.axis_index("head").astype(jnp.int32)[None]
+
+    def swap(block, k):
+        if k == 0:
+            return block
+        return lax.ppermute(block, MEMBERS, [(i, i ^ k) for i in range(devices)])
+
+    other = swap(hidden, 1)
+    ids = route_ids[0].T
+    ids = jnp.concatenate([ids, swap(ids, 1)], axis=1)
+    rows, code, *outgoing = prep(me, ids, hidden, other, modulation, devices // 2, capacity)
+    rows_a = [swap(outgoing[k // 2], k) for k in CHUNK_A]
+
+    qkv = jnp.transpose(guide_qkv[0], (1, 0, 2))
+    queries = unit_rows(qkv[..., :HD].astype(jnp.float32)).astype(jnp.bfloat16)
+    keys = unit_rows(qkv[..., HD : 2 * HD].astype(jnp.float32)).astype(jnp.bfloat16)
+    kv = jnp.concatenate([keys, qkv[..., 2 * HD :]], axis=-1)
+    logits = jnp.dot(rows.astype(jnp.float32), router_weight, precision=lax.Precision.HIGHEST)
+    named = jnp.arange(EXPERTS, dtype=jnp.int32)[None, :]
+    picked = [
+        jnp.sum(jnp.where(ids[j][:, None] == named, logits, 0.0), axis=1, keepdims=True) for j in range(TOP)
+    ]
+    first = jax.nn.sigmoid(picked[0] - picked[1])
+    slot_codes = code.T
+
+    rows_a, second, kv, first, slot_codes, queries = lax.optimization_barrier(
+        (rows_a, [outgoing[k // 2] for k in CHUNK_B], kv, first, slot_codes, queries)
+    )
+    rows_b = [swap(block, k) for block, k in zip(second, CHUNK_B)]
+    near = swap(kv, 4)
+
+    done_a = ffn(rows_a, gate_weight, up_weight, down_weight)
+    done_a, kv_far = lax.optimization_barrier((done_a, kv))
+    back_a = [swap(block, k) for block, k in zip(done_a, CHUNK_A)]
+    far = swap(kv_far, 8)
+
+    done_b = ffn(rows_b, gate_weight, up_weight, down_weight)
+    done_b, far, near, queries = lax.optimization_barrier((done_b, far, near, queries))
+    back_b = [swap(block, k) for block, k in zip(done_b, CHUNK_B)]
+    relayed = swap(far, 4)
+
+    keep, send = attend(head, queries, [kv, near, far, relayed], guide_out)
+    got = swap(send, 1)
+
+    back = dict(zip(CHUNK_A + CHUNK_B, back_a + back_b))
+    keep_moe, send_moe = combine([back[k] for k in sorted(back)], slot_codes, first)
+    got_moe = swap(send_moe, 1)
+    return finish(
+        keep_moe, got_moe, hidden, modulation, main_final, keep, got, guide_final, latent, guidance, step_size
+    )
 
 
 def route_slots(flat_ids, block_slots, per_index, copies):
@@ -48,7 +386,7 @@
     return (jax.nn.silu(gate_vals) * up_vals * keep_mask).astype(jnp.bfloat16)
 
 
-def body(
+def spread_body(
     hidden,
     modulation,
     router_weight,
@@ -148,7 +486,6 @@
         preferred_element_type=jnp.float32,
     )
     weight_total = jnp.transpose(jnp.sum(weights, axis=-1), (0, 2, 1))
-    weighted_sum, weight_total = (weighted_sum, weight_total)
     attended = (weighted_sum / weight_total[..., None]).astype(jnp.bfloat16)
     partial_mix = jnp.einsum(
         "lqhc,hcd->lqd", attended, guide_out, preferred_element_type=jnp.float32
@@ -183,4 +520,8 @@
         P(("groups", "dp")),
     )
     out_specs = P(("groups", "dp"), ("expert", "head"), None)
+    sizes = dict(mesh.shape)
+    members = sizes["expert"] * sizes["dp"] * sizes["head"]
+    direct = members == EXPERTS and sizes["expert"] == 4 and sizes["head"] == 2
+    body = direct_body if direct else spread_body
     return jax.shard_map(body, mesh=mesh, in_specs=in_specs, out_specs=out_specs, check_vma=False)

time: 397 us -> 134 us (0.34)
  matrix products: 159 us -> 0.74 us
  waiting for transfers between devices: 107 us -> 27.8 us
  blocking collectives: 62.9 us -> 0 us
  Pallas kernels: 0 us -> 55.7 us
  starting transfers between devices: 4.64 us -> 31.9 us
  local copies, waits for them, and re-layouts: 32.5 us -> 14 us
  between operations: 16.5 us -> 1.56 us
  other arithmetic: 14 us -> 2.28 us
    dot_general x8 -> x1, matrix products: 159 us -> 0.74 us  [direct_step(): jnp.dot(rows.astype(jnp.float32), router_weight, precision=lax.Precision....]
    pallas_call x0 -> x6, Pallas kernels: none -> 55.7 us  [the longest x2 49.6 us: ffn(): pl.pallas_call(functools.partial(ffn_kernel, blocks), grid=(units // tile...]
    all_gather x1 -> x0, waiting for transfers between devices: 45.6 us -> none  [body(): piece = lax.all_gather(received_rows, ('dp', 'head'), axis=0, tiled=True)]
    all_to_all x1 -> x0, blocking collectives: 43.2 us -> none  [body(): lax.all_to_all(outgoing, 'expert', split_axis=0, concat_axis=0, tiled=True)]
    reduce_scatter x2 -> x0, waiting for transfers between devices: 41.7 us -> none  [the longest x1 38.2 us: body(): lax.psum_scatter(lax.optimization_barrier(term.astype(jnp.bfloat16)).asty...]
    ppermute x0 -> x21, starting transfers between devices: none -> 31.9 us  [swap(): return lax.ppermute(block, MEMBERS, [(i, i ^ k) for i in range(devices)])]
    ppermute x0 -> x21, waiting for transfers between devices: none -> 27.8 us  [swap(): return lax.ppermute(block, MEMBERS, [(i, i ^ k) for i in range(devices)])]
    all_gather x1 -> x0, blocking collectives: 19.7 us -> none  [body(): piece = lax.all_gather(key_value, 'expert', axis=1, tiled=True)]
  transfers between devices with their start and end apart: 4 -> 21, of which waited for: 4 -> 5; matrix products, arithmetic and copies ran while one was open for 3% -> 4% of each run, Pallas kernels for 0% -> 39%
where the time goes in v1:
time: 134 us
  Pallas kernels  55.7 us (42%)
  starting transfers between devices  31.9 us (24%)
  waiting for transfers between devices  27.8 us (21%)
  local copies, waits for them, and re-layouts  14 us (10%)
  other arithmetic  2.28 us (2%)
  between operations  1.56 us (1%)
    pallas_call x2, Pallas kernels, ffn(): pl.pallas_call(functools.partial(ffn_kernel, blocks), grid=(units // tile...  49.6 us
    ppermute x21, starting transfers between devices, swap(): return lax.ppermute(block, MEMBERS, [(i, i ^ k) for i in range(devices)])  31.9 us
    ppermute x21, waiting for transfers between devices, swap(): return lax.ppermute(block, MEMBERS, [(i, i ^ k) for i in range(devices)])  27.8 us
    unnamed x57, local copies, waits for them, and re-layouts  13 us
  transfers between devices with their start and end apart: 21, of which 5 were waited for; matrix products, arithmetic and copies ran while one was open for 4% of the time, Pallas kernels for 39%

profile of v1, /device:TPU:0, one launch (start us, length us, event | category | flops | bytes accessed | tf_op | source)
XLA Modules:
  0.0 134.0 jit_solution(9750725676858541551)
XLA Ops:
  0.6 1.1 copy.24
  4.8 1.0 copy-done.2
  5.8 1.8 %prep.1 = (bf16[256,1536]{1,0:T(8,128)(2,1)S(1)}, s32[2,256]{1,0:T(2,128)S(1)}, bf16[64,1536]{1,0:T(8,128)(2,1)S(1)}, bf16[64,1536]{1,0:T(8,128)(2,1)S(1)}, bf16...) custom-call(s32[1]{0:T(128)} %bitcast.me_ref, ...), custom_call_target="tpu_custom_call" | custom-call | flops 402653184 | bytes 1572864 | tf_op jit(solution)/shard_map/prep/pallas_call | solution.py:75
  8.2 4.0 %collective-permute-start.2 = (bf16[64,1536]{1,0:T(8,128)(2,1)S(1)}, bf16[64,1536]{1,0:T(8,128)(2,1)S(1)}, u32[]{:S(2)}, u32[]{:S(2)}) collective-permute-start(bf16[64,1536]{1,0:T(8,128)(2,1)S(1)} %get-tuple-element.51), channel_id=1, source_target_pairs={{0,8},{1,9},{2,10},{3,11},{4,12},{5,13},{6,14},{7,15},{8,0},{9,1},... | collective-permute-start | bytes 589832 | tf_op jit(solution)/shard_map/ppermute | solution.py:318
  12.3 1.3 %collective-permute-start.3 = (bf16[64,1536]{1,0:T(8,128)(2,1)S(1)}, bf16[64,1536]{1,0:T(8,128)(2,1)S(1)}, u32[]{:S(2)}, u32[]{:S(2)}) collective-permute-start(bf16[64,1536]{1,0:T(8,128)(2,1)S(1)} %get-tuple-element.52), channel_id=1, source_target_pairs={{0,12},{1,13},{2,14},{3,15},{4,8},{5,9},{6,10},{7,11},{8,4},{9,5},... | collective-permute-start | bytes 589832 | tf_op jit(solution)/shard_map/ppermute | solution.py:318
  14.7 11.7 %collective-permute-done.2.refs_0_ = bf16[64,1536]{1,0:T(8,128)(2,1)S(1)} collective-permute-done((bf16[64,1536]{1,0:T(8,128)(2,1)S(1)}, bf16[64,1536]{1,0:T(8,128)(2,1)S(1)}, u32[]{:S(2)}, u32[]{:S(2)}) %collective-permute-start.2) | collective-permute-done | bytes 196640 | tf_op jit(solution)/shard_map/ppermute | solution.py:318
  27.3 6.4 %collective-permute-start.5 = (bf16[64,1536]{1,0:T(8,128)(2,1)S(1)}, bf16[64,1536]{1,0:T(8,128)(2,1)S(1)}, u32[]{:S(2)}, u32[]{:S(2)}) collective-permute-start(bf16[64,1536]{1,0:T(8,128)(2,1)S(1)} %get-tuple-element.73), channel_id=1, source_target_pairs={{0,10},{1,11},{2,8},{3,9},{4,14},{5,15},{6,12},{7,13},{8,2},{9,3},... | collective-permute-start | bytes 589832 | tf_op jit(solution)/shard_map/ppermute | solution.py:318
  34.3 1.5 %collective-permute-start.8 = (bf16[64,1536]{1,0:T(8,128)(2,1)S(1)}, bf16[64,1536]{1,0:T(8,128)(2,1)S(1)}, u32[]{:S(2)}, u32[]{:S(2)}) collective-permute-start(bf16[64,1536]{1,0:T(8,128)(2,1)S(1)} %get-tuple-element.76), channel_id=1, source_target_pairs={{0,2},{1,3},{2,0},{3,1},{4,6},{5,7},{6,4},{7,5},{8,10},{9,11},{10,... | collective-permute-start | bytes 589832 | tf_op jit(solution)/shard_map/ppermute | solution.py:318
  35.7 1.8 %collective-permute-start.10 = (bf16[3,256,128]{2,1,0:T(8,128)(2,1)S(1)}, bf16[3,256,128]{2,1,0:T(8,128)(2,1)S(1)}, u32[]{:S(2)}, u32[]{:S(2)}) collective-permute-start(bf16[3,256,128]{2,1,0:T(8,128)(2,1)S(1)} %pad_maximum_fusion.refs_0_), channel_id=1, source_target_pairs={{0,4},{1,5},{2,6},{3,7},{4,0},{5,1},{6,2},{7,3},{8,12},{9,13},{10,... | collective-permute-start | bytes 589832 | tf_op jit(solution)/shard_map/ppermute | solution.py:318
  37.6 24.9 %ffn.2 = (bf16[64,1536]{1,0:T(8,128)(2,1)}, bf16[64,1536]{1,0:T(8,128)(2,1)}, bf16[64,1536]{1,0:T(8,128)(2,1)}, bf16[64,1536]{1,0:T(8,128)(2,1)}) custom-call(bf16[64,1536]{1,0:T(8,128)(2,1)} %copy-done.18, bf16[64,1536]{1,0:T(8,128)(2,1)} %copy-done.20, bf16[64,1536]{1,0:T(8,128)(2,1)} %collective-permute-done.4.refs_2_, bf16[64,1536]{1,0:T(8,128)(2,1)} %copy-done.4, ...), custom_call_target="tpu_custom_call" | custom-call | flops 14495514624 | bytes 56623104 | tf_op jit(solution)/shard_map/ffn/pallas_call | solution.py:134
  62.5 2.0 %collective-permute-start.9 = (bf16[3,256,128]{2,1,0:T(8,128)(2,1)S(1)}, bf16[3,256,128]{2,1,0:T(8,128)(2,1)S(1)}, u32[]{:S(2)}, u32[]{:S(2)}) collective-permute-start(bf16[3,256,128]{2,1,0:T(8,128)(2,1)S(1)} %pad_maximum_fusion.refs_0_), channel_id=1, source_target_pairs={{0,8},{1,9},{2,10},{3,11},{4,12},{5,13},{6,14},{7,15},{8,0},{9,1},... | collective-permute-start | bytes 589832 | tf_op jit(solution)/shard_map/ppermute | solution.py:318
  64.6 2.0 %collective-permute-start.12 = (bf16[64,1536]{1,0:T(8,128)(2,1)}, bf16[64,1536]{1,0:T(8,128)(2,1)S(1)}, u32[]{:S(2)}, u32[]{:S(2)}) collective-permute-start(bf16[64,1536]{1,0:T(8,128)(2,1)} %get-tuple-element.84), channel_id=1, source_target_pairs={{0,4},{1,5},{2,6},{3,7},{4,0},{5,1},{6,2},{7,3},{8,12},{9,13},{10,... | collective-permute-start | bytes 589832 | tf_op jit(solution)/shard_map/ppermute | solution.py:318
  66.7 2.4 %collective-permute-start.16 = (bf16[64,1536]{1,0:T(8,128)(2,1)}, bf16[64,1536]{1,0:T(8,128)(2,1)S(1)}, u32[]{:S(2)}, u32[]{:S(2)}) collective-permute-start(bf16[64,1536]{1,0:T(8,128)(2,1)} %get-tuple-element.88), channel_id=1, source_target_pairs={{0,12},{1,13},{2,14},{3,15},{4,8},{5,9},{6,10},{7,11},{8,4},{9,5},... | collective-permute-start | bytes 589832 | tf_op jit(solution)/shard_map/ppermute | solution.py:318
  69.0 24.7 %ffn.3 = (bf16[64,1536]{1,0:T(8,128)(2,1)}, bf16[64,1536]{1,0:T(8,128)(2,1)}, bf16[64,1536]{1,0:T(8,128)(2,1)}, bf16[64,1536]{1,0:T(8,128)(2,1)}) custom-call(bf16[64,1536]{1,0:T(8,128)(2,1)} %copy-done.17, bf16[64,1536]{1,0:T(8,128)(2,1)} %copy-done.19, bf16[64,1536]{1,0:T(8,128)(2,1)} %copy-done.21, bf16[64,1536]{1,0:T(8,128)(2,1)} %copy-done.22, ...), custom_call_target="tpu_custom_call" | custom-call | flops 14495514624 | bytes 56623104 | tf_op jit(solution)/shard_map/ffn/pallas_call | solution.py:134
  93.8 1.6 %collective-permute-start.11 = (bf16[64,1536]{1,0:T(8,128)(2,1)}, bf16[64,1536]{1,0:T(8,128)(2,1)S(1)}, u32[]{:S(2)}, u32[]{:S(2)}) collective-permute-start(bf16[64,1536]{1,0:T(8,128)(2,1)} %get-tuple-element.83), channel_id=1, source_target_pairs={{0,2},{1,3},{2,0},{3,1},{4,6},{5,7},{6,4},{7,5},{8,10},{9,11},{10,... | collective-permute-start | bytes 589832 | tf_op jit(solution)/shard_map/ppermute | solution.py:318
  95.3 1.0 collective-permute-start.13
  96.3 1.9 %collective-permute-start.15 = (bf16[64,1536]{1,0:T(8,128)(2,1)}, bf16[64,1536]{1,0:T(8,128)(2,1)S(1)}, u32[]{:S(2)}, u32[]{:S(2)}) collective-permute-start(bf16[64,1536]{1,0:T(8,128)(2,1)} %get-tuple-element.87), channel_id=1, source_target_pairs={{0,10},{1,11},{2,8},{3,9},{4,14},{5,15},{6,12},{7,13},{8,2},{9,3},... | collective-permute-start | bytes 589832 | tf_op jit(solution)/shard_map/ppermute | solution.py:318
  98.3 2.3 %collective-permute-start.17 = (bf16[64,1536]{1,0:T(8,128)(2,1)}, bf16[64,1536]{1,0:T(8,128)(2,1)S(1)}, u32[]{:S(2)}, u32[]{:S(2)}) collective-permute-start(bf16[64,1536]{1,0:T(8,128)(2,1)} %get-tuple-element.89), channel_id=1, source_target_pairs={{0,14},{1,15},{2,12},{3,13},{4,10},{5,11},{6,8},{7,9},{8,6},{9,7},... | collective-permute-start | bytes 589832 | tf_op jit(solution)/shard_map/ppermute | solution.py:318
  101.4 8.6 %collective-permute-done.11.refs_1_ = bf16[64,1536]{1,0:T(8,128)(2,1)S(1)} collective-permute-done((bf16[64,1536]{1,0:T(8,128)(2,1)}, bf16[64,1536]{1,0:T(8,128)(2,1)S(1)}, u32[]{:S(2)}, u32[]{:S(2)}) %collective-permute-start.11) | collective-permute-done | bytes 196640 | tf_op jit(solution)/shard_map/ppermute | solution.py:318
  111.4 1.2 collective-permute-done.15.refs_5_
  118.6 1.0 combine.1
  119.7 2.2 %collective-permute-start.19 = (bf16[3,256,128]{2,1,0:T(8,128)(2,1)S(1)}, bf16[3,256,128]{2,1,0:T(8,128)(2,1)S(1)}, u32[]{:S(2)}, u32[]{:S(2)}) collective-permute-start(bf16[3,256,128]{2,1,0:T(8,128)(2,1)S(1)} %collective-permute-done.9.refs_2_), channel_id=1, source_target_pairs={{0,4},{1,5},{2,6},{3,7},{4,0},{5,1},{6,2},{7,3},{8,12},{9,13},{10,... | collective-permute-start | bytes 589832 | tf_op jit(solution)/shard_map/ppermute | solution.py:318
  121.9 5.5 %collective-permute-done.19.refs_3_ = bf16[3,256,128]{2,1,0:T(8,128)(2,1)S(1)} collective-permute-done((bf16[3,256,128]{2,1,0:T(8,128)(2,1)S(1)}, bf16[3,256,128]{2,1,0:T(8,128)(2,1)S(1)}, u32[]{:S(2)}, u32[]{:S(2)}) %collective-permute-start.19) | collective-permute-done | bytes 196640 | tf_op jit(solution)/shard_map/ppermute | solution.py:318
  128.3 2.6 %attend.1 = (f32[128,384]{1,0:T(8,128)S(1)}, bf16[128,384]{1,0:T(8,128)(2,1)}) custom-call(s32[1]{0:T(128)} %bitcast.11.head_ref, bf16[3,256,64]{2,1,0:T(8,128)(2,1)S(1)} %get-tuple-element.92.q_ref, bf16[3,256,128]{2,1,0:T(8,128)(2,1)S(1)} %pad_maximum_fusion.refs_0_, bf16[3,256,128]{2,1,0:T(8,128)(2,1)S(1)} %collective-permute-done.10.refs_1_, ...), custom_call_target="tpu_custom_call" | custom-call | flops 201326592 | bytes 786432 | tf_op jit(solution)/shard_map/attend/pallas_call | solution.py:190
  (93 shorter events, 17.9 us)
Async XLA Ops:
  0.0 3.3 %collective-permute-start = (s32[2,128]{1,0:T(2,128)}, s32[2,128]{1,0:T(2,128)S(1)}, u32[]{:S(2)}, u32[]{:S(2)}) collective-permute-start(s32[2,128]{1,0:T(2,128)} %bitcast.21), channel_id=1, source_target_pairs={{0,1},{1,0},{2,3},{3,2},{4,5},{5,4},{6,7},{7,6},{8,9},{9,8},{10,11... | collective-permute-start | bytes 3080 | tf_op jit(solution)/shard_map/ppermute | solution.py:318
  0.5 4.3 %collective-permute-start.1 = (bf16[1,128,1536]{2,1,0:T(8,128)(2,1)}, bf16[1,128,1536]{2,1,0:T(8,128)(2,1)S(1)}, u32[]{:S(2)}, u32[]{:S(2)}) collective-permute-start(bf16[1,128,1536]{2,1,0:T(8,128)(2,1)} %hidden_ref.1), channel_id=1, source_target_pairs={{0,1},{1,0},{2,3},{3,2},{4,5},{5,4},{6,7},{7,6},{8,9},{9,8},{10,11... | collective-permute-start | bytes 1179656 | tf_op jit(solution)/shard_map/ppermute | solution.py:318
  8.2 18.2 %collective-permute-start.2 = (bf16[64,1536]{1,0:T(8,128)(2,1)S(1)}, bf16[64,1536]{1,0:T(8,128)(2,1)S(1)}, u32[]{:S(2)}, u32[]{:S(2)}) collective-permute-start(bf16[64,1536]{1,0:T(8,128)(2,1)S(1)} %get-tuple-element.51), channel_id=1, source_target_pairs={{0,8},{1,9},{2,10},{3,11},{4,12},{5,13},{6,14},{7,15},{8,0},{9,1},... | collective-permute-start | bytes 589832 | tf_op jit(solution)/shard_map/ppermute | solution.py:318
  12.3 14.2 %collective-permute-start.3 = (bf16[64,1536]{1,0:T(8,128)(2,1)S(1)}, bf16[64,1536]{1,0:T(8,128)(2,1)S(1)}, u32[]{:S(2)}, u32[]{:S(2)}) collective-permute-start(bf16[64,1536]{1,0:T(8,128)(2,1)S(1)} %get-tuple-element.52), channel_id=1, source_target_pairs={{0,12},{1,13},{2,14},{3,15},{4,8},{5,9},{6,10},{7,11},{8,4},{9,5},... | collective-permute-start | bytes 589832 | tf_op jit(solution)/shard_map/ppermute | solution.py:318
  13.6 13.7 %collective-permute-start.4 = (bf16[64,1536]{1,0:T(8,128)(2,1)S(1)}, bf16[64,1536]{1,0:T(8,128)(2,1)}, u32[]{:S(2)}, u32[]{:S(2)}) collective-permute-start(bf16[64,1536]{1,0:T(8,128)(2,1)S(1)} %get-tuple-element.53), channel_id=1, source_target_pairs={{0,4},{1,5},{2,6},{3,7},{4,0},{5,1},{6,2},{7,3},{8,12},{9,13},{10,... | collective-permute-start | bytes 589832 | tf_op jit(solution)/shard_map/ppermute | solution.py:318
  27.3 35.2 %collective-permute-start.5 = (bf16[64,1536]{1,0:T(8,128)(2,1)S(1)}, bf16[64,1536]{1,0:T(8,128)(2,1)S(1)}, u32[]{:S(2)}, u32[]{:S(2)}) collective-permute-start(bf16[64,1536]{1,0:T(8,128)(2,1)S(1)} %get-tuple-element.73), channel_id=1, source_target_pairs={{0,10},{1,11},{2,8},{3,9},{4,14},{5,15},{6,12},{7,13},{8,2},{9,3},... | collective-permute-start | bytes 589832 | tf_op jit(solution)/shard_map/ppermute | solution.py:318
  33.7 30.9 %collective-permute-start.6 = (bf16[64,1536]{1,0:T(8,128)(2,1)S(1)}, bf16[64,1536]{1,0:T(8,128)(2,1)S(1)}, u32[]{:S(2)}, u32[]{:S(2)}) collective-permute-start(bf16[64,1536]{1,0:T(8,128)(2,1)S(1)} %get-tuple-element.74), channel_id=1, source_target_pairs={{0,14},{1,15},{2,12},{3,13},{4,10},{5,11},{6,8},{7,9},{8,6},{9,7},... | collective-permute-start | bytes 589832 | tf_op jit(solution)/shard_map/ppermute | solution.py:318
  34.1 32.5 %collective-permute-start.7 = (bf16[64,1536]{1,0:T(8,128)(2,1)S(1)}, bf16[64,1536]{1,0:T(8,128)(2,1)S(1)}, u32[]{:S(2)}, u32[]{:S(2)}) collective-permute-start(bf16[64,1536]{1,0:T(8,128)(2,1)S(1)} %get-tuple-element.75), channel_id=1, source_target_pairs={{0,6},{1,7},{2,4},{3,5},{4,2},{5,3},{6,0},{7,1},{8,14},{9,15},{10,... | collective-permute-start | bytes 589832 | tf_op jit(solution)/shard_map/ppermute | solution.py:318
  34.3 32.4 %collective-permute-start.8 = (bf16[64,1536]{1,0:T(8,128)(2,1)S(1)}, bf16[64,1536]{1,0:T(8,128)(2,1)S(1)}, u32[]{:S(2)}, u32[]{:S(2)}) collective-permute-start(bf16[64,1536]{1,0:T(8,128)(2,1)S(1)} %get-tuple-element.76), channel_id=1, source_target_pairs={{0,2},{1,3},{2,0},{3,1},{4,6},{5,7},{6,4},{7,5},{8,10},{9,11},{10,... | collective-permute-start | bytes 589832 | tf_op jit(solution)/shard_map/ppermute | solution.py:318
  35.7 58.0 %collective-permute-start.10 = (bf16[3,256,128]{2,1,0:T(8,128)(2,1)S(1)}, bf16[3,256,128]{2,1,0:T(8,128)(2,1)S(1)}, u32[]{:S(2)}, u32[]{:S(2)}) collective-permute-start(bf16[3,256,128]{2,1,0:T(8,128)(2,1)S(1)} %pad_maximum_fusion.refs_0_), channel_id=1, source_target_pairs={{0,4},{1,5},{2,6},{3,7},{4,0},{5,1},{6,2},{7,3},{8,12},{9,13},{10,... | collective-permute-start | bytes 589832 | tf_op jit(solution)/shard_map/ppermute | solution.py:318
  62.5 71.5 %copy-start.1 = (f32[1536,16]{0,1:T(8,128)S(1)}, f32[1536,16]{0,1:T(8,128)}, u32[]{:S(2)}) copy-start(f32[1536,16]{0,1:T(8,128)} %param.16) | copy-start | bytes 294916
  62.5 68.7 %copy-start.25 = (f32[1,128,16]{1,2,0:T(8,128)S(1)}, f32[1,128,16]{1,2,0:T(8,128)}, u32[]{:S(2)}) copy-start(f32[1,128,16]{1,2,0:T(8,128)} %param.25) | copy-start | bytes 24580
  62.5 70.2 %copy-start.3 = (bf16[1,128,1536]{2,1,0:T(8,128)(2,1)S(1)}, bf16[1,128,1536]{2,1,0:T(8,128)(2,1)}, u32[]{:S(2)}) copy-start(bf16[1,128,1536]{2,1,0:T(8,128)(2,1)} %hidden_ref.1) | copy-start | bytes 1179652
  62.5 31.2 %collective-permute-start.9 = (bf16[3,256,128]{2,1,0:T(8,128)(2,1)S(1)}, bf16[3,256,128]{2,1,0:T(8,128)(2,1)S(1)}, u32[]{:S(2)}, u32[]{:S(2)}) collective-permute-start(bf16[3,256,128]{2,1,0:T(8,128)(2,1)S(1)} %pad_maximum_fusion.refs_0_), channel_id=1, source_target_pairs={{0,8},{1,9},{2,10},{3,11},{4,12},{5,13},{6,14},{7,15},{8,0},{9,1},... | collective-permute-start | bytes 589832 | tf_op jit(solution)/shard_map/ppermute | solution.py:318
  64.6 31.8 %collective-permute-start.12 = (bf16[64,1536]{1,0:T(8,128)(2,1)}, bf16[64,1536]{1,0:T(8,128)(2,1)S(1)}, u32[]{:S(2)}, u32[]{:S(2)}) collective-permute-start(bf16[64,1536]{1,0:T(8,128)(2,1)} %get-tuple-element.84), channel_id=1, source_target_pairs={{0,4},{1,5},{2,6},{3,7},{4,0},{5,1},{6,2},{7,3},{8,12},{9,13},{10,... | collective-permute-start | bytes 589832 | tf_op jit(solution)/shard_map/ppermute | solution.py:318
  66.6 31.7 %collective-permute-start.14 = (bf16[64,1536]{1,0:T(8,128)(2,1)}, bf16[64,1536]{1,0:T(8,128)(2,1)S(1)}, u32[]{:S(2)}, u32[]{:S(2)}) collective-permute-start(bf16[64,1536]{1,0:T(8,128)(2,1)} %get-tuple-element.86), channel_id=1, source_target_pairs={{0,8},{1,9},{2,10},{3,11},{4,12},{5,13},{6,14},{7,15},{8,0},{9,1},... | collective-permute-start | bytes 589832 | tf_op jit(solution)/shard_map/ppermute | solution.py:318
  66.7 34.1 %collective-permute-start.16 = (bf16[64,1536]{1,0:T(8,128)(2,1)}, bf16[64,1536]{1,0:T(8,128)(2,1)S(1)}, u32[]{:S(2)}, u32[]{:S(2)}) collective-permute-start(bf16[64,1536]{1,0:T(8,128)(2,1)} %get-tuple-element.88), channel_id=1, source_target_pairs={{0,12},{1,13},{2,14},{3,15},{4,8},{5,9},{6,10},{7,11},{8,4},{9,5},... | collective-permute-start | bytes 589832 | tf_op jit(solution)/shard_map/ppermute | solution.py:318
  93.8 16.2 %collective-permute-start.11 = (bf16[64,1536]{1,0:T(8,128)(2,1)}, bf16[64,1536]{1,0:T(8,128)(2,1)S(1)}, u32[]{:S(2)}, u32[]{:S(2)}) collective-permute-start(bf16[64,1536]{1,0:T(8,128)(2,1)} %get-tuple-element.83), channel_id=1, source_target_pairs={{0,2},{1,3},{2,0},{3,1},{4,6},{5,7},{6,4},{7,5},{8,10},{9,11},{10,... | collective-permute-start | bytes 589832 | tf_op jit(solution)/shard_map/ppermute | solution.py:318
  95.3 15.3 %collective-permute-start.13 = (bf16[64,1536]{1,0:T(8,128)(2,1)}, bf16[64,1536]{1,0:T(8,128)(2,1)S(1)}, u32[]{:S(2)}, u32[]{:S(2)}) collective-permute-start(bf16[64,1536]{1,0:T(8,128)(2,1)} %get-tuple-element.85), channel_id=1, source_target_pairs={{0,6},{1,7},{2,4},{3,5},{4,2},{5,3},{6,0},{7,1},{8,14},{9,15},{10,... | collective-permute-start | bytes 589832 | tf_op jit(solution)/shard_map/ppermute | solution.py:318
  96.3 16.2 %collective-permute-start.15 = (bf16[64,1536]{1,0:T(8,128)(2,1)}, bf16[64,1536]{1,0:T(8,128)(2,1)S(1)}, u32[]{:S(2)}, u32[]{:S(2)}) collective-permute-start(bf16[64,1536]{1,0:T(8,128)(2,1)} %get-tuple-element.87), channel_id=1, source_target_pairs={{0,10},{1,11},{2,8},{3,9},{4,14},{5,15},{6,12},{7,13},{8,2},{9,3},... | collective-permute-start | bytes 589832 | tf_op jit(solution)/shard_map/ppermute | solution.py:318
  98.3 15.0 %collective-permute-start.17 = (bf16[64,1536]{1,0:T(8,128)(2,1)}, bf16[64,1536]{1,0:T(8,128)(2,1)S(1)}, u32[]{:S(2)}, u32[]{:S(2)}) collective-permute-start(bf16[64,1536]{1,0:T(8,128)(2,1)} %get-tuple-element.89), channel_id=1, source_target_pairs={{0,14},{1,15},{2,12},{3,13},{4,10},{5,11},{6,8},{7,9},{8,6},{9,7},... | collective-permute-start | bytes 589832 | tf_op jit(solution)/shard_map/ppermute | solution.py:318
  119.6 13.1 %collective-permute-start.18 = (bf16[128,1536]{1,0:T(8,128)(2,1)S(1)}, bf16[128,1536]{1,0:T(8,128)(2,1)S(1)}, u32[]{:S(2)}, u32[]{:S(2)}) collective-permute-start(bf16[128,1536]{1,0:T(8,128)(2,1)S(1)} %get-tuple-element.91), channel_id=1, source_target_pairs={{0,1},{1,0},{2,3},{3,2},{4,5},{5,4},{6,7},{7,6},{8,9},{9,8},{10,11... | collective-permute-start | bytes 1179656 | tf_op jit(solution)/shard_map/ppermute | solution.py:318
  119.7 7.7 %collective-permute-start.19 = (bf16[3,256,128]{2,1,0:T(8,128)(2,1)S(1)}, bf16[3,256,128]{2,1,0:T(8,128)(2,1)S(1)}, u32[]{:S(2)}, u32[]{:S(2)}) collective-permute-start(bf16[3,256,128]{2,1,0:T(8,128)(2,1)S(1)} %collective-permute-done.9.refs_2_), channel_id=1, source_target_pairs={{0,4},{1,5},{2,6},{3,7},{4,0},{5,1},{6,2},{7,3},{8,12},{9,13},{10,... | collective-permute-start | bytes 589832 | tf_op jit(solution)/shard_map/ppermute | solution.py:318
  130.9 1.8 %collective-permute-start.20 = (bf16[128,384]{1,0:T(8,128)(2,1)}, bf16[128,384]{1,0:T(8,128)(2,1)S(1)}, u32[]{:S(2)}, u32[]{:S(2)}) collective-permute-start(bf16[128,384]{1,0:T(8,128)(2,1)} %get-tuple-element.96), channel_id=1, source_target_pairs={{0,1},{1,0},{2,3},{3,2},{4,5},{5,4},{6,7},{7,6},{8,9},{9,8},{10,11... | collective-permute-start | bytes 294920 | tf_op jit(solution)/shard_map/ppermute | solution.py:318
  (23 other events, 251.0 us)

commit v2 on v1

--- a/solution.py
+++ b/solution.py
@@ -20,7 +20,7 @@
 MIB = 1024 * 1024
 MEMBERS = ("expert", "dp", "head")
 CHUNK_A = [8, 12, 4, 0]
-CHUNK_B = [10, 14, 6, 2]
+CHUNK_B = [2, 6, 10, 14]
 
 
 def layer_norm(values):
@@ -33,16 +33,56 @@
     return values / jnp.sqrt(jnp.mean(values * values, axis=-1, keepdims=True) + epsilon)
 
 
-def prep_kernel(chips, capacity, me_ref, ids_ref, own_ref, other_ref, mod_ref, rows_ref, code_ref, *out_refs):
-    tokens = own_ref.shape[1]
+def modulate(values, mod_ref):
+    return (layer_norm(values.astype(jnp.float32)) * (1.0 + mod_ref[1]) + mod_ref[0]).astype(jnp.bfloat16)
+
+
+def fetch(pairs, sems):
+    copies = [pltpu.make_async_copy(src, dst, sems.at[i]) for i, (src, dst) in enumerate(pairs)]
+    for copy in copies:
+        copy.start()
+    for copy in copies:
+        copy.wait()
+
+
+def own_rows_kernel(own_hbm, mod_hbm, rows_ref, own, mod, sems):
+    fetch([(own_hbm, own), (mod_hbm, mod)], sems)
+    rows_ref[...] = modulate(own[0], mod)
+
+
+def own_rows(own, modulation):
+    hbm = pl.BlockSpec(memory_space=pl.ANY)
+    return pl.pallas_call(
+        own_rows_kernel,
+        in_specs=[hbm] * 2,
+        out_specs=pl.BlockSpec(memory_space=pltpu.VMEM),
+        out_shape=jax.ShapeDtypeStruct(own.shape[1:], jnp.bfloat16),
+        scratch_shapes=[
+            pltpu.VMEM(own.shape, own.dtype),
+            pltpu.VMEM(modulation.shape, modulation.dtype),
+            pltpu.SemaphoreType.DMA((2,)),
+        ],
+        compiler_params=pltpu.CompilerParams(vmem_limit_bytes=16 * MIB),
+        cost_estimate=pl.CostEstimate(flops=8 * own.size, bytes_accessed=4 * own.size, transcendentals=0),
+        name="own_rows",
+    )(own, modulation)
+
+
+def prep_kernel(
+    chips, capacity, me_ref, own_ids_hbm, other_ids_hbm, own_rows_ref, other_hbm, mod_hbm, rows_ref, code_ref, *refs
+):
+    out_refs, (own_ids, other_ids, other, mod, sems) = refs[:chips], refs[chips:]
+    tokens = own_rows_ref.shape[0]
     both = 2 * tokens
-    for i, ref in enumerate((own_ref, other_ref)):
-        rows_ref[i * tokens : (i + 1) * tokens, :] = (
-            layer_norm(ref[0].astype(jnp.float32)) * (1.0 + mod_ref[0, 1:2, :]) + mod_ref[0, 0:1, :]
-        ).astype(jnp.bfloat16)
+    fetch(
+        [(own_ids_hbm, own_ids), (other_ids_hbm, other_ids), (other_hbm, other), (mod_hbm, mod)], sems
+    )
+    rows_ref[:tokens, :] = own_rows_ref[...]
+    rows_ref[tokens:, :] = modulate(other[0], mod)
     me = me_ref[0]
+    ids = jnp.concatenate([own_ids[0], other_ids[0]], axis=1)
     experts = lax.broadcasted_iota(jnp.int32, (EXPERTS, both), 0)
-    named = [experts == ids_ref[j : j + 1, :] for j in range(TOP)]
+    named = [experts == ids[j : j + 1, :] for j in range(TOP)]
     tally = functools.reduce(jnp.logical_or, named).astype(jnp.float32).astype(jnp.bfloat16)
     earlier = lax.broadcasted_iota(jnp.int32, (both, both), 0)
     later = lax.broadcasted_iota(jnp.int32, (both, both), 1)
@@ -55,7 +95,7 @@
     hit = None
     for j in range(TOP):
         own_rank = jnp.sum(jnp.where(named[j], rank, 0.0), axis=0, keepdims=True).astype(jnp.int32)
-        away = jnp.bitwise_xor(ids_ref[j : j + 1, :], me)
+        away = jnp.bitwise_xor(ids[j : j + 1, :], me)
         code = lax.shift_right_logical(away, 1) * (2 * capacity) + second + own_rank
         code = jnp.where(jnp.bitwise_and(away, 1) == 0, code, -1)
         code_ref[j : j + 1, :] = code
@@ -69,113 +109,271 @@
         ).astype(jnp.bfloat16)
 
 
-def prep(me, ids, own, other, modulation, chips, capacity):
-    tokens, width = own.shape[1:]
-    vmem = pl.BlockSpec(memory_space=pltpu.VMEM)
+def prep(me, own_ids, other_ids, rows, other, modulation, chips, capacity):
+    tokens, width = rows.shape
+    vmem, hbm = pl.BlockSpec(memory_space=pltpu.VMEM), pl.BlockSpec(memory_space=pl.ANY)
     return pl.pallas_call(
         functools.partial(prep_kernel, chips, capacity),
-        in_specs=[pl.BlockSpec(memory_space=pltpu.SMEM)] + [vmem] * 4,
+        in_specs=[pl.BlockSpec(memory_space=pltpu.SMEM), hbm, hbm, vmem, hbm, hbm],
         out_specs=[vmem] * (2 + chips),
         out_shape=[
             jax.ShapeDtypeStruct((2 * tokens, width), jnp.bfloat16),
             jax.ShapeDtypeStruct((TOP, 2 * tokens), jnp.int32),
         ]
         + [jax.ShapeDtypeStruct((2 * capacity, width), jnp.bfloat16)] * chips,
-        compiler_params=pltpu.CompilerParams(vmem_limit_bytes=24 * MIB),
+        scratch_shapes=[
+            pltpu.VMEM(own_ids.shape, own_ids.dtype),
+            pltpu.VMEM(other_ids.shape, other_ids.dtype),
+            pltpu.VMEM(other.shape, other.dtype),
+            pltpu.VMEM(modulation.shape, modulation.dtype),
+            pltpu.SemaphoreType.DMA((4,)),
+        ],
+        compiler_params=pltpu.CompilerParams(vmem_limit_bytes=16 * MIB),
         cost_estimate=pl.CostEstimate(
             flops=8 * chips * capacity * tokens * width,
             bytes_accessed=4 * chips * capacity * width,
             transcendentals=0,
         ),
         name="prep",
-    )(me, ids, own, other, modulation)
-
-
-def ffn_kernel(blocks, *refs):
+    )(me, own_ids, other_ids, rows, other, modulation)
+
+
+RESIDENT = 1
+
+
+def weight_tile(units):
+    return 768 if units % 768 == 0 else 128
+
+
+def resident_kernel(gate_hbm, up_hbm, down_hbm, gate_ref, up_ref, down_ref, sems):
+    part = pl.ds(0, gate_ref.shape[1])
+    fetch(
+        [(gate_hbm.at[:, part], gate_ref), (up_hbm.at[:, part], up_ref), (down_hbm.at[part, :], down_ref)], sems
+    )
+
+
+def resident(gate_weight, up_weight, down_weight):
+    width, units = gate_weight.shape
+    kept = RESIDENT * weight_tile(units)
+    vmem, hbm = pl.BlockSpec(memory_space=pltpu.VMEM), pl.BlockSpec(memory_space=pl.ANY)
+    return pl.pallas_call(
+        resident_kernel,
+        in_specs=[hbm] * 3,
+        out_specs=[vmem] * 3,
+        out_shape=[
+            jax.ShapeDtypeStruct((width, kept), jnp.bfloat16),
+            jax.ShapeDtypeStruct((width, kept), jnp.bfloat16),
+            jax.ShapeDtypeStruct((kept, width), jnp.bfloat16),
+        ],
+        scratch_shapes=[pltpu.SemaphoreType.DMA((3,))],
+        compiler_params=pltpu.CompilerParams(vmem_limit_bytes=46 * MIB),
+        cost_estimate=pl.CostEstimate(flops=0, bytes_accessed=6 * width * kept, transcendentals=0),
+        name="resident",
+    )(gate_weight, up_weight, down_weight)
+
+
+def ffn_kernel(blocks, tiles, *refs):
     row_refs = refs[:blocks]
-    gate_ref, up_ref, down_ref = refs[blocks : blocks + 3]
-    out_refs = refs[blocks + 3 : 2 * blocks + 3]
-    rows, total = refs[2 * blocks + 3 :]
-    step, last = pl.program_id(0), pl.num_programs(0) - 1
-    capacity = row_refs[0].shape[0]
-
-    @pl.when(step == 0)
-    def _():
-        for i in range(blocks):
-            rows[i * capacity : (i + 1) * capacity, :] = row_refs[i][...]
-
-    gate_vals = jnp.dot(rows[...], gate_ref[...], preferred_element_type=jnp.float32)
-    up_vals = jnp.dot(rows[...], up_ref[...], preferred_element_type=jnp.float32)
-    activated = (gate_vals / (1.0 + jnp.exp(-gate_vals)) * up_vals).astype(jnp.bfloat16)
-    term = jnp.dot(activated, down_ref[...], preferred_element_type=jnp.float32)
-
-    @pl.when(step == 0)
-    def _():
-        total[...] = term
-
-    @pl.when(jnp.logical_and(step > 0, step < last))
-    def _():
-        total[...] += term
-
-    @pl.when(step == last)
-    def _():
-        done = (total[...] + term).astype(jnp.bfloat16)
-        for i in range(blocks):
-            out_refs[i][...] = done[i * capacity : (i + 1) * capacity, :]
-
-
-def ffn(row_blocks, gate_weight, up_weight, down_weight):
+    kept_gate, kept_up, kept_down, gate_hbm, up_hbm, down_hbm = refs[blocks : blocks + 6]
+    out_refs = refs[blocks + 6 : 2 * blocks + 6]
+    rows, total, hidden, gate, up, down, sems = refs[2 * blocks + 6 :]
+    size = row_refs[0].shape[0]
+    slots, tile = down.shape[0], down.shape[1]
+
+    def copies(step):
+        slot, part = lax.rem(step, slots), pl.ds(pl.multiple_of(step * tile, tile), tile)
+        return (
+            pltpu.make_async_copy(gate_hbm.at[:, part], gate.at[slot], sems.at[0, slot]),
+            pltpu.make_async_copy(up_hbm.at[:, part], up.at[slot], sems.at[1, slot]),
+            pltpu.make_async_copy(down_hbm.at[part, :], down.at[slot], sems.at[2, slot]),
+        )
+
+    def start(step):
+        for copy in copies(step):
+            copy.start()
+
+    def units_of(gate_tile, up_tile):
+        gate_vals = jnp.dot(rows[...], gate_tile, preferred_element_type=jnp.float32)
+        up_vals = jnp.dot(rows[...], up_tile, preferred_element_type=jnp.float32)
+        return gate_vals, up_vals
+
+    def activate(gate_vals, up_vals):
+        return (gate_vals / (1.0 + jnp.exp(-gate_vals)) * up_vals).astype(jnp.bfloat16)
+
+    def part_of(step):
+        return slice(step * tile, (step + 1) * tile)
+
+    for step in range(RESIDENT, min(RESIDENT + slots, tiles)):
+        start(jnp.int32(step))
+    for i in range(blocks):
+        rows[i * size : (i + 1) * size, :] = row_refs[i][...]
+    hidden[0] = activate(*units_of(kept_gate[:, part_of(0)], kept_up[:, part_of(0)]))
+
+    for step in range(1, RESIDENT):
+        vals = units_of(kept_gate[:, part_of(step)], kept_up[:, part_of(step)])
+        term = jnp.dot(hidden[(step - 1) % 2], kept_down[part_of(step - 1), :], preferred_element_type=jnp.float32)
+        total[...] = term if step == 1 else total[...] + term
+        hidden[step % 2] = activate(*vals)
+
+    def wait_units(step):
+        gate_copy, up_copy, _ = copies(step)
+        gate_copy.wait()
+        up_copy.wait()
+
+    wait_units(jnp.int32(RESIDENT))
+    vals = units_of(gate[RESIDENT % slots], up[RESIDENT % slots])
+    term = jnp.dot(
+        hidden[(RESIDENT - 1) % 2], kept_down[part_of(RESIDENT - 1), :], preferred_element_type=jnp.float32
+    )
+    total[...] = term if RESIDENT == 1 else total[...] + term
+    hidden[RESIDENT % 2] = activate(*vals)
+
+    def body(step, carry):
+        slot, last = lax.rem(step, slots), lax.rem(step - 1, slots)
+        wait_units(step)
+        copies(step - 1)[2].wait()
+        now = lax.rem(step, 2)
+        vals = units_of(gate[slot], up[slot])
+        total[...] += jnp.dot(hidden[1 - now], down[last], preferred_element_type=jnp.float32)
+        hidden[now] = activate(*vals)
+
+        @pl.when(step + slots - 1 < tiles)
+        def _():
+            start(step + slots - 1)
+
+        return carry
+
+    lax.fori_loop(RESIDENT + 1, tiles, body, 0)
+    copies(jnp.int32(tiles - 1))[2].wait()
+    done = total[...] + jnp.dot(
+        hidden[(tiles - 1) % 2], down[(tiles - 1) % slots], preferred_element_type=jnp.float32
+    )
+    for i in range(blocks):
+        out_refs[i][...] = done[i * size : (i + 1) * size, :].astype(jnp.bfloat16)
+
+
+def ffn(row_blocks, kept, gate_weight, up_weight, down_weight):
     blocks = len(row_blocks)
-    capacity, width = row_blocks[0].shape
+    size, width = row_blocks[0].shape
     units = gate_weight.shape[1]
-    tile = 1024 if units % 1024 == 0 else units
-    rows = blocks * capacity
-    whole = pl.BlockSpec((capacity, width), lambda s: (0, 0))
+    tile = weight_tile(units)
+    rows, slots = blocks * size, 3
+    vmem, hbm = pl.BlockSpec(memory_space=pltpu.VMEM), pl.BlockSpec(memory_space=pl.ANY)
     return pl.pallas_call(
-        functools.partial(ffn_kernel, blocks),
-        grid=(units // tile,),
-        in_specs=[whole] * blocks
-        + [
-            pl.BlockSpec((width, tile), lambda s: (0, s)),
-            pl.BlockSpec((width, tile), lambda s: (0, s)),
-            pl.BlockSpec((tile, width), lambda s: (s, 0)),
-        ],
-        out_specs=[whole] * blocks,
-        out_shape=[jax.ShapeDtypeStruct((capacity, width), jnp.bfloat16)] * blocks,
-        scratch_shapes=[pltpu.VMEM((rows, width), jnp.bfloat16), pltpu.VMEM((rows, width), jnp.float32)],
-        compiler_params=pltpu.CompilerParams(vmem_limit_bytes=56 * MIB),
+        functools.partial(ffn_kernel, blocks, units // tile),
+        in_specs=[vmem] * (blocks + 3) + [hbm] * 3,
+        out_specs=[vmem] * blocks,
+        out_shape=[jax.ShapeDtypeStruct((size, width), jnp.bfloat16)] * blocks,
+        scratch_shapes=[
+            pltpu.VMEM((rows, width), jnp.bfloat16),
+            pltpu.VMEM((rows, width), jnp.float32),
+            pltpu.VMEM((2, rows, tile), jnp.bfloat16),
+            pltpu.VMEM((slots, width, tile), jnp.bfloat16),
+            pltpu.VMEM((slots, width, tile), jnp.bfloat16),
+            pltpu.VMEM((slots, tile, width), jnp.bfloat16),
+            pltpu.SemaphoreType.DMA((3, slots)),
+        ],
+        compiler_params=pltpu.CompilerParams(vmem_limit_bytes=36 * MIB),
         cost_estimate=pl.CostEstimate(
             flops=6 * rows * width * units,
             bytes_accessed=6 * width * units,
             transcendentals=rows * units,
         ),
         name="ffn",
-    )(*row_blocks, gate_weight, up_weight, down_weight)
+    )(*row_blocks, *kept, gate_weight, up_weight, down_weight)
+
+
+def side_kernel(
+    rows_ref, router_hbm, own_ids_hbm, other_ids_hbm, code_ref, qkv_hbm, q_ref, kv_ref, routes_ref, router_ref,
+    own_ids_ref, other_ids_ref, qkv, sems
+):
+    copy = pltpu.make_async_copy(qkv_hbm, qkv, sems.at[3])
+    copy.start()
+    fetch([(router_hbm, router_ref), (own_ids_hbm, own_ids_ref), (other_ids_hbm, other_ids_ref)], sems)
+    logits = lax.dot_general(
+        router_ref[...],
+        rows_ref[...].astype(jnp.float32),
+        (((1,), (1,)), ((), ())),
+        precision=lax.Precision.HIGHEST,
+        preferred_element_type=jnp.float32,
+    )
+    ids = jnp.concatenate([own_ids_ref[0], other_ids_ref[0]], axis=1)
+    experts = lax.broadcasted_iota(jnp.int32, logits.shape, 0)
+    picked = [
+        jnp.sum(jnp.where(experts == ids[j : j + 1, :], logits, 0.0), axis=0, keepdims=True)
+        for j in range(TOP)
+    ]
+    first = 1.0 / (1.0 + jnp.exp(picked[1] - picked[0]))
+    line = lax.broadcasted_iota(jnp.int32, (8, first.shape[1]), 0)
+    table = jnp.where(line == 0, first, 0.0)
+    for j in range(TOP):
+        table = jnp.where(line == j + 1, code_ref[j : j + 1, :].astype(jnp.float32), table)
+    routes_ref[...] = jnp.transpose(table)
+
+    def unit(values):
+        return (
+            values / jnp.sqrt(jnp.mean(values * values, axis=0, keepdims=True) + epsilon)
+        ).astype(jnp.bfloat16)
+
+    copy.wait()
+    for h in range(qkv.shape[0]):
+        q_ref[h] = unit(qkv[h, :HD, :].astype(jnp.float32))
+        kv_ref[h, :HD, :] = unit(qkv[h, HD : 2 * HD, :].astype(jnp.float32))
+        kv_ref[h, HD:, :] = qkv[h, 2 * HD :, :]
+
+
+def side(rows, router, own_ids, other_ids, code, qkv):
+    heads, _, tokens = qkv.shape
+    vmem, hbm = pl.BlockSpec(memory_space=pltpu.VMEM), pl.BlockSpec(memory_space=pl.ANY)
+    return pl.pallas_call(
+        side_kernel,
+        in_specs=[vmem, hbm, hbm, hbm, vmem, hbm],
+        out_specs=[vmem] * 3,
+        out_shape=[
+            jax.ShapeDtypeStruct((heads, HD, tokens), jnp.bfloat16),
+            jax.ShapeDtypeStruct((heads, 2 * HD, tokens), jnp.bfloat16),
+            jax.ShapeDtypeStruct((rows.shape[0], 8), jnp.float32),
+        ],
+        scratch_shapes=[
+            pltpu.VMEM(router.shape, router.dtype),
+            pltpu.VMEM(own_ids.shape, own_ids.dtype),
+            pltpu.VMEM(other_ids.shape, other_ids.dtype),
+            pltpu.VMEM(qkv.shape, qkv.dtype),
+            pltpu.SemaphoreType.DMA((4,)),
+        ],
+        compiler_params=pltpu.CompilerParams(vmem_limit_bytes=16 * MIB),
+        cost_estimate=pl.CostEstimate(
+            flops=6 * qkv.size + 12 * rows.size * EXPERTS, bytes_accessed=4 * qkv.size, transcendentals=0
+        ),
+        name="side",
+    )(rows, router, own_ids, other_ids, code, qkv)
 
 
 def attend_kernel(pieces, head_ref, q_ref, *refs):
     kv_refs = refs[:pieces]
     out_ref, keep_ref, send_ref, mix = refs[pieces:]
-    heads, queries = q_ref.shape[:2]
-    acc = None
+    heads, _, queries = q_ref.shape
     for h in range(heads):
-        q = q_ref[h]
         sums, weighted = None, None
         for kv_ref in kv_refs:
             scores = lax.dot_general(
-                q, kv_ref[h, :, :HD], (((1,), (1,)), ((), ())), preferred_element_type=jnp.float32
+                kv_ref[h, :HD, :], q_ref[h], (((0,), (0,)), ((), ())), preferred_element_type=jnp.float32
             ) * (score_scale / HD)
             weights = jnp.exp(scores - score_scale)
-            part = jnp.sum(weights, axis=-1, keepdims=True)
+            part = jnp.sum(weights, axis=0, keepdims=True)
             value = jnp.dot(
-                weights.astype(jnp.bfloat16), kv_ref[h, :, HD:], preferred_element_type=jnp.float32
+                kv_ref[h, HD:, :], weights.astype(jnp.bfloat16), preferred_element_type=jnp.float32
             )
             sums = part if sums is None else sums + part
             weighted = value if weighted is None else weighted + value
         attended = (weighted / sums).astype(jnp.bfloat16)
-        term = jnp.dot(attended, out_ref[h], preferred_element_type=jnp.float32)
-        acc = term if acc is None else acc + term
-    mix[...] = acc
+        term = lax.dot_general(
+            attended, out_ref[h], (((0,), (0,)), ((), ())), preferred_element_type=jnp.float32
+        )
+        if h == 0:
+            mix[...] = term
+        else:
+            mix[...] += term
     half = queries // 2
     mine = head_ref[0]
     keep_ref[...] = mix[pl.ds(pl.multiple_of(mine * half, half), half), :]
@@ -183,8 +381,8 @@
 
 
 def attend(head, queries, kv_pieces, guide_out):
-    heads, count, _ = queries.shape
-    keys = sum(piece.shape[1] for piece in kv_pieces)
+    heads, _, count = queries.shape
+    keys = sum(piece.shape[2] for piece in kv_pieces)
     wide = guide_out.shape[-1]
     vmem = pl.BlockSpec(memory_space=pltpu.VMEM)
     return pl.pallas_call(
@@ -196,7 +394,7 @@
             jax.ShapeDtypeStruct((count // 2, wide), jnp.bfloat16),
         ],
         scratch_shapes=[pltpu.VMEM((count, wide), jnp.float32)],
-        compiler_params=pltpu.CompilerParams(vmem_limit_bytes=32 * MIB),
+        compiler_params=pltpu.CompilerParams(vmem_limit_bytes=16 * MIB),
         cost_estimate=pl.CostEstimate(
             flops=4 * heads * count * keys * HD,
             bytes_accessed=4 * heads * keys * HD,
@@ -206,62 +404,71 @@
     )(head, queries, *kv_pieces, guide_out)
 
 
-def combine_kernel(blocks, code_ref, first_ref, *refs):
-    row_refs, (keep_ref, send_ref, rows) = refs[:blocks], refs[blocks:]
+def combine_kernel(blocks, parity, routes_ref, *refs):
+    row_refs, refs = refs[:blocks], refs[blocks:]
+    before_refs, (keep_ref, send_ref, rows, sems) = refs[:-4], refs[-4:]
     size = row_refs[0].shape[0]
-    for i in range(blocks):
-        rows[i * size : (i + 1) * size, :] = row_refs[i][...]
-    both = code_ref.shape[0]
-    tokens = both // 2
-    slots = lax.broadcasted_iota(jnp.int32, (tokens, blocks * size), 1)
+    if before_refs:
+        for i in range(blocks):
+            rows[i * size : (i + 1) * size, :] = row_refs[i][...]
+    else:
+        fetch([(row_refs[i], rows.at[pl.ds(i * size, size), :]) for i in range(blocks)], sems)
+    tokens = routes_ref.shape[0] // 2
+    lane = lax.broadcasted_iota(jnp.int32, (tokens, blocks * size), 1)
+    slots = (lane + (lax.div(lane, size) + parity) * size).astype(jnp.float32)
     for i, out_ref in enumerate((keep_ref, send_ref)):
         part = slice(i * tokens, (i + 1) * tokens)
-        first = first_ref[part, :]
-        total = None
+        first = routes_ref[part, 0:1]
+        total = before_refs[i][...] if before_refs else None
         for j, weight in enumerate((first, 1.0 - first)):
-            pick = (slots == code_ref[part, j : j + 1]).astype(jnp.float32).astype(jnp.bfloat16)
+            pick = (slots == routes_ref[part, j + 1 : j + 2]).astype(jnp.float32).astype(jnp.bfloat16)
             term = weight * jnp.dot(pick, rows[...], preferred_element_type=jnp.float32)
             total = term if total is None else total + term
         out_ref[...] = total.astype(out_ref.dtype)
 
 
-def combine(row_blocks, code, first):
+def combine(row_blocks, parity, routes, before, send_type):
     blocks = len(row_blocks)
     size, width = row_blocks[0].shape
-    tokens = code.shape[0] // 2
+    tokens = routes.shape[0] // 2
     vmem = pl.BlockSpec(memory_space=pltpu.VMEM)
     return pl.pallas_call(
-        functools.partial(combine_kernel, blocks),
-        in_specs=[vmem] * (2 + blocks),
+        functools.partial(combine_kernel, blocks, parity),
+        in_specs=[vmem] + [vmem if before else pl.BlockSpec(memory_space=pl.ANY)] * blocks + [vmem] * len(before),
         out_specs=[vmem] * 2,
         out_shape=[
             jax.ShapeDtypeStruct((tokens, width), jnp.float32),
-            jax.ShapeDtypeStruct((tokens, width), jnp.bfloat16),
-        ],
-        scratch_shapes=[pltpu.VMEM((blocks * size, width), jnp.bfloat16)],
-        compiler_params=pltpu.CompilerParams(vmem_limit_bytes=24 * MIB),
+            jax.ShapeDtypeStruct((tokens, width), send_type),
+        ],
+        scratch_shapes=[
+            pltpu.VMEM((blocks * size, width), jnp.bfloat16),
+            pltpu.SemaphoreType.DMA((blocks,)),
+        ],
+        compiler_params=pltpu.CompilerParams(vmem_limit_bytes=16 * MIB),
         cost_estimate=pl.CostEstimate(
             flops=8 * tokens * blocks * size * width,
             bytes_accessed=2 * blocks * size * width,
             transcendentals=0,
         ),
         name="combine",
-    )(code, first, *row_blocks)
+    )(routes, *row_blocks, *before)
 
 
 def finish_kernel(
     keep_moe_ref, got_moe_ref, hidden_ref, mod_ref, final_ref, keep_ref, got_ref, guide_final_ref, latent_ref,
     guidance_ref, step_ref, out_ref
 ):
+    def velocity(weight_ref, values):
+        return lax.dot_general(
+            weight_ref[...],
+            layer_norm(values).astype(jnp.bfloat16),
+            (((1,), (1,)), ((), ())),
+            preferred_element_type=jnp.float32,
+        )
+
     moe_out = keep_moe_ref[...] + got_moe_ref[...].astype(jnp.float32)
-    updated = hidden_ref[0].astype(jnp.float32) + mod_ref[0, 2:3, :] * moe_out
-    main_velocity = jnp.dot(
-        layer_norm(updated).astype(jnp.bfloat16), final_ref[...], preferred_element_type=jnp.float32
-    )
-    guide_mix = keep_ref[...] + got_ref[...].astype(jnp.float32)
-    guide_velocity = jnp.dot(
-        layer_norm(guide_mix).astype(jnp.bfloat16), guide_final_ref[...], preferred_element_type=jnp.float32
-    )
+    main_velocity = velocity(final_ref, hidden_ref[0].astype(jnp.float32) + mod_ref[2] * moe_out)
+    guide_velocity = velocity(guide_final_ref, keep_ref[...] + got_ref[...].astype(jnp.float32))
     guided = guide_velocity + guidance_ref[0] * (main_velocity - guide_velocity)
     out_ref[0] = latent_ref[0] + step_ref[0] * guided
 
@@ -280,26 +487,8 @@
     )(keep_moe, got_moe, hidden, modulation, main_final, keep, got, guide_final, latent, guidance, step_size)
 
 
-def direct_body(
-    hidden,
-    modulation,
-    router_weight,
-    route_ids,
-    gate_weight,
-    up_weight,
-    down_weight,
-    main_final,
-    guide_qkv,
-    guide_out,
-    guide_final,
-    latent,
-    guidance,
-    step_size,
-):
-    return direct_step(
-        hidden, modulation, router_weight, route_ids, gate_weight, up_weight, down_weight, main_final,
-        guide_qkv, guide_out, guide_final, latent, guidance, step_size,
-    )
+def direct_body(*args):
+    return direct_step(*args)
 
 
 def direct_step(
@@ -317,49 +506,43 @@
             return block
         return lax.ppermute(block, MEMBERS, [(i, i ^ k) for i in range(devices)])
 
+    modulation = jnp.transpose(modulation, (1, 0, 2))
+    ids = jnp.transpose(route_ids, (0, 2, 1))
     other = swap(hidden, 1)
-    ids = route_ids[0].T
-    ids = jnp.concatenate([ids, swap(ids, 1)], axis=1)
-    rows, code, *outgoing = prep(me, ids, hidden, other, modulation, devices // 2, capacity)
+    other_ids = swap(ids, 1)
+    rows = own_rows(hidden, modulation)
+    rows, code, *outgoing = prep(me, ids, other_ids, rows, other, modulation, devices // 2, capacity)
     rows_a = [swap(outgoing[k // 2], k) for k in CHUNK_A]
-
-    qkv = jnp.transpose(guide_qkv[0], (1, 0, 2))
-    queries = unit_rows(qkv[..., :HD].astype(jnp.float32)).astype(jnp.bfloat16)
-    keys = unit_rows(qkv[..., HD : 2 * HD].astype(jnp.float32)).astype(jnp.bfloat16)
-    kv = jnp.concatenate([keys, qkv[..., 2 * HD :]], axis=-1)
-    logits = jnp.dot(rows.astype(jnp.float32), router_weight, precision=lax.Precision.HIGHEST)
-    named = jnp.arange(EXPERTS, dtype=jnp.int32)[None, :]
-    picked = [
-        jnp.sum(jnp.where(ids[j][:, None] == named, logits, 0.0), axis=1, keepdims=True) for j in range(TOP)
-    ]
-    first = jax.nn.sigmoid(picked[0] - picked[1])
-    slot_codes = code.T
-
-    rows_a, second, kv, first, slot_codes, queries = lax.optimization_barrier(
-        (rows_a, [outgoing[k // 2] for k in CHUNK_B], kv, first, slot_codes, queries)
-    )
-    rows_b = [swap(block, k) for block, k in zip(second, CHUNK_B)]
+    rows_b = [swap(outgoing[k // 2], k) for k in CHUNK_B]
+    queries, kv, routes = side(
+        rows, router_weight.T, ids, other_ids, code, jnp.transpose(guide_qkv[0], (1, 2, 0))
+    )
+    weights, _ = lax.optimization_barrier(((gate_weight, up_weight, down_weight), routes))
+    kept = resident(*weights)
+    far = swap(kv, 8)
     near = swap(kv, 4)
-
-    done_a = ffn(rows_a, gate_weight, up_weight, down_weight)
-    done_a, kv_far = lax.optimization_barrier((done_a, kv))
+    rows_a, routes, queries = lax.optimization_barrier((rows_a, routes, queries))
+
+    done_a = ffn(rows_a, kept, gate_weight, up_weight, down_weight)
     back_a = [swap(block, k) for block, k in zip(done_a, CHUNK_A)]
-    far = swap(kv_far, 8)
-
-    done_b = ffn(rows_b, gate_weight, up_weight, down_weight)
-    done_b, far, near, queries = lax.optimization_barrier((done_b, far, near, queries))
+
+    done_b = ffn(rows_b, kept, gate_weight, up_weight, down_weight)
+    done_b, queries, back_a, far, near = lax.optimization_barrier((done_b, queries, back_a, far, near))
     back_b = [swap(block, k) for block, k in zip(done_b, CHUNK_B)]
     relayed = swap(far, 4)
 
     keep, send = attend(head, queries, [kv, near, far, relayed], guide_out)
     got = swap(send, 1)
-
-    back = dict(zip(CHUNK_A + CHUNK_B, back_a + back_b))
-    keep_moe, send_moe = combine([back[k] for k in sorted(back)], slot_codes, first)
+    sums = combine([block for _, block in sorted(zip(CHUNK_A, back_a), key=lambda pair: pair[0])], 0, routes, (), jnp.float32)
+    keep_moe, send_moe = combine(
+        [block for _, block in sorted(zip(CHUNK_B, back_b), key=lambda pair: pair[0])], 1, routes, sums, jnp.bfloat16
+    )
     got_moe = swap(send_moe, 1)
-    return finish(
-        keep_moe, got_moe, hidden, modulation, main_final, keep, got, guide_final, latent, guidance, step_size
-    )
+    result = finish(
+        keep_moe, got_moe, hidden, modulation, main_final.T, keep, got, guide_final.T,
+        jnp.transpose(latent, (0, 2, 1)), guidance, step_size,
+    )
+    return jnp.transpose(result, (0, 2, 1))
 
 
 def route_slots(flat_ids, block_slots, per_index, copies):

time: 134 us -> 108 us (0.81)
  local copies, waits for them, and re-layouts: 14 us -> 4.27 us
  waiting for transfers between devices: 27.8 us -> 19.9 us
  Pallas kernels: 55.7 us -> 50.5 us
  other arithmetic: 2.28 us -> 0 us
    unnamed x57 -> x22, local copies, waits for them, and re-layouts: 13 us -> 4.27 us
    ppermute x21, waiting for transfers between devices: 27.8 us -> 19.9 us  [swap(): return lax.ppermute(block, MEMBERS, [(i, i ^ k) for i in range(devices)])]
    pallas_call x3 -> x7, Pallas kernels: 50.7 us -> 45.3 us  [the longest x2 37.4 us: ffn(): pl.pallas_call(functools.partial(ffn_kernel, blocks, units // tile), in_s...]
    concatenate x3 -> x0, other arithmetic: 1.57 us -> none  [the longest x2 1.44 us: direct_step(): ids = jnp.concatenate([ids, swap(ids, 1)], axis=1)]
  transfers between devices with their start and end apart: 21 -> 21, of which waited for: 5 -> 4; matrix products, arithmetic and copies ran while one was open for 4% -> 0% of each run, Pallas kernels for 39% -> 43%
where the time goes in v2:
time: 108 us
  Pallas kernels  50.5 us (47%)
  starting transfers between devices  32 us (30%)
  waiting for transfers between devices  19.9 us (18%)
  local copies, waits for them, and re-layouts  4.27 us (4%)
  between operations  1.57 us (1%)
    pallas_call x2, Pallas kernels, ffn(): pl.pallas_call(functools.partial(ffn_kernel, blocks, units // tile), in_s...  37.4 us
    ppermute x21, starting transfers between devices, swap(): return lax.ppermute(block, MEMBERS, [(i, i ^ k) for i in range(devices)])  32 us
    ppermute x21, waiting for transfers between devices, swap(): return lax.ppermute(block, MEMBERS, [(i, i ^ k) for i in range(devices)])  19.9 us
    unnamed x22, local copies, waits for them, and re-layouts  4.27 us
    pallas_call x1, Pallas kernels, resident(): pl.pallas_call(resident_kernel, in_specs=[hbm] * 3, out_specs=[vmem] * 3,...  3.15 us
    pallas_call x2, Pallas kernels, combine(): pl.pallas_call(functools.partial(combine_kernel, blocks, parity), in_spec...  2.35 us
    pallas_call x1, Pallas kernels, attend(): pl.pallas_call(functools.partial(attend_kernel, len(kv_pieces)), in_specs...  2.16 us
  transfers between devices with their start and end apart: 21, of which 4 were waited for; matrix products, arithmetic and copies ran while one was open for 0% of the time, Pallas kernels for 43%

profile of v2, /device:TPU:0, one launch (start us, length us, event | category | flops | bytes accessed | tf_op | source)
XLA Modules:
  0.0 108.2 jit_solution(15799604179619733629)
XLA Ops:
  3.5 1.8 %prep.1 = (bf16[256,1536]{1,0:T(8,128)(2,1)S(1)}, s32[2,256]{1,0:T(2,128)S(1)}, bf16[64,1536]{1,0:T(8,128)(2,1)S(1)}, bf16[64,1536]{1,0:T(8,128)(2,1)S(1)}, bf16...) custom-call(s32[1]{0:T(128)} %bitcast.me_ref, ...), custom_call_target="tpu_custom_call" | custom-call | flops 402653184 | bytes 1572864 | tf_op jit(solution)/shard_map/prep/pallas_call | solution.py:115
  5.3 4.1 %collective-permute-start.2 = (bf16[64,1536]{1,0:T(8,128)(2,1)S(1)}, bf16[64,1536]{1,0:T(8,128)(2,1)S(1)}, u32[]{:S(2)}, u32[]{:S(2)}) collective-permute-start(bf16[64,1536]{1,0:T(8,128)(2,1)S(1)} %get-tuple-element.55), channel_id=1, source_target_pairs={{0,8},{1,9},{2,10},{3,11},{4,12},{5,13},{6,14},{7,15},{8,0},{9,1},... | collective-permute-start | bytes 589832 | tf_op jit(solution)/shard_map/ppermute | solution.py:507
  9.4 1.3 %collective-permute-start.3 = (bf16[64,1536]{1,0:T(8,128)(2,1)S(1)}, bf16[64,1536]{1,0:T(8,128)(2,1)S(1)}, u32[]{:S(2)}, u32[]{:S(2)}) collective-permute-start(bf16[64,1536]{1,0:T(8,128)(2,1)S(1)} %get-tuple-element.56), channel_id=1, source_target_pairs={{0,12},{1,13},{2,14},{3,15},{4,8},{5,9},{6,10},{7,11},{8,4},{9,5},... | collective-permute-start | bytes 589832 | tf_op jit(solution)/shard_map/ppermute | solution.py:507
  11.0 1.5 %collective-permute-start.5 = (bf16[64,1536]{1,0:T(8,128)(2,1)S(1)}, bf16[64,1536]{1,0:T(8,128)(2,1)S(1)}, u32[]{:S(2)}, u32[]{:S(2)}) collective-permute-start(bf16[64,1536]{1,0:T(8,128)(2,1)S(1)} %get-tuple-element.64), channel_id=1, source_target_pairs={{0,2},{1,3},{2,0},{3,1},{4,6},{5,7},{6,4},{7,5},{8,10},{9,11},{10,... | collective-permute-start | bytes 589832 | tf_op jit(solution)/shard_map/ppermute | solution.py:507
  12.5 1.8 %collective-permute-start.6 = (bf16[64,1536]{1,0:T(8,128)(2,1)S(1)}, bf16[64,1536]{1,0:T(8,128)(2,1)S(1)}, u32[]{:S(2)}, u32[]{:S(2)}) collective-permute-start(bf16[64,1536]{1,0:T(8,128)(2,1)S(1)} %get-tuple-element.65), channel_id=1, source_target_pairs={{0,6},{1,7},{2,4},{3,5},{4,2},{5,3},{6,0},{7,1},{8,14},{9,15},{10,... | collective-permute-start | bytes 589832 | tf_op jit(solution)/shard_map/ppermute | solution.py:507
  16.1 1.8 %side.1 = (bf16[3,64,256]{2,1,0:T(8,128)(2,1)S(1)}, bf16[3,128,256]{2,1,0:T(8,128)(2,1)S(1)}, f32[256,8]{1,0:T(8,128)S(1)}) custom-call(bf16[256,1536]{1,0:T(8,128)(2,1)S(1)} %get-tuple-element.59.rows_ref, f32[16,1536]{1,0:T(8,128)S(1)} %bitcast.13, s32[1,2,128]{2,1,0:T(2,128)S(1)} %bitcast.22, s32[1,2,128]{2,1,0:T(2,128)S(1)} %collective-permute-done.other_ids_hbm, ...), custom_call_target="tpu_custom_call" | custom-call | flops 76382208 | bytes 589824 | tf_op jit(solution)/shard_map/side/pallas_call | solution.py:328
  17.9 3.1 %resident.1 = (bf16[1536,768]{1,0:T(8,128)(2,1)S(1)}, bf16[1536,768]{1,0:T(8,128)(2,1)S(1)}, bf16[768,1536]{1,0:T(8,128)(2,1)S(1)}) custom-call(bf16[1536,6144]{1,0:T(8,128)(2,1)} %refs_7_.3, bf16[1536,6144]{1,0:T(8,128)(2,1)} %refs_8_.3, bf16[6144,1536]{1,0:T(8,128)(2,1)} %refs_9_.3), custom_call_target="tpu_custom_call" | custom-call | bytes 7077888 | tf_op jit(solution)/shard_map/resident/pallas_call | solution.py:159
  21.0 2.6 %collective-permute-done.2.refs_0_ = bf16[64,1536]{1,0:T(8,128)(2,1)S(1)} collective-permute-done((bf16[64,1536]{1,0:T(8,128)(2,1)S(1)}, bf16[64,1536]{1,0:T(8,128)(2,1)S(1)}, u32[]{:S(2)}, u32[]{:S(2)}) %collective-permute-start.2) | collective-permute-done | bytes 196640 | tf_op jit(solution)/shard_map/ppermute | solution.py:507
  24.4 3.1 %collective-permute-start.8 = (bf16[64,1536]{1,0:T(8,128)(2,1)S(1)}, bf16[64,1536]{1,0:T(8,128)(2,1)S(1)}, u32[]{:S(2)}, u32[]{:S(2)}) collective-permute-start(bf16[64,1536]{1,0:T(8,128)(2,1)S(1)} %get-tuple-element.67), channel_id=1, source_target_pairs={{0,14},{1,15},{2,12},{3,13},{4,10},{5,11},{6,8},{7,9},{8,6},{9,7},... | collective-permute-start | bytes 589832 | tf_op jit(solution)/shard_map/ppermute | solution.py:507
  27.5 4.4 %collective-permute-start.12 = (bf16[3,128,256]{2,1,0:T(8,128)(2,1)S(1)}, bf16[3,128,256]{2,1,0:T(8,128)(2,1)S(1)}, u32[]{:S(2)}, u32[]{:S(2)}) collective-permute-start(bf16[3,128,256]{2,1,0:T(8,128)(2,1)S(1)} %get-tuple-element.87.refs_0_), channel_id=1, source_target_pairs={{0,8},{1,9},{2,10},{3,11},{4,12},{5,13},{6,14},{7,15},{8,0},{9,1},... | collective-permute-start | bytes 589832 | tf_op jit(solution)/shard_map/ppermute | solution.py:507
  31.9 18.7 %ffn.3 = (bf16[64,1536]{1,0:T(8,128)(2,1)S(1)}, bf16[64,1536]{1,0:T(8,128)(2,1)S(1)}, bf16[64,1536]{1,0:T(8,128)(2,1)S(1)}, bf16[64,1536]{1,0:T(8,128)(2,1)S(1)}) custom-call(bf16[64,1536]{1,0:T(8,128)(2,1)S(1)} %collective-permute-done.2.refs_0_, bf16[64,1536]{1,0:T(8,128)(2,1)S(1)} %collective-permute-done.3.refs_1_, ...), custom_call_target="tpu_custom_call" | custom-call | flops 14495514624 | bytes 56623104 | tf_op jit(solution)/shard_map/ffn/pallas_call | solution.py:262
  51.1 2.9 %collective-permute-start.9 = (bf16[64,1536]{1,0:T(8,128)(2,1)S(1)}, bf16[64,1536]{1,0:T(8,128)(2,1)S(1)}, u32[]{:S(2)}, u32[]{:S(2)}) collective-permute-start(bf16[64,1536]{1,0:T(8,128)(2,1)S(1)} %get-tuple-element.83), channel_id=1, source_target_pairs={{0,8},{1,9},{2,10},{3,11},{4,12},{5,13},{6,14},{7,15},{8,0},{9,1},... | collective-permute-start | bytes 589832 | tf_op jit(solution)/shard_map/ppermute | solution.py:507
  54.1 1.1 collective-permute-start.10
  55.3 18.7 %ffn.2 = (bf16[64,1536]{1,0:T(8,128)(2,1)S(1)}, bf16[64,1536]{1,0:T(8,128)(2,1)S(1)}, bf16[64,1536]{1,0:T(8,128)(2,1)S(1)}, bf16[64,1536]{1,0:T(8,128)(2,1)S(1)}) custom-call(bf16[64,1536]{1,0:T(8,128)(2,1)S(1)} %collective-permute-done.5.refs_0_, bf16[64,1536]{1,0:T(8,128)(2,1)S(1)} %collective-permute-done.6.refs_1_, ...), custom_call_target="tpu_custom_call" | custom-call | flops 14495514624 | bytes 56623104 | tf_op jit(solution)/shard_map/ffn/pallas_call | solution.py:262
  74.5 3.1 %collective-permute-start.15 = (bf16[64,1536]{1,0:T(8,128)(2,1)S(1)}, bf16[64,1536]{1,0:T(8,128)(2,1)S(1)}, u32[]{:S(2)}, u32[]{:S(2)}) collective-permute-start(bf16[64,1536]{1,0:T(8,128)(2,1)S(1)} %get-tuple-element.89), channel_id=1, source_target_pairs={{0,6},{1,7},{2,4},{3,5},{4,2},{5,3},{6,0},{7,1},{8,14},{9,15},{10,... | collective-permute-start | bytes 589832 | tf_op jit(solution)/shard_map/ppermute | solution.py:507
  77.6 1.3 %collective-permute-start.16 = (bf16[64,1536]{1,0:T(8,128)(2,1)S(1)}, bf16[64,1536]{1,0:T(8,128)(2,1)S(1)}, u32[]{:S(2)}, u32[]{:S(2)}) collective-permute-start(bf16[64,1536]{1,0:T(8,128)(2,1)S(1)} %get-tuple-element.90), channel_id=1, source_target_pairs={{0,10},{1,11},{2,8},{3,9},{4,14},{5,15},{6,12},{7,13},{8,2},{9,3},... | collective-permute-start | bytes 589832 | tf_op jit(solution)/shard_map/ppermute | solution.py:507
  78.9 2.0 %collective-permute-start.17 = (bf16[64,1536]{1,0:T(8,128)(2,1)S(1)}, bf16[64,1536]{1,0:T(8,128)(2,1)S(1)}, u32[]{:S(2)}, u32[]{:S(2)}) collective-permute-start(bf16[64,1536]{1,0:T(8,128)(2,1)S(1)} %get-tuple-element.91), channel_id=1, source_target_pairs={{0,14},{1,15},{2,12},{3,13},{4,10},{5,11},{6,8},{7,9},{8,6},{9,7},... | collective-permute-start | bytes 589832 | tf_op jit(solution)/shard_map/ppermute | solution.py:507
  80.9 1.6 %combine.2 = (f32[128,1536]{1,0:T(8,128)S(1)}, f32[128,1536]{1,0:T(8,128)S(1)}) custom-call(f32[256,8]{1,0:T(8,128)S(1)} %get-tuple-element.63.routes_ref, bf16[64,1536]{1,0:T(8,128)(2,1)S(1)} %get-tuple-element.92.refs_0_, bf16[64,1536]{1,0:T(8,128)(2,1)S(1)} %collective-permute-done.11.refs_1_, bf16[64,1536]{1,0:T(8,128)(2,1)S(1)} %collective-permute-done.9.refs_2_, ...), custom_call_target="tpu_custom_call" | custom-call | flops 402653184 | bytes 786432 | tf_op jit(solution)/shard_map/combine/pallas_call | solution.py:435
  82.5 5.0 %collective-permute-done.14.refs_0_ = bf16[64,1536]{1,0:T(8,128)(2,1)S(1)} collective-permute-done((bf16[64,1536]{1,0:T(8,128)(2,1)S(1)}, bf16[64,1536]{1,0:T(8,128)(2,1)S(1)}, u32[]{:S(2)}, u32[]{:S(2)}) %collective-permute-start.14) | collective-permute-done | bytes 196640 | tf_op jit(solution)/shard_map/ppermute | solution.py:507
  87.5 6.8 %collective-permute-done.16.refs_2_ = bf16[64,1536]{1,0:T(8,128)(2,1)S(1)} collective-permute-done((bf16[64,1536]{1,0:T(8,128)(2,1)S(1)}, bf16[64,1536]{1,0:T(8,128)(2,1)S(1)}, u32[]{:S(2)}, u32[]{:S(2)}) %collective-permute-start.16) | collective-permute-done | bytes 196640 | tf_op jit(solution)/shard_map/ppermute | solution.py:507
  95.1 2.7 %collective-permute-start.19 = (bf16[3,128,256]{2,1,0:T(8,128)(2,1)S(1)}, bf16[3,128,256]{2,1,0:T(8,128)(2,1)S(1)}, u32[]{:S(2)}, u32[]{:S(2)}) collective-permute-start(bf16[3,128,256]{2,1,0:T(8,128)(2,1)S(1)} %collective-permute-done.12.refs_2_), channel_id=1, source_target_pairs={{0,4},{1,5},{2,6},{3,7},{4,0},{5,1},{6,2},{7,3},{8,12},{9,13},{10,... | collective-permute-start | bytes 589832 | tf_op jit(solution)/shard_map/ppermute | solution.py:507
  97.8 5.5 %collective-permute-done.19.refs_3_ = bf16[3,128,256]{2,1,0:T(8,128)(2,1)S(1)} collective-permute-done((bf16[3,128,256]{2,1,0:T(8,128)(2,1)S(1)}, bf16[3,128,256]{2,1,0:T(8,128)(2,1)S(1)}, u32[]{:S(2)}, u32[]{:S(2)}) %collective-permute-start.19) | collective-permute-done | bytes 196640 | tf_op jit(solution)/shard_map/ppermute | solution.py:507
  103.3 2.2 %attend.1 = (f32[128,384]{1,0:T(8,128)S(1)}, bf16[128,384]{1,0:T(8,128)(2,1)S(1)}) custom-call(s32[1]{0:T(128)} %bitcast.7.head_ref, bf16[3,64,256]{2,1,0:T(8,128)(2,1)S(1)} %get-tuple-element.100.q_ref, bf16[3,128,256]{2,1,0:T(8,128)(2,1)S(1)} %get-tuple-element.87.refs_0_, bf16[3,128,256]{2,1,0:T(8,128)(2,1)S(1)} %collective-permute-done.13.refs_1_, ...), custom_call_target="tpu_custom_call" | custom-call | flops 201326592 | bytes 786432 | tf_op jit(solution)/shard_map/attend/pallas_call | solution.py:388
  106.9 1.2 %finish.1 = f32[1,16,128]{2,1,0:T(8,128)} custom-call(f32[128,1536]{1,0:T(8,128)S(1)} %get-tuple-element.98.keep_moe_ref, bf16[128,1536]{1,0:T(8,128)(2,1)S(1)} %collective-permute-done.18.got_moe_ref, bf16[1,128,1536]{2,1,0:T(8,128)(2,1)S(1)} %copy-done.1, f32[3,1,1536]{2,1,0:T(1,128)S(1)} %bitcast.16, bf16[16,1536]{1,0:T(8,128)(2,1)S(1)} %bitcast.17, ...), custom_call_target="tpu_custom_call" | custom-call | flops 12582912 | bytes 1572864 | tf_op jit(solution)/shard_map/finish/pallas_call | solution.py:479
  (50 shorter events, 8.3 us)
Async XLA Ops:
  0.0 2.8 %collective-permute-start.1 = (bf16[1,128,1536]{2,1,0:T(8,128)(2,1)}, bf16[1,128,1536]{2,1,0:T(8,128)(2,1)S(1)}, u32[]{:S(2)}, u32[]{:S(2)}) collective-permute-start(bf16[1,128,1536]{2,1,0:T(8,128)(2,1)} %hidden_ref.1), channel_id=1, source_target_pairs={{0,1},{1,0},{2,3},{3,2},{4,5},{5,4},{6,7},{7,6},{8,9},{9,8},{10,11... | collective-permute-start | bytes 1179656 | tf_op jit(solution)/shard_map/ppermute | solution.py:507
  0.5 2.3 %collective-permute-start = (s32[1,2,128]{2,1,0:T(2,128)}, s32[1,2,128]{2,1,0:T(2,128)S(1)}, u32[]{:S(2)}, u32[]{:S(2)}) collective-permute-start(s32[1,2,128]{2,1,0:T(2,128)} %bitcast.20), channel_id=1, source_target_pairs={{0,1},{1,0},{2,3},{3,2},{4,5},{5,4},{6,7},{7,6},{8,9},{9,8},{10,11... | collective-permute-start | bytes 3080 | tf_op jit(solution)/shard_map/ppermute | solution.py:507
  5.3 18.4 %collective-permute-start.2 = (bf16[64,1536]{1,0:T(8,128)(2,1)S(1)}, bf16[64,1536]{1,0:T(8,128)(2,1)S(1)}, u32[]{:S(2)}, u32[]{:S(2)}) collective-permute-start(bf16[64,1536]{1,0:T(8,128)(2,1)S(1)} %get-tuple-element.55), channel_id=1, source_target_pairs={{0,8},{1,9},{2,10},{3,11},{4,12},{5,13},{6,14},{7,15},{8,0},{9,1},... | collective-permute-start | bytes 589832 | tf_op jit(solution)/shard_map/ppermute | solution.py:507
  9.4 15.0 %collective-permute-start.3 = (bf16[64,1536]{1,0:T(8,128)(2,1)S(1)}, bf16[64,1536]{1,0:T(8,128)(2,1)S(1)}, u32[]{:S(2)}, u32[]{:S(2)}) collective-permute-start(bf16[64,1536]{1,0:T(8,128)(2,1)S(1)} %get-tuple-element.56), channel_id=1, source_target_pairs={{0,12},{1,13},{2,14},{3,15},{4,8},{5,9},{6,10},{7,11},{8,4},{9,5},... | collective-permute-start | bytes 589832 | tf_op jit(solution)/shard_map/ppermute | solution.py:507
  10.7 16.8 %collective-permute-start.4 = (bf16[64,1536]{1,0:T(8,128)(2,1)S(1)}, bf16[64,1536]{1,0:T(8,128)(2,1)S(1)}, u32[]{:S(2)}, u32[]{:S(2)}) collective-permute-start(bf16[64,1536]{1,0:T(8,128)(2,1)S(1)} %get-tuple-element.57), channel_id=1, source_target_pairs={{0,4},{1,5},{2,6},{3,7},{4,0},{5,1},{6,2},{7,3},{8,12},{9,13},{10,... | collective-permute-start | bytes 589832 | tf_op jit(solution)/shard_map/ppermute | solution.py:507
  11.0 39.7 %collective-permute-start.5 = (bf16[64,1536]{1,0:T(8,128)(2,1)S(1)}, bf16[64,1536]{1,0:T(8,128)(2,1)S(1)}, u32[]{:S(2)}, u32[]{:S(2)}) collective-permute-start(bf16[64,1536]{1,0:T(8,128)(2,1)S(1)} %get-tuple-element.64), channel_id=1, source_target_pairs={{0,2},{1,3},{2,0},{3,1},{4,6},{5,7},{6,4},{7,5},{8,10},{9,11},{10,... | collective-permute-start | bytes 589832 | tf_op jit(solution)/shard_map/ppermute | solution.py:507
  12.5 38.7 %collective-permute-start.6 = (bf16[64,1536]{1,0:T(8,128)(2,1)S(1)}, bf16[64,1536]{1,0:T(8,128)(2,1)S(1)}, u32[]{:S(2)}, u32[]{:S(2)}) collective-permute-start(bf16[64,1536]{1,0:T(8,128)(2,1)S(1)} %get-tuple-element.65), channel_id=1, source_target_pairs={{0,6},{1,7},{2,4},{3,5},{4,2},{5,3},{6,0},{7,1},{8,14},{9,15},{10,... | collective-permute-start | bytes 589832 | tf_op jit(solution)/shard_map/ppermute | solution.py:507
  23.6 30.5 %collective-permute-start.7 = (bf16[64,1536]{1,0:T(8,128)(2,1)S(1)}, bf16[64,1536]{1,0:T(8,128)(2,1)S(1)}, u32[]{:S(2)}, u32[]{:S(2)}) collective-permute-start(bf16[64,1536]{1,0:T(8,128)(2,1)S(1)} %get-tuple-element.66), channel_id=1, source_target_pairs={{0,10},{1,11},{2,8},{3,9},{4,14},{5,15},{6,12},{7,13},{8,2},{9,3},... | collective-permute-start | bytes 589832 | tf_op jit(solution)/shard_map/ppermute | solution.py:507
  24.4 30.7 %collective-permute-start.8 = (bf16[64,1536]{1,0:T(8,128)(2,1)S(1)}, bf16[64,1536]{1,0:T(8,128)(2,1)S(1)}, u32[]{:S(2)}, u32[]{:S(2)}) collective-permute-start(bf16[64,1536]{1,0:T(8,128)(2,1)S(1)} %get-tuple-element.67), channel_id=1, source_target_pairs={{0,14},{1,15},{2,12},{3,13},{4,10},{5,11},{6,8},{7,9},{8,6},{9,7},... | collective-permute-start | bytes 589832 | tf_op jit(solution)/shard_map/ppermute | solution.py:507
  27.5 46.5 %collective-permute-start.12 = (bf16[3,128,256]{2,1,0:T(8,128)(2,1)S(1)}, bf16[3,128,256]{2,1,0:T(8,128)(2,1)S(1)}, u32[]{:S(2)}, u32[]{:S(2)}) collective-permute-start(bf16[3,128,256]{2,1,0:T(8,128)(2,1)S(1)} %get-tuple-element.87.refs_0_), channel_id=1, source_target_pairs={{0,8},{1,9},{2,10},{3,11},{4,12},{5,13},{6,14},{7,15},{8,0},{9,1},... | collective-permute-start | bytes 589832 | tf_op jit(solution)/shard_map/ppermute | solution.py:507
  50.7 23.3 %collective-permute-start.13 = (bf16[3,128,256]{2,1,0:T(8,128)(2,1)S(1)}, bf16[3,128,256]{2,1,0:T(8,128)(2,1)S(1)}, u32[]{:S(2)}, u32[]{:S(2)}) collective-permute-start(bf16[3,128,256]{2,1,0:T(8,128)(2,1)S(1)} %get-tuple-element.87.refs_0_), channel_id=1, source_target_pairs={{0,4},{1,5},{2,6},{3,7},{4,0},{5,1},{6,2},{7,3},{8,12},{9,13},{10,... | collective-permute-start | bytes 589832 | tf_op jit(solution)/shard_map/ppermute | solution.py:507
  51.1 22.9 %collective-permute-start.9 = (bf16[64,1536]{1,0:T(8,128)(2,1)S(1)}, bf16[64,1536]{1,0:T(8,128)(2,1)S(1)}, u32[]{:S(2)}, u32[]{:S(2)}) collective-permute-start(bf16[64,1536]{1,0:T(8,128)(2,1)S(1)} %get-tuple-element.83), channel_id=1, source_target_pairs={{0,8},{1,9},{2,10},{3,11},{4,12},{5,13},{6,14},{7,15},{8,0},{9,1},... | collective-permute-start | bytes 589832 | tf_op jit(solution)/shard_map/ppermute | solution.py:507
  54.1 20.0 %collective-permute-start.10 = (bf16[64,1536]{1,0:T(8,128)(2,1)S(1)}, bf16[64,1536]{1,0:T(8,128)(2,1)S(1)}, u32[]{:S(2)}, u32[]{:S(2)}) collective-permute-start(bf16[64,1536]{1,0:T(8,128)(2,1)S(1)} %get-tuple-element.84), channel_id=1, source_target_pairs={{0,12},{1,13},{2,14},{3,15},{4,8},{5,9},{6,10},{7,11},{8,4},{9,5},... | collective-permute-start | bytes 589832 | tf_op jit(solution)/shard_map/ppermute | solution.py:507
  55.1 51.7 %copy-start.5 = (f32[1,3,1536]{2,0,1:T(1,128)S(1)}, f32[1,3,1536]{2,0,1:T(1,128)}, u32[]{:S(2)}) copy-start(f32[1,3,1536]{2,0,1:T(1,128)} %param.15) | copy-start | bytes 55300
  55.1 51.7 %copy-start.6 = (bf16[1536,16]{0,1:T(8,128)(2,1)S(1)}, bf16[1536,16]{0,1:T(8,128)(2,1)}, u32[]{:S(2)}) copy-start(bf16[1536,16]{0,1:T(8,128)(2,1)} %param.21) | copy-start | bytes 147460
  55.2 51.7 %copy-start.7 = (bf16[384,16]{0,1:T(8,128)(2,1)S(1)}, bf16[384,16]{0,1:T(8,128)(2,1)}, u32[]{:S(2)}) copy-start(bf16[384,16]{0,1:T(8,128)(2,1)} %param.24) | copy-start | bytes 36868
  55.2 18.9 %collective-permute-start.11 = (bf16[64,1536]{1,0:T(8,128)(2,1)S(1)}, bf16[64,1536]{1,0:T(8,128)(2,1)S(1)}, u32[]{:S(2)}, u32[]{:S(2)}) collective-permute-start(bf16[64,1536]{1,0:T(8,128)(2,1)S(1)} %get-tuple-element.85), channel_id=1, source_target_pairs={{0,4},{1,5},{2,6},{3,7},{4,0},{5,1},{6,2},{7,3},{8,12},{9,13},{10,... | collective-permute-start | bytes 589832 | tf_op jit(solution)/shard_map/ppermute | solution.py:507
  74.0 13.4 %collective-permute-start.14 = (bf16[64,1536]{1,0:T(8,128)(2,1)S(1)}, bf16[64,1536]{1,0:T(8,128)(2,1)S(1)}, u32[]{:S(2)}, u32[]{:S(2)}) collective-permute-start(bf16[64,1536]{1,0:T(8,128)(2,1)S(1)} %get-tuple-element.88), channel_id=1, source_target_pairs={{0,2},{1,3},{2,0},{3,1},{4,6},{5,7},{6,4},{7,5},{8,10},{9,11},{10,... | collective-permute-start | bytes 589832 | tf_op jit(solution)/shard_map/ppermute | solution.py:507
  74.5 12.9 %collective-permute-start.15 = (bf16[64,1536]{1,0:T(8,128)(2,1)S(1)}, bf16[64,1536]{1,0:T(8,128)(2,1)S(1)}, u32[]{:S(2)}, u32[]{:S(2)}) collective-permute-start(bf16[64,1536]{1,0:T(8,128)(2,1)S(1)} %get-tuple-element.89), channel_id=1, source_target_pairs={{0,6},{1,7},{2,4},{3,5},{4,2},{5,3},{6,0},{7,1},{8,14},{9,15},{10,... | collective-permute-start | bytes 589832 | tf_op jit(solution)/shard_map/ppermute | solution.py:507
  77.6 16.7 %collective-permute-start.16 = (bf16[64,1536]{1,0:T(8,128)(2,1)S(1)}, bf16[64,1536]{1,0:T(8,128)(2,1)S(1)}, u32[]{:S(2)}, u32[]{:S(2)}) collective-permute-start(bf16[64,1536]{1,0:T(8,128)(2,1)S(1)} %get-tuple-element.90), channel_id=1, source_target_pairs={{0,10},{1,11},{2,8},{3,9},{4,14},{5,15},{6,12},{7,13},{8,2},{9,3},... | collective-permute-start | bytes 589832 | tf_op jit(solution)/shard_map/ppermute | solution.py:507
  78.9 15.4 %collective-permute-start.17 = (bf16[64,1536]{1,0:T(8,128)(2,1)S(1)}, bf16[64,1536]{1,0:T(8,128)(2,1)S(1)}, u32[]{:S(2)}, u32[]{:S(2)}) collective-permute-start(bf16[64,1536]{1,0:T(8,128)(2,1)S(1)} %get-tuple-element.91), channel_id=1, source_target_pairs={{0,14},{1,15},{2,12},{3,13},{4,10},{5,11},{6,8},{7,9},{8,6},{9,7},... | collective-permute-start | bytes 589832 | tf_op jit(solution)/shard_map/ppermute | solution.py:507
  95.0 11.9 %collective-permute-start.18 = (bf16[128,1536]{1,0:T(8,128)(2,1)S(1)}, bf16[128,1536]{1,0:T(8,128)(2,1)S(1)}, u32[]{:S(2)}, u32[]{:S(2)}) collective-permute-start(bf16[128,1536]{1,0:T(8,128)(2,1)S(1)} %get-tuple-element.99), channel_id=1, source_target_pairs={{0,1},{1,0},{2,3},{3,2},{4,5},{5,4},{6,7},{7,6},{8,9},{9,8},{10,11... | collective-permute-start | bytes 1179656 | tf_op jit(solution)/shard_map/ppermute | solution.py:507
  95.1 8.2 %collective-permute-start.19 = (bf16[3,128,256]{2,1,0:T(8,128)(2,1)S(1)}, bf16[3,128,256]{2,1,0:T(8,128)(2,1)S(1)}, u32[]{:S(2)}, u32[]{:S(2)}) collective-permute-start(bf16[3,128,256]{2,1,0:T(8,128)(2,1)S(1)} %collective-permute-done.12.refs_2_), channel_id=1, source_target_pairs={{0,4},{1,5},{2,6},{3,7},{4,0},{5,1},{6,2},{7,3},{8,12},{9,13},{10,... | collective-permute-start | bytes 589832 | tf_op jit(solution)/shard_map/ppermute | solution.py:507
  105.5 1.4 %collective-permute-start.20 = (bf16[128,384]{1,0:T(8,128)(2,1)S(1)}, bf16[128,384]{1,0:T(8,128)(2,1)S(1)}, u32[]{:S(2)}, u32[]{:S(2)}) collective-permute-start(bf16[128,384]{1,0:T(8,128)(2,1)S(1)} %get-tuple-element.104), channel_id=1, source_target_pairs={{0,1},{1,0},{2,3},{3,2},{4,5},{5,4},{6,7},{7,6},{8,9},{9,8},{10,11... | collective-permute-start | bytes 294920 | tf_op jit(solution)/shard_map/ppermute | solution.py:507
  (8 other events, 155.9 us)

commit v3 on v2

--- a/solution.py
+++ b/solution.py
@@ -19,8 +19,8 @@
 score_scale = 8.0
 MIB = 1024 * 1024
 MEMBERS = ("expert", "dp", "head")
-CHUNK_A = [8, 12, 4, 0]
-CHUNK_B = [2, 6, 10, 14]
+CHUNK_A = [8, 12, 4, 2]
+CHUNK_B = [6, 10, 14, 0]
 
 
 def layer_norm(values):
@@ -45,38 +45,34 @@
         copy.wait()
 
 
-def own_rows_kernel(own_hbm, mod_hbm, rows_ref, own, mod, sems):
-    fetch([(own_hbm, own), (mod_hbm, mod)], sems)
-    rows_ref[...] = modulate(own[0], mod)
-
-
-def own_rows(own, modulation):
-    hbm = pl.BlockSpec(memory_space=pl.ANY)
+def own_rows_kernel(own_hbm, mod_hbm, ids_hbm, rows_ref, mod_ref, ids_ref, own, sems):
+    fetch([(own_hbm, own), (mod_hbm, mod_ref), (ids_hbm, ids_ref)], sems)
+    rows_ref[...] = modulate(own[0], mod_ref)
+
+
+def own_rows(own, modulation, ids):
+    hbm, vmem = pl.BlockSpec(memory_space=pltpu.HBM), pl.BlockSpec(memory_space=pltpu.VMEM)
     return pl.pallas_call(
         own_rows_kernel,
-        in_specs=[hbm] * 2,
-        out_specs=pl.BlockSpec(memory_space=pltpu.VMEM),
-        out_shape=jax.ShapeDtypeStruct(own.shape[1:], jnp.bfloat16),
-        scratch_shapes=[
-            pltpu.VMEM(own.shape, own.dtype),
-            pltpu.VMEM(modulation.shape, modulation.dtype),
-            pltpu.SemaphoreType.DMA((2,)),
+        in_specs=[hbm] * 3,
+        out_specs=[vmem] * 3,
+        out_shape=[
+            jax.ShapeDtypeStruct(own.shape[1:], jnp.bfloat16),
+            jax.ShapeDtypeStruct(modulation.shape, modulation.dtype),
+            jax.ShapeDtypeStruct(ids.shape, ids.dtype),
         ],
+        scratch_shapes=[pltpu.VMEM(own.shape, own.dtype), pltpu.SemaphoreType.DMA((3,))],
         compiler_params=pltpu.CompilerParams(vmem_limit_bytes=16 * MIB),
         cost_estimate=pl.CostEstimate(flops=8 * own.size, bytes_accessed=4 * own.size, transcendentals=0),
         name="own_rows",
-    )(own, modulation)
+    )(own, modulation, ids)
 
 
 def prep_kernel(
-    chips, capacity, me_ref, own_ids_hbm, other_ids_hbm, own_rows_ref, other_hbm, mod_hbm, rows_ref, code_ref, *refs
+    chips, capacity, me_ref, own_ids, other_ids, own_rows_ref, other, mod, rows_ref, code_ref, *out_refs
 ):
-    out_refs, (own_ids, other_ids, other, mod, sems) = refs[:chips], refs[chips:]
     tokens = own_rows_ref.shape[0]
     both = 2 * tokens
-    fetch(
-        [(own_ids_hbm, own_ids), (other_ids_hbm, other_ids), (other_hbm, other), (mod_hbm, mod)], sems
-    )
     rows_ref[:tokens, :] = own_rows_ref[...]
     rows_ref[tokens:, :] = modulate(other[0], mod)
     me = me_ref[0]
@@ -111,23 +107,16 @@
 
 def prep(me, own_ids, other_ids, rows, other, modulation, chips, capacity):
     tokens, width = rows.shape
-    vmem, hbm = pl.BlockSpec(memory_space=pltpu.VMEM), pl.BlockSpec(memory_space=pl.ANY)
+    vmem = pl.BlockSpec(memory_space=pltpu.VMEM)
     return pl.pallas_call(
         functools.partial(prep_kernel, chips, capacity),
-        in_specs=[pl.BlockSpec(memory_space=pltpu.SMEM), hbm, hbm, vmem, hbm, hbm],
+        in_specs=[pl.BlockSpec(memory_space=pltpu.SMEM)] + [vmem] * 5,
         out_specs=[vmem] * (2 + chips),
         out_shape=[
             jax.ShapeDtypeStruct((2 * tokens, width), jnp.bfloat16),
             jax.ShapeDtypeStruct((TOP, 2 * tokens), jnp.int32),
         ]
         + [jax.ShapeDtypeStruct((2 * capacity, width), jnp.bfloat16)] * chips,
-        scratch_shapes=[
-            pltpu.VMEM(own_ids.shape, own_ids.dtype),
-            pltpu.VMEM(other_ids.shape, other_ids.dtype),
-            pltpu.VMEM(other.shape, other.dtype),
-            pltpu.VMEM(modulation.shape, modulation.dtype),
-            pltpu.SemaphoreType.DMA((4,)),
-        ],
         compiler_params=pltpu.CompilerParams(vmem_limit_bytes=16 * MIB),
         cost_estimate=pl.CostEstimate(
             flops=8 * chips * capacity * tokens * width,
@@ -155,7 +144,7 @@
 def resident(gate_weight, up_weight, down_weight):
     width, units = gate_weight.shape
     kept = RESIDENT * weight_tile(units)
-    vmem, hbm = pl.BlockSpec(memory_space=pltpu.VMEM), pl.BlockSpec(memory_space=pl.ANY)
+    vmem, hbm = pl.BlockSpec(memory_space=pltpu.VMEM), pl.BlockSpec(memory_space=pltpu.HBM)
     return pl.pallas_call(
         resident_kernel,
         in_specs=[hbm] * 3,
@@ -258,7 +247,7 @@
     units = gate_weight.shape[1]
     tile = weight_tile(units)
     rows, slots = blocks * size, 3
-    vmem, hbm = pl.BlockSpec(memory_space=pltpu.VMEM), pl.BlockSpec(memory_space=pl.ANY)
+    vmem, hbm = pl.BlockSpec(memory_space=pltpu.VMEM), pl.BlockSpec(memory_space=pltpu.HBM)
     return pl.pallas_call(
         functools.partial(ffn_kernel, blocks, units // tile),
         in_specs=[vmem] * (blocks + 3) + [hbm] * 3,
@@ -284,12 +273,12 @@
 
 
 def side_kernel(
-    rows_ref, router_hbm, own_ids_hbm, other_ids_hbm, code_ref, qkv_hbm, q_ref, kv_ref, routes_ref, router_ref,
-    own_ids_ref, other_ids_ref, qkv, sems
+    rows_ref, router_hbm, own_ids_ref, other_ids_ref, code_ref, qkv_hbm, q_ref, kv_ref, routes_ref, router_ref,
+    qkv, sems
 ):
-    copy = pltpu.make_async_copy(qkv_hbm, qkv, sems.at[3])
+    copy = pltpu.make_async_copy(qkv_hbm, qkv, sems.at[1])
     copy.start()
-    fetch([(router_hbm, router_ref), (own_ids_hbm, own_ids_ref), (other_ids_hbm, other_ids_ref)], sems)
+    fetch([(router_hbm, router_ref)], sems)
     logits = lax.dot_general(
         router_ref[...],
         rows_ref[...].astype(jnp.float32),
@@ -324,10 +313,10 @@
 
 def side(rows, router, own_ids, other_ids, code, qkv):
     heads, _, tokens = qkv.shape
-    vmem, hbm = pl.BlockSpec(memory_space=pltpu.VMEM), pl.BlockSpec(memory_space=pl.ANY)
+    vmem, hbm = pl.BlockSpec(memory_space=pltpu.VMEM), pl.BlockSpec(memory_space=pltpu.HBM)
     return pl.pallas_call(
         side_kernel,
-        in_specs=[vmem, hbm, hbm, hbm, vmem, hbm],
+        in_specs=[vmem, hbm, vmem, vmem, vmem, hbm],
         out_specs=[vmem] * 3,
         out_shape=[
             jax.ShapeDtypeStruct((heads, HD, tokens), jnp.bfloat16),
@@ -336,10 +325,8 @@
         ],
         scratch_shapes=[
             pltpu.VMEM(router.shape, router.dtype),
-            pltpu.VMEM(own_ids.shape, own_ids.dtype),
-            pltpu.VMEM(other_ids.shape, other_ids.dtype),
             pltpu.VMEM(qkv.shape, qkv.dtype),
-            pltpu.SemaphoreType.DMA((4,)),
+            pltpu.SemaphoreType.DMA((2,)),
         ],
         compiler_params=pltpu.CompilerParams(vmem_limit_bytes=16 * MIB),
         cost_estimate=pl.CostEstimate(
@@ -404,7 +391,8 @@
     )(head, queries, *kv_pieces, guide_out)
 
 
-def combine_kernel(blocks, parity, routes_ref, *refs):
+def combine_kernel(chips, routes_ref, *refs):
+    blocks = len(chips)
     row_refs, refs = refs[:blocks], refs[blocks:]
     before_refs, (keep_ref, send_ref, rows, sems) = refs[:-4], refs[-4:]
     size = row_refs[0].shape[0]
@@ -415,7 +403,11 @@
         fetch([(row_refs[i], rows.at[pl.ds(i * size, size), :]) for i in range(blocks)], sems)
     tokens = routes_ref.shape[0] // 2
     lane = lax.broadcasted_iota(jnp.int32, (tokens, blocks * size), 1)
-    slots = (lane + (lax.div(lane, size) + parity) * size).astype(jnp.float32)
+    slots = lane
+    for i, chip in enumerate(chips):
+        inside = jnp.logical_and(lane >= i * size, lane < (i + 1) * size)
+        slots = jnp.where(inside, lane + (chip - i) * size, slots)
+    slots = slots.astype(jnp.float32)
     for i, out_ref in enumerate((keep_ref, send_ref)):
         part = slice(i * tokens, (i + 1) * tokens)
         first = routes_ref[part, 0:1]
@@ -427,13 +419,13 @@
         out_ref[...] = total.astype(out_ref.dtype)
 
 
-def combine(row_blocks, parity, routes, before, send_type):
+def combine(row_blocks, chips, routes, before, send_type):
     blocks = len(row_blocks)
     size, width = row_blocks[0].shape
     tokens = routes.shape[0] // 2
     vmem = pl.BlockSpec(memory_space=pltpu.VMEM)
     return pl.pallas_call(
-        functools.partial(combine_kernel, blocks, parity),
+        functools.partial(combine_kernel, chips),
         in_specs=[vmem] + [vmem if before else pl.BlockSpec(memory_space=pl.ANY)] * blocks + [vmem] * len(before),
         out_specs=[vmem] * 2,
         out_shape=[
@@ -510,13 +502,13 @@
     ids = jnp.transpose(route_ids, (0, 2, 1))
     other = swap(hidden, 1)
     other_ids = swap(ids, 1)
-    rows = own_rows(hidden, modulation)
-    rows, code, *outgoing = prep(me, ids, other_ids, rows, other, modulation, devices // 2, capacity)
+    rows, near_modulation, near_ids = own_rows(hidden, modulation, ids)
+    rows, code, *outgoing = prep(
+        me, near_ids, other_ids, rows, other, near_modulation, devices // 2, capacity
+    )
     rows_a = [swap(outgoing[k // 2], k) for k in CHUNK_A]
     rows_b = [swap(outgoing[k // 2], k) for k in CHUNK_B]
-    queries, kv, routes = side(
-        rows, router_weight.T, ids, other_ids, code, jnp.transpose(guide_qkv[0], (1, 2, 0))
-    )
+    queries, kv, routes = side(rows, router_weight.T, near_ids, other_ids, code, jnp.transpose(guide_qkv[0], (1, 2, 0)))
     weights, _ = lax.optimization_barrier(((gate_weight, up_weight, down_weight), routes))
     kept = resident(*weights)
     far = swap(kv, 8)
@@ -533,10 +525,8 @@
 
     keep, send = attend(head, queries, [kv, near, far, relayed], guide_out)
     got = swap(send, 1)
-    sums = combine([block for _, block in sorted(zip(CHUNK_A, back_a), key=lambda pair: pair[0])], 0, routes, (), jnp.float32)
-    keep_moe, send_moe = combine(
-        [block for _, block in sorted(zip(CHUNK_B, back_b), key=lambda pair: pair[0])], 1, routes, sums, jnp.bfloat16
-    )
+    sums = combine(back_a, [k // 2 for k in CHUNK_A], routes, (), jnp.float32)
+    keep_moe, send_moe = combine(back_b, [k // 2 for k in CHUNK_B], routes, sums, jnp.bfloat16)
     got_moe = swap(send_moe, 1)
     result = finish(
         keep_moe, got_moe, hidden, modulation, main_final.T, keep, got, guide_final.T,

time: 108 us -> 112 us (1.037)
  starting transfers between devices: 32 us -> 36.9 us
    ppermute x21, starting transfers between devices: 32 us -> 36.9 us  [swap(): return lax.ppermute(block, MEMBERS, [(i, i ^ k) for i in range(devices)])]
  transfers between devices with their start and end apart: 21 -> 21, of which waited for: 4 -> 4; matrix products, arithmetic and copies ran while one was open for 0% -> 0% of each run, Pallas kernels for 43% -> 42%
where the time goes in v3:
time: 112 us
  Pallas kernels  50.2 us (45%)
  starting transfers between devices  36.9 us (33%)
  waiting for transfers between devices  19.2 us (17%)
  local copies, waits for them, and re-layouts  4.28 us (4%)
  between operations  1.54 us (1%)
    pallas_call x2, Pallas kernels, ffn(): pl.pallas_call(functools.partial(ffn_kernel, blocks, units // tile), in_s...  37.4 us
    ppermute x21, starting transfers between devices, swap(): return lax.ppermute(block, MEMBERS, [(i, i ^ k) for i in range(devices)])  36.9 us
    ppermute x21, waiting for transfers between devices, swap(): return lax.ppermute(block, MEMBERS, [(i, i ^ k) for i in range(devices)])  19.2 us
    unnamed x22, local copies, waits for them, and re-layouts  4.28 us
    pallas_call x1, Pallas kernels, resident(): pl.pallas_call(resident_kernel, in_specs=[hbm] * 3, out_specs=[vmem] * 3,...  3.14 us
    pallas_call x2, Pallas kernels, combine(): pl.pallas_call(functools.partial(combine_kernel, chips), in_specs=[vmem]...  2.35 us
  transfers between devices with their start and end apart: 21, of which 4 were waited for; matrix products, arithmetic and copies ran while one was open for 0% of the time, Pallas kernels for 42%

profile of v3, /device:TPU:0, one launch (start us, length us, event | category | flops | bytes accessed | tf_op | source)
XLA Modules:
  0.0 112.1 jit_solution(2744453213111083176)
XLA Ops:
  3.5 1.5 %prep.1 = (bf16[256,1536]{1,0:T(8,128)(2,1)S(1)}, s32[2,256]{1,0:T(2,128)S(1)}, bf16[64,1536]{1,0:T(8,128)(2,1)S(1)}, bf16[64,1536]{1,0:T(8,128)(2,1)S(1)}, bf16...) custom-call(s32[1]{0:T(128)} %bitcast.me_ref, ...), custom_call_target="tpu_custom_call" | custom-call | flops 402653184 | bytes 1572864 | tf_op jit(solution)/shard_map/prep/pallas_call | solution.py:111
  5.0 4.1 %collective-permute-start.2 = (bf16[64,1536]{1,0:T(8,128)(2,1)S(1)}, bf16[64,1536]{1,0:T(8,128)(2,1)S(1)}, u32[]{:S(2)}, u32[]{:S(2)}) collective-permute-start(bf16[64,1536]{1,0:T(8,128)(2,1)S(1)} %get-tuple-element.61), channel_id=1, source_target_pairs={{0,8},{1,9},{2,10},{3,11},{4,12},{5,13},{6,14},{7,15},{8,0},{9,1},... | collective-permute-start | bytes 589832 | tf_op jit(solution)/shard_map/ppermute | solution.py:499
  9.2 1.3 %collective-permute-start.3 = (bf16[64,1536]{1,0:T(8,128)(2,1)S(1)}, bf16[64,1536]{1,0:T(8,128)(2,1)S(1)}, u32[]{:S(2)}, u32[]{:S(2)}) collective-permute-start(bf16[64,1536]{1,0:T(8,128)(2,1)S(1)} %get-tuple-element.62), channel_id=1, source_target_pairs={{0,12},{1,13},{2,14},{3,15},{4,8},{5,9},{6,10},{7,11},{8,4},{9,5},... | collective-permute-start | bytes 589832 | tf_op jit(solution)/shard_map/ppermute | solution.py:499
  10.7 1.5 %collective-permute-start.5 = (bf16[64,1536]{1,0:T(8,128)(2,1)S(1)}, bf16[64,1536]{1,0:T(8,128)(2,1)S(1)}, u32[]{:S(2)}, u32[]{:S(2)}) collective-permute-start(bf16[64,1536]{1,0:T(8,128)(2,1)S(1)} %get-tuple-element.64), channel_id=1, source_target_pairs={{0,2},{1,3},{2,0},{3,1},{4,6},{5,7},{6,4},{7,5},{8,10},{9,11},{10,... | collective-permute-start | bytes 589832 | tf_op jit(solution)/shard_map/ppermute | solution.py:499
  14.1 1.8 %side.1 = (bf16[3,64,256]{2,1,0:T(8,128)(2,1)S(1)}, bf16[3,128,256]{2,1,0:T(8,128)(2,1)S(1)}, f32[256,8]{1,0:T(8,128)S(1)}) custom-call(bf16[256,1536]{1,0:T(8,128)(2,1)S(1)} %get-tuple-element.65.rows_ref, f32[16,1536]{1,0:T(8,128)S(1)} %bitcast.13, s32[1,2,128]{2,1,0:T(2,128)S(1)} %get-tuple-element.58.own_ids.own_ids_ref, ...), custom_call_target="tpu_custom_call" | custom-call | flops 76382208 | bytes 589824 | tf_op jit(solution)/shard_map/side/pallas_call | solution.py:317
  15.9 2.9 %collective-permute-start.13 = (bf16[3,128,256]{2,1,0:T(8,128)(2,1)S(1)}, bf16[3,128,256]{2,1,0:T(8,128)(2,1)S(1)}, u32[]{:S(2)}, u32[]{:S(2)}) collective-permute-start(bf16[3,128,256]{2,1,0:T(8,128)(2,1)S(1)} %get-tuple-element.93.refs_0_), channel_id=1, source_target_pairs={{0,8},{1,9},{2,10},{3,11},{4,12},{5,13},{6,14},{7,15},{8,0},{9,1},... | collective-permute-start | bytes 589832 | tf_op jit(solution)/shard_map/ppermute | solution.py:499
  18.7 3.1 %resident.1 = (bf16[1536,768]{1,0:T(8,128)(2,1)S(1)}, bf16[1536,768]{1,0:T(8,128)(2,1)S(1)}, bf16[768,1536]{1,0:T(8,128)(2,1)S(1)}) custom-call(bf16[1536,6144]{1,0:T(8,128)(2,1)} %refs_7_.3, bf16[1536,6144]{1,0:T(8,128)(2,1)} %refs_8_.3, bf16[6144,1536]{1,0:T(8,128)(2,1)} %refs_9_.3), custom_call_target="tpu_custom_call" | custom-call | bytes 7077888 | tf_op jit(solution)/shard_map/resident/pallas_call | solution.py:148
  21.9 2.0 %collective-permute-done.2.refs_0_ = bf16[64,1536]{1,0:T(8,128)(2,1)S(1)} collective-permute-done((bf16[64,1536]{1,0:T(8,128)(2,1)S(1)}, bf16[64,1536]{1,0:T(8,128)(2,1)S(1)}, u32[]{:S(2)}, u32[]{:S(2)}) %collective-permute-start.2) | collective-permute-done | bytes 196640 | tf_op jit(solution)/shard_map/ppermute | solution.py:499
  24.2 9.4 %collective-permute-start.6 = (bf16[64,1536]{1,0:T(8,128)(2,1)S(1)}, bf16[64,1536]{1,0:T(8,128)(2,1)S(1)}, u32[]{:S(2)}, u32[]{:S(2)}) collective-permute-start(bf16[64,1536]{1,0:T(8,128)(2,1)S(1)} %get-tuple-element.70), channel_id=1, source_target_pairs={{0,6},{1,7},{2,4},{3,5},{4,2},{5,3},{6,0},{7,1},{8,14},{9,15},{10,... | collective-permute-start | bytes 589832 | tf_op jit(solution)/shard_map/ppermute | solution.py:499
  33.6 1.1 %collective-permute-start.7 = (bf16[64,1536]{1,0:T(8,128)(2,1)S(1)}, bf16[64,1536]{1,0:T(8,128)(2,1)S(1)}, u32[]{:S(2)}, u32[]{:S(2)}) collective-permute-start(bf16[64,1536]{1,0:T(8,128)(2,1)S(1)} %get-tuple-element.71), channel_id=1, source_target_pairs={{0,10},{1,11},{2,8},{3,9},{4,14},{5,15},{6,12},{7,13},{8,2},{9,3},... | collective-permute-start | bytes 589832 | tf_op jit(solution)/shard_map/ppermute | solution.py:499
  34.8 1.5 %collective-permute-start.8 = (bf16[64,1536]{1,0:T(8,128)(2,1)S(1)}, bf16[64,1536]{1,0:T(8,128)(2,1)S(1)}, u32[]{:S(2)}, u32[]{:S(2)}) collective-permute-start(bf16[64,1536]{1,0:T(8,128)(2,1)S(1)} %get-tuple-element.72), channel_id=1, source_target_pairs={{0,14},{1,15},{2,12},{3,13},{4,10},{5,11},{6,8},{7,9},{8,6},{9,7},... | collective-permute-start | bytes 589832 | tf_op jit(solution)/shard_map/ppermute | solution.py:499
  36.3 18.7 %ffn.3 = (bf16[64,1536]{1,0:T(8,128)(2,1)S(1)}, bf16[64,1536]{1,0:T(8,128)(2,1)S(1)}, bf16[64,1536]{1,0:T(8,128)(2,1)S(1)}, bf16[64,1536]{1,0:T(8,128)(2,1)S(1)}) custom-call(bf16[64,1536]{1,0:T(8,128)(2,1)S(1)} %collective-permute-done.2.refs_0_, bf16[64,1536]{1,0:T(8,128)(2,1)S(1)} %collective-permute-done.3.refs_1_, ...), custom_call_target="tpu_custom_call" | custom-call | flops 14495514624 | bytes 56623104 | tf_op jit(solution)/shard_map/ffn/pallas_call | solution.py:251
  55.0 3.0 %collective-permute-start.9 = (bf16[64,1536]{1,0:T(8,128)(2,1)S(1)}, bf16[64,1536]{1,0:T(8,128)(2,1)S(1)}, u32[]{:S(2)}, u32[]{:S(2)}) collective-permute-start(bf16[64,1536]{1,0:T(8,128)(2,1)S(1)} %get-tuple-element.89), channel_id=1, source_target_pairs={{0,8},{1,9},{2,10},{3,11},{4,12},{5,13},{6,14},{7,15},{8,0},{9,1},... | collective-permute-start | bytes 589832 | tf_op jit(solution)/shard_map/ppermute | solution.py:499
  58.0 1.2 %collective-permute-start.10 = (bf16[64,1536]{1,0:T(8,128)(2,1)S(1)}, bf16[64,1536]{1,0:T(8,128)(2,1)S(1)}, u32[]{:S(2)}, u32[]{:S(2)}) collective-permute-start(bf16[64,1536]{1,0:T(8,128)(2,1)S(1)} %get-tuple-element.90), channel_id=1, source_target_pairs={{0,12},{1,13},{2,14},{3,15},{4,8},{5,9},{6,10},{7,11},{8,4},{9,5},... | collective-permute-start | bytes 589832 | tf_op jit(solution)/shard_map/ppermute | solution.py:499
  60.1 18.7 %ffn.2 = (bf16[64,1536]{1,0:T(8,128)(2,1)S(1)}, bf16[64,1536]{1,0:T(8,128)(2,1)S(1)}, bf16[64,1536]{1,0:T(8,128)(2,1)S(1)}, bf16[64,1536]{1,0:T(8,128)(2,1)S(1)}) custom-call(bf16[64,1536]{1,0:T(8,128)(2,1)S(1)} %collective-permute-done.6.refs_0_, bf16[64,1536]{1,0:T(8,128)(2,1)S(1)} %collective-permute-done.7.refs_1_, ...), custom_call_target="tpu_custom_call" | custom-call | flops 14495514624 | bytes 56623104 | tf_op jit(solution)/shard_map/ffn/pallas_call | solution.py:251
  78.9 2.7 %collective-permute-start.15 = (bf16[64,1536]{1,0:T(8,128)(2,1)S(1)}, bf16[64,1536]{1,0:T(8,128)(2,1)S(1)}, u32[]{:S(2)}, u32[]{:S(2)}) collective-permute-start(bf16[64,1536]{1,0:T(8,128)(2,1)S(1)} %get-tuple-element.94), channel_id=1, source_target_pairs={{0,6},{1,7},{2,4},{3,5},{4,2},{5,3},{6,0},{7,1},{8,14},{9,15},{10,... | collective-permute-start | bytes 589832 | tf_op jit(solution)/shard_map/ppermute | solution.py:499
  81.6 1.2 %collective-permute-start.16 = (bf16[64,1536]{1,0:T(8,128)(2,1)S(1)}, bf16[64,1536]{1,0:T(8,128)(2,1)S(1)}, u32[]{:S(2)}, u32[]{:S(2)}) collective-permute-start(bf16[64,1536]{1,0:T(8,128)(2,1)S(1)} %get-tuple-element.95), channel_id=1, source_target_pairs={{0,10},{1,11},{2,8},{3,9},{4,14},{5,15},{6,12},{7,13},{8,2},{9,3},... | collective-permute-start | bytes 589832 | tf_op jit(solution)/shard_map/ppermute | solution.py:499
  82.8 2.1 %collective-permute-start.17 = (bf16[64,1536]{1,0:T(8,128)(2,1)S(1)}, bf16[64,1536]{1,0:T(8,128)(2,1)S(1)}, u32[]{:S(2)}, u32[]{:S(2)}) collective-permute-start(bf16[64,1536]{1,0:T(8,128)(2,1)S(1)} %get-tuple-element.96), channel_id=1, source_target_pairs={{0,14},{1,15},{2,12},{3,13},{4,10},{5,11},{6,8},{7,9},{8,6},{9,7},... | collective-permute-start | bytes 589832 | tf_op jit(solution)/shard_map/ppermute | solution.py:499
  84.9 1.6 %combine.2 = (f32[128,1536]{1,0:T(8,128)S(1)}, f32[128,1536]{1,0:T(8,128)S(1)}) custom-call(f32[256,8]{1,0:T(8,128)S(1)} %get-tuple-element.69.routes_ref, bf16[64,1536]{1,0:T(8,128)(2,1)S(1)} %collective-permute-done.9.refs_0_, bf16[64,1536]{1,0:T(8,128)(2,1)S(1)} %collective-permute-done.10.refs_1_, bf16[64,1536]{1,0:T(8,128)(2,1)S(1)} %collective-permute-done.11.refs_2_, ...), custom_call_target="tpu_custom_call" | custom-call | flops 402653184 | bytes 786432 | tf_op jit(solution)/shard_map/combine/pallas_call | solution.py:427
  87.1 11.1 %collective-permute-done.16.refs_1_ = bf16[64,1536]{1,0:T(8,128)(2,1)S(1)} collective-permute-done((bf16[64,1536]{1,0:T(8,128)(2,1)S(1)}, bf16[64,1536]{1,0:T(8,128)(2,1)S(1)}, u32[]{:S(2)}, u32[]{:S(2)}) %collective-permute-start.16) | collective-permute-done | bytes 196640 | tf_op jit(solution)/shard_map/ppermute | solution.py:499
  99.0 2.7 %collective-permute-start.19 = (bf16[3,128,256]{2,1,0:T(8,128)(2,1)S(1)}, bf16[3,128,256]{2,1,0:T(8,128)(2,1)S(1)}, u32[]{:S(2)}, u32[]{:S(2)}) collective-permute-start(bf16[3,128,256]{2,1,0:T(8,128)(2,1)S(1)} %collective-permute-done.13.refs_2_), channel_id=1, source_target_pairs={{0,4},{1,5},{2,6},{3,7},{4,0},{5,1},{6,2},{7,3},{8,12},{9,13},{10,... | collective-permute-start | bytes 589832 | tf_op jit(solution)/shard_map/ppermute | solution.py:499
  101.7 5.5 %collective-permute-done.19.refs_3_ = bf16[3,128,256]{2,1,0:T(8,128)(2,1)S(1)} collective-permute-done((bf16[3,128,256]{2,1,0:T(8,128)(2,1)S(1)}, bf16[3,128,256]{2,1,0:T(8,128)(2,1)S(1)}, u32[]{:S(2)}, u32[]{:S(2)}) %collective-permute-start.19) | collective-permute-done | bytes 196640 | tf_op jit(solution)/shard_map/ppermute | solution.py:499
  107.2 2.2 %attend.1 = (f32[128,384]{1,0:T(8,128)S(1)}, bf16[128,384]{1,0:T(8,128)(2,1)S(1)}) custom-call(s32[1]{0:T(128)} %bitcast.7.head_ref, bf16[3,64,256]{2,1,0:T(8,128)(2,1)S(1)} %get-tuple-element.106.q_ref, bf16[3,128,256]{2,1,0:T(8,128)(2,1)S(1)} %get-tuple-element.93.refs_0_, bf16[3,128,256]{2,1,0:T(8,128)(2,1)S(1)} %collective-permute-done.14.refs_1_, ...), custom_call_target="tpu_custom_call" | custom-call | flops 201326592 | bytes 786432 | tf_op jit(solution)/shard_map/attend/pallas_call | solution.py:375
  110.8 1.2 %finish.1 = f32[1,16,128]{2,1,0:T(8,128)} custom-call(f32[128,1536]{1,0:T(8,128)S(1)} %get-tuple-element.104.keep_moe_ref, bf16[128,1536]{1,0:T(8,128)(2,1)S(1)} %collective-permute-done.18.got_moe_ref, bf16[1,128,1536]{2,1,0:T(8,128)(2,1)S(1)} %copy-done.1, f32[3,1,1536]{2,1,0:T(1,128)S(1)} %bitcast.15, bf16[16,1536]{1,0:T(8,128)(2,1)S(1)} %bitcast.16, ...), custom_call_target="tpu_custom_call" | custom-call | flops 12582912 | bytes 1572864 | tf_op jit(solution)/shard_map/finish/pallas_call | solution.py:471
  (50 shorter events, 8.2 us)
Async XLA Ops:
  0.0 3.5 %collective-permute-start.1 = (bf16[1,128,1536]{2,1,0:T(8,128)(2,1)}, bf16[1,128,1536]{2,1,0:T(8,128)(2,1)S(1)}, u32[]{:S(2)}, u32[]{:S(2)}) collective-permute-start(bf16[1,128,1536]{2,1,0:T(8,128)(2,1)} %hidden_ref.1), channel_id=1, source_target_pairs={{0,1},{1,0},{2,3},{3,2},{4,5},{5,4},{6,7},{7,6},{8,9},{9,8},{10,11... | collective-permute-start | bytes 1179656 | tf_op jit(solution)/shard_map/ppermute | solution.py:499
  0.5 3.0 %collective-permute-start = (s32[1,2,128]{2,1,0:T(2,128)}, s32[1,2,128]{2,1,0:T(2,128)S(1)}, u32[]{:S(2)}, u32[]{:S(2)}) collective-permute-start(s32[1,2,128]{2,1,0:T(2,128)} %bitcast.19), channel_id=1, source_target_pairs={{0,1},{1,0},{2,3},{3,2},{4,5},{5,4},{6,7},{7,6},{8,9},{9,8},{10,11... | collective-permute-start | bytes 3080 | tf_op jit(solution)/shard_map/ppermute | solution.py:499
  5.0 18.9 %collective-permute-start.2 = (bf16[64,1536]{1,0:T(8,128)(2,1)S(1)}, bf16[64,1536]{1,0:T(8,128)(2,1)S(1)}, u32[]{:S(2)}, u32[]{:S(2)}) collective-permute-start(bf16[64,1536]{1,0:T(8,128)(2,1)S(1)} %get-tuple-element.61), channel_id=1, source_target_pairs={{0,8},{1,9},{2,10},{3,11},{4,12},{5,13},{6,14},{7,15},{8,0},{9,1},... | collective-permute-start | bytes 589832 | tf_op jit(solution)/shard_map/ppermute | solution.py:499
  9.2 15.0 %collective-permute-start.3 = (bf16[64,1536]{1,0:T(8,128)(2,1)S(1)}, bf16[64,1536]{1,0:T(8,128)(2,1)S(1)}, u32[]{:S(2)}, u32[]{:S(2)}) collective-permute-start(bf16[64,1536]{1,0:T(8,128)(2,1)S(1)} %get-tuple-element.62), channel_id=1, source_target_pairs={{0,12},{1,13},{2,14},{3,15},{4,8},{5,9},{6,10},{7,11},{8,4},{9,5},... | collective-permute-start | bytes 589832 | tf_op jit(solution)/shard_map/ppermute | solution.py:499
  10.5 23.1 %collective-permute-start.4 = (bf16[64,1536]{1,0:T(8,128)(2,1)S(1)}, bf16[64,1536]{1,0:T(8,128)(2,1)S(1)}, u32[]{:S(2)}, u32[]{:S(2)}) collective-permute-start(bf16[64,1536]{1,0:T(8,128)(2,1)S(1)} %get-tuple-element.63), channel_id=1, source_target_pairs={{0,4},{1,5},{2,6},{3,7},{4,0},{5,1},{6,2},{7,3},{8,12},{9,13},{10,... | collective-permute-start | bytes 589832 | tf_op jit(solution)/shard_map/ppermute | solution.py:499
  10.7 24.1 %collective-permute-start.5 = (bf16[64,1536]{1,0:T(8,128)(2,1)S(1)}, bf16[64,1536]{1,0:T(8,128)(2,1)S(1)}, u32[]{:S(2)}, u32[]{:S(2)}) collective-permute-start(bf16[64,1536]{1,0:T(8,128)(2,1)S(1)} %get-tuple-element.64), channel_id=1, source_target_pairs={{0,2},{1,3},{2,0},{3,1},{4,6},{5,7},{6,4},{7,5},{8,10},{9,11},{10,... | collective-permute-start | bytes 589832 | tf_op jit(solution)/shard_map/ppermute | solution.py:499
  15.9 43.3 %collective-permute-start.13 = (bf16[3,128,256]{2,1,0:T(8,128)(2,1)S(1)}, bf16[3,128,256]{2,1,0:T(8,128)(2,1)S(1)}, u32[]{:S(2)}, u32[]{:S(2)}) collective-permute-start(bf16[3,128,256]{2,1,0:T(8,128)(2,1)S(1)} %get-tuple-element.93.refs_0_), channel_id=1, source_target_pairs={{0,8},{1,9},{2,10},{3,11},{4,12},{5,13},{6,14},{7,15},{8,0},{9,1},... | collective-permute-start | bytes 589832 | tf_op jit(solution)/shard_map/ppermute | solution.py:499
  23.9 54.9 %collective-permute-start.14 = (bf16[3,128,256]{2,1,0:T(8,128)(2,1)S(1)}, bf16[3,128,256]{2,1,0:T(8,128)(2,1)S(1)}, u32[]{:S(2)}, u32[]{:S(2)}) collective-permute-start(bf16[3,128,256]{2,1,0:T(8,128)(2,1)S(1)} %get-tuple-element.93.refs_0_), channel_id=1, source_target_pairs={{0,4},{1,5},{2,6},{3,7},{4,0},{5,1},{6,2},{7,3},{8,12},{9,13},{10,... | collective-permute-start | bytes 589832 | tf_op jit(solution)/shard_map/ppermute | solution.py:499
  24.2 30.8 %collective-permute-start.6 = (bf16[64,1536]{1,0:T(8,128)(2,1)S(1)}, bf16[64,1536]{1,0:T(8,128)(2,1)S(1)}, u32[]{:S(2)}, u32[]{:S(2)}) collective-permute-start(bf16[64,1536]{1,0:T(8,128)(2,1)S(1)} %get-tuple-element.70), channel_id=1, source_target_pairs={{0,6},{1,7},{2,4},{3,5},{4,2},{5,3},{6,0},{7,1},{8,14},{9,15},{10,... | collective-permute-start | bytes 589832 | tf_op jit(solution)/shard_map/ppermute | solution.py:499
  33.6 24.3 %collective-permute-start.7 = (bf16[64,1536]{1,0:T(8,128)(2,1)S(1)}, bf16[64,1536]{1,0:T(8,128)(2,1)S(1)}, u32[]{:S(2)}, u32[]{:S(2)}) collective-permute-start(bf16[64,1536]{1,0:T(8,128)(2,1)S(1)} %get-tuple-element.71), channel_id=1, source_target_pairs={{0,10},{1,11},{2,8},{3,9},{4,14},{5,15},{6,12},{7,13},{8,2},{9,3},... | collective-permute-start | bytes 589832 | tf_op jit(solution)/shard_map/ppermute | solution.py:499
  34.8 24.4 %collective-permute-start.8 = (bf16[64,1536]{1,0:T(8,128)(2,1)S(1)}, bf16[64,1536]{1,0:T(8,128)(2,1)S(1)}, u32[]{:S(2)}, u32[]{:S(2)}) collective-permute-start(bf16[64,1536]{1,0:T(8,128)(2,1)S(1)} %get-tuple-element.72), channel_id=1, source_target_pairs={{0,14},{1,15},{2,12},{3,13},{4,10},{5,11},{6,8},{7,9},{8,6},{9,7},... | collective-permute-start | bytes 589832 | tf_op jit(solution)/shard_map/ppermute | solution.py:499
  55.0 23.8 %collective-permute-start.9 = (bf16[64,1536]{1,0:T(8,128)(2,1)S(1)}, bf16[64,1536]{1,0:T(8,128)(2,1)S(1)}, u32[]{:S(2)}, u32[]{:S(2)}) collective-permute-start(bf16[64,1536]{1,0:T(8,128)(2,1)S(1)} %get-tuple-element.89), channel_id=1, source_target_pairs={{0,8},{1,9},{2,10},{3,11},{4,12},{5,13},{6,14},{7,15},{8,0},{9,1},... | collective-permute-start | bytes 589832 | tf_op jit(solution)/shard_map/ppermute | solution.py:499
  58.0 20.9 %collective-permute-start.10 = (bf16[64,1536]{1,0:T(8,128)(2,1)S(1)}, bf16[64,1536]{1,0:T(8,128)(2,1)S(1)}, u32[]{:S(2)}, u32[]{:S(2)}) collective-permute-start(bf16[64,1536]{1,0:T(8,128)(2,1)S(1)} %get-tuple-element.90), channel_id=1, source_target_pairs={{0,12},{1,13},{2,14},{3,15},{4,8},{5,9},{6,10},{7,11},{8,4},{9,5},... | collective-permute-start | bytes 589832 | tf_op jit(solution)/shard_map/ppermute | solution.py:499
  59.2 19.7 %collective-permute-start.11 = (bf16[64,1536]{1,0:T(8,128)(2,1)S(1)}, bf16[64,1536]{1,0:T(8,128)(2,1)S(1)}, u32[]{:S(2)}, u32[]{:S(2)}) collective-permute-start(bf16[64,1536]{1,0:T(8,128)(2,1)S(1)} %get-tuple-element.91), channel_id=1, source_target_pairs={{0,4},{1,5},{2,6},{3,7},{4,0},{5,1},{6,2},{7,3},{8,12},{9,13},{10,... | collective-permute-start | bytes 589832 | tf_op jit(solution)/shard_map/ppermute | solution.py:499
  59.2 19.7 %collective-permute-start.12 = (bf16[64,1536]{1,0:T(8,128)(2,1)S(1)}, bf16[64,1536]{1,0:T(8,128)(2,1)S(1)}, u32[]{:S(2)}, u32[]{:S(2)}) collective-permute-start(bf16[64,1536]{1,0:T(8,128)(2,1)S(1)} %get-tuple-element.92), channel_id=1, source_target_pairs={{0,2},{1,3},{2,0},{3,1},{4,6},{5,7},{6,4},{7,5},{8,10},{9,11},{10,... | collective-permute-start | bytes 589832 | tf_op jit(solution)/shard_map/ppermute | solution.py:499
  60.1 50.7 %copy-start.6 = (bf16[1536,16]{0,1:T(8,128)(2,1)S(1)}, bf16[1536,16]{0,1:T(8,128)(2,1)}, u32[]{:S(2)}) copy-start(bf16[1536,16]{0,1:T(8,128)(2,1)} %param.21) | copy-start | bytes 147460
  60.1 50.7 %copy-start.7 = (bf16[384,16]{0,1:T(8,128)(2,1)S(1)}, bf16[384,16]{0,1:T(8,128)(2,1)}, u32[]{:S(2)}) copy-start(bf16[384,16]{0,1:T(8,128)(2,1)} %param.24) | copy-start | bytes 36868
  60.1 50.7 %copy-start.8 = (f32[1,128,16]{1,2,0:T(8,128)S(1)}, f32[1,128,16]{1,2,0:T(8,128)}, u32[]{:S(2)}) copy-start(f32[1,128,16]{1,2,0:T(8,128)} %param.25) | copy-start | bytes 24580
  78.9 8.2 %collective-permute-start.15 = (bf16[64,1536]{1,0:T(8,128)(2,1)S(1)}, bf16[64,1536]{1,0:T(8,128)(2,1)S(1)}, u32[]{:S(2)}, u32[]{:S(2)}) collective-permute-start(bf16[64,1536]{1,0:T(8,128)(2,1)S(1)} %get-tuple-element.94), channel_id=1, source_target_pairs={{0,6},{1,7},{2,4},{3,5},{4,2},{5,3},{6,0},{7,1},{8,14},{9,15},{10,... | collective-permute-start | bytes 589832 | tf_op jit(solution)/shard_map/ppermute | solution.py:499
  81.6 16.6 %collective-permute-start.16 = (bf16[64,1536]{1,0:T(8,128)(2,1)S(1)}, bf16[64,1536]{1,0:T(8,128)(2,1)S(1)}, u32[]{:S(2)}, u32[]{:S(2)}) collective-permute-start(bf16[64,1536]{1,0:T(8,128)(2,1)S(1)} %get-tuple-element.95), channel_id=1, source_target_pairs={{0,10},{1,11},{2,8},{3,9},{4,14},{5,15},{6,12},{7,13},{8,2},{9,3},... | collective-permute-start | bytes 589832 | tf_op jit(solution)/shard_map/ppermute | solution.py:499
  82.8 15.4 %collective-permute-start.17 = (bf16[64,1536]{1,0:T(8,128)(2,1)S(1)}, bf16[64,1536]{1,0:T(8,128)(2,1)S(1)}, u32[]{:S(2)}, u32[]{:S(2)}) collective-permute-start(bf16[64,1536]{1,0:T(8,128)(2,1)S(1)} %get-tuple-element.96), channel_id=1, source_target_pairs={{0,14},{1,15},{2,12},{3,13},{4,10},{5,11},{6,8},{7,9},{8,6},{9,7},... | collective-permute-start | bytes 589832 | tf_op jit(solution)/shard_map/ppermute | solution.py:499
  98.9 11.9 %collective-permute-start.18 = (bf16[128,1536]{1,0:T(8,128)(2,1)S(1)}, bf16[128,1536]{1,0:T(8,128)(2,1)S(1)}, u32[]{:S(2)}, u32[]{:S(2)}) collective-permute-start(bf16[128,1536]{1,0:T(8,128)(2,1)S(1)} %get-tuple-element.105), channel_id=1, source_target_pairs={{0,1},{1,0},{2,3},{3,2},{4,5},{5,4},{6,7},{7,6},{8,9},{9,8},{10,11... | collective-permute-start | bytes 1179656 | tf_op jit(solution)/shard_map/ppermute | solution.py:499
  99.0 8.2 %collective-permute-start.19 = (bf16[3,128,256]{2,1,0:T(8,128)(2,1)S(1)}, bf16[3,128,256]{2,1,0:T(8,128)(2,1)S(1)}, u32[]{:S(2)}, u32[]{:S(2)}) collective-permute-start(bf16[3,128,256]{2,1,0:T(8,128)(2,1)S(1)} %collective-permute-done.13.refs_2_), channel_id=1, source_target_pairs={{0,4},{1,5},{2,6},{3,7},{4,0},{5,1},{6,2},{7,3},{8,12},{9,13},{10,... | collective-permute-start | bytes 589832 | tf_op jit(solution)/shard_map/ppermute | solution.py:499
  109.4 1.4 %collective-permute-start.20 = (bf16[128,384]{1,0:T(8,128)(2,1)S(1)}, bf16[128,384]{1,0:T(8,128)(2,1)S(1)}, u32[]{:S(2)}, u32[]{:S(2)}) collective-permute-start(bf16[128,384]{1,0:T(8,128)(2,1)S(1)} %get-tuple-element.110), channel_id=1, source_target_pairs={{0,1},{1,0},{2,3},{3,2},{4,5},{5,4},{6,7},{7,6},{8,9},{9,8},{10,11... | collective-permute-start | bytes 294920 | tf_op jit(solution)/shard_map/ppermute | solution.py:499
  (8 other events, 152.8 us)

commit v4 on v3

--- a/solution.py
+++ b/solution.py
@@ -272,13 +272,7 @@
     )(*row_blocks, *kept, gate_weight, up_weight, down_weight)
 
 
-def side_kernel(
-    rows_ref, router_hbm, own_ids_ref, other_ids_ref, code_ref, qkv_hbm, q_ref, kv_ref, routes_ref, router_ref,
-    qkv, sems
-):
-    copy = pltpu.make_async_copy(qkv_hbm, qkv, sems.at[1])
-    copy.start()
-    fetch([(router_hbm, router_ref)], sems)
+def routes_kernel(rows_ref, router_ref, own_ids_ref, other_ids_ref, code_ref, routes_ref):
     logits = lax.dot_general(
         router_ref[...],
         rows_ref[...].astype(jnp.float32),
@@ -299,41 +293,52 @@
         table = jnp.where(line == j + 1, code_ref[j : j + 1, :].astype(jnp.float32), table)
     routes_ref[...] = jnp.transpose(table)
 
+
+def route_table(rows, router, own_ids, other_ids, code):
+    vmem = pl.BlockSpec(memory_space=pltpu.VMEM)
+    return pl.pallas_call(
+        routes_kernel,
+        in_specs=[vmem] * 5,
+        out_specs=vmem,
+        out_shape=jax.ShapeDtypeStruct((rows.shape[0], 8), jnp.float32),
+        compiler_params=pltpu.CompilerParams(vmem_limit_bytes=16 * MIB),
+        cost_estimate=pl.CostEstimate(
+            flops=12 * rows.size * EXPERTS, bytes_accessed=2 * rows.size, transcendentals=0
+        ),
+        name="route_table",
+    )(rows, router, own_ids, other_ids, code)
+
+
+def side_kernel(qkv_hbm, q_ref, kv_ref, qkv, sems):
+    fetch([(qkv_hbm, qkv)], sems)
+
     def unit(values):
         return (
             values / jnp.sqrt(jnp.mean(values * values, axis=0, keepdims=True) + epsilon)
         ).astype(jnp.bfloat16)
 
-    copy.wait()
     for h in range(qkv.shape[0]):
         q_ref[h] = unit(qkv[h, :HD, :].astype(jnp.float32))
         kv_ref[h, :HD, :] = unit(qkv[h, HD : 2 * HD, :].astype(jnp.float32))
         kv_ref[h, HD:, :] = qkv[h, 2 * HD :, :]
 
 
-def side(rows, router, own_ids, other_ids, code, qkv):
+def side(qkv):
     heads, _, tokens = qkv.shape
     vmem, hbm = pl.BlockSpec(memory_space=pltpu.VMEM), pl.BlockSpec(memory_space=pltpu.HBM)
     return pl.pallas_call(
         side_kernel,
-        in_specs=[vmem, hbm, vmem, vmem, vmem, hbm],
-        out_specs=[vmem] * 3,
+        in_specs=[hbm],
+        out_specs=[vmem] * 2,
         out_shape=[
             jax.ShapeDtypeStruct((heads, HD, tokens), jnp.bfloat16),
             jax.ShapeDtypeStruct((heads, 2 * HD, tokens), jnp.bfloat16),
-            jax.ShapeDtypeStruct((rows.shape[0], 8), jnp.float32),
         ],
-        scratch_shapes=[
-            pltpu.VMEM(router.shape, router.dtype),
-            pltpu.VMEM(qkv.shape, qkv.dtype),
-            pltpu.SemaphoreType.DMA((2,)),
-        ],
+        scratch_shapes=[pltpu.VMEM(qkv.shape, qkv.dtype), pltpu.SemaphoreType.DMA((1,))],
         compiler_params=pltpu.CompilerParams(vmem_limit_bytes=16 * MIB),
-        cost_estimate=pl.CostEstimate(
-            flops=6 * qkv.size + 12 * rows.size * EXPERTS, bytes_accessed=4 * qkv.size, transcendentals=0
-        ),
+        cost_estimate=pl.CostEstimate(flops=6 * qkv.size, bytes_accessed=4 * qkv.size, transcendentals=0),
         name="side",
-    )(rows, router, own_ids, other_ids, code, qkv)
+    )(qkv)
 
 
 def attend_kernel(pieces, head_ref, q_ref, *refs):
@@ -508,23 +513,26 @@
     )
     rows_a = [swap(outgoing[k // 2], k) for k in CHUNK_A]
     rows_b = [swap(outgoing[k // 2], k) for k in CHUNK_B]
-    queries, kv, routes = side(rows, router_weight.T, near_ids, other_ids, code, jnp.transpose(guide_qkv[0], (1, 2, 0)))
-    weights, _ = lax.optimization_barrier(((gate_weight, up_weight, down_weight), routes))
+    queries, kv = side(jnp.transpose(guide_qkv[0], (1, 2, 0)))
+    weights, _ = lax.optimization_barrier(((gate_weight, up_weight, down_weight), kv))
     kept = resident(*weights)
     far = swap(kv, 8)
     near = swap(kv, 4)
-    rows_a, routes, queries = lax.optimization_barrier((rows_a, routes, queries))
+    rows_a, queries = lax.optimization_barrier((rows_a, queries))
 
     done_a = ffn(rows_a, kept, gate_weight, up_weight, down_weight)
     back_a = [swap(block, k) for block, k in zip(done_a, CHUNK_A)]
 
     done_b = ffn(rows_b, kept, gate_weight, up_weight, down_weight)
-    done_b, queries, back_a, far, near = lax.optimization_barrier((done_b, queries, back_a, far, near))
+    done_b, queries, back_a, far, near, rows = lax.optimization_barrier(
+        (done_b, queries, back_a, far, near, rows)
+    )
     back_b = [swap(block, k) for block, k in zip(done_b, CHUNK_B)]
     relayed = swap(far, 4)
 
     keep, send = attend(head, queries, [kv, near, far, relayed], guide_out)
     got = swap(send, 1)
+    routes = route_table(rows, router_weight.T, near_ids, other_ids, code)
     sums = combine(back_a, [k // 2 for k in CHUNK_A], routes, (), jnp.float32)
     keep_moe, send_moe = combine(back_b, [k // 2 for k in CHUNK_B], routes, sums, jnp.bfloat16)
     got_moe = swap(send_moe, 1)

time: 112 us -> 112 us (level)
  no operation moved by 1% of the time
where the time goes in v4:
time: 112 us
  Pallas kernels  50.3 us (45%)
  starting transfers between devices  37.1 us (33%)
  waiting for transfers between devices  19.5 us (17%)
  local copies, waits for them, and re-layouts  3.39 us (3%)
  between operations  1.55 us (1%)
    pallas_call x2, Pallas kernels, ffn(): pl.pallas_call(functools.partial(ffn_kernel, blocks, units // tile), in_s...  37.6 us
    ppermute x21, starting transfers between devices, swap(): return lax.ppermute(block, MEMBERS, [(i, i ^ k) for i in range(devices)])  37.1 us
    ppermute x21, waiting for transfers between devices, swap(): return lax.ppermute(block, MEMBERS, [(i, i ^ k) for i in range(devices)])  19.5 us
    unnamed x22, local copies, waits for them, and re-layouts  3.39 us
    pallas_call x1, Pallas kernels, resident(): pl.pallas_call(resident_kernel, in_specs=[hbm] * 3, out_specs=[vmem] * 3,...  3.14 us
    pallas_call x2, Pallas kernels, combine(): pl.pallas_call(functools.partial(combine_kernel, chips), in_specs=[vmem]...  2.39 us
  transfers between devices with their start and end apart: 21, of which 4 were waited for; matrix products, arithmetic and copies ran while one was open for 0% of the time, Pallas kernels for 42%

profile of v4, /device:TPU:0, one launch (start us, length us, event | category | flops | bytes accessed | tf_op | source)
XLA Modules:
  0.0 111.8 jit_solution(9937963958187271412)
XLA Ops:
  3.5 1.5 %prep.1 = (bf16[256,1536]{1,0:T(8,128)(2,1)S(1)}, s32[2,256]{1,0:T(2,128)S(1)}, bf16[64,1536]{1,0:T(8,128)(2,1)S(1)}, bf16[64,1536]{1,0:T(8,128)(2,1)S(1)}, bf16...) custom-call(s32[1]{0:T(128)} %bitcast.me_ref, ...), custom_call_target="tpu_custom_call" | custom-call | flops 402653184 | bytes 1572864 | tf_op jit(solution)/shard_map/prep/pallas_call | solution.py:111
  5.0 4.1 %collective-permute-start.5 = (bf16[64,1536]{1,0:T(8,128)(2,1)S(1)}, bf16[64,1536]{1,0:T(8,128)(2,1)S(1)}, u32[]{:S(2)}, u32[]{:S(2)}) collective-permute-start(bf16[64,1536]{1,0:T(8,128)(2,1)S(1)} %get-tuple-element.75), channel_id=1, source_target_pairs={{0,8},{1,9},{2,10},{3,11},{4,12},{5,13},{6,14},{7,15},{8,0},{9,1},... | collective-permute-start | bytes 589832 | tf_op jit(solution)/shard_map/ppermute | solution.py:504
  9.1 1.3 %collective-permute-start.6 = (bf16[64,1536]{1,0:T(8,128)(2,1)S(1)}, bf16[64,1536]{1,0:T(8,128)(2,1)S(1)}, u32[]{:S(2)}, u32[]{:S(2)}) collective-permute-start(bf16[64,1536]{1,0:T(8,128)(2,1)S(1)} %get-tuple-element.76), channel_id=1, source_target_pairs={{0,12},{1,13},{2,14},{3,15},{4,8},{5,9},{6,10},{7,11},{8,4},{9,5},... | collective-permute-start | bytes 589832 | tf_op jit(solution)/shard_map/ppermute | solution.py:504
  10.7 1.5 %collective-permute-start.8 = (bf16[64,1536]{1,0:T(8,128)(2,1)S(1)}, bf16[64,1536]{1,0:T(8,128)(2,1)S(1)}, u32[]{:S(2)}, u32[]{:S(2)}) collective-permute-start(bf16[64,1536]{1,0:T(8,128)(2,1)S(1)} %get-tuple-element.78), channel_id=1, source_target_pairs={{0,2},{1,3},{2,0},{3,1},{4,6},{5,7},{6,4},{7,5},{8,10},{9,11},{10,... | collective-permute-start | bytes 589832 | tf_op jit(solution)/shard_map/ppermute | solution.py:504
  13.3 2.9 %collective-permute-start.13 = (bf16[3,128,256]{2,1,0:T(8,128)(2,1)S(1)}, bf16[3,128,256]{2,1,0:T(8,128)(2,1)S(1)}, u32[]{:S(2)}, u32[]{:S(2)}) collective-permute-start(bf16[3,128,256]{2,1,0:T(8,128)(2,1)S(1)} %get-tuple-element.64.refs_0_), channel_id=1, source_target_pairs={{0,8},{1,9},{2,10},{3,11},{4,12},{5,13},{6,14},{7,15},{8,0},{9,1},... | collective-permute-start | bytes 589832 | tf_op jit(solution)/shard_map/ppermute | solution.py:504
  16.2 3.1 %resident.1 = (bf16[1536,768]{1,0:T(8,128)(2,1)S(1)}, bf16[1536,768]{1,0:T(8,128)(2,1)S(1)}, bf16[768,1536]{1,0:T(8,128)(2,1)S(1)}) custom-call(bf16[1536,6144]{1,0:T(8,128)(2,1)} %refs_7_.3, bf16[1536,6144]{1,0:T(8,128)(2,1)} %refs_8_.3, bf16[6144,1536]{1,0:T(8,128)(2,1)} %refs_9_.3), custom_call_target="tpu_custom_call" | custom-call | bytes 7077888 | tf_op jit(solution)/shard_map/resident/pallas_call | solution.py:148
  19.4 4.5 %collective-permute-done.5.refs_0_ = bf16[64,1536]{1,0:T(8,128)(2,1)S(1)} collective-permute-done((bf16[64,1536]{1,0:T(8,128)(2,1)S(1)}, bf16[64,1536]{1,0:T(8,128)(2,1)S(1)}, u32[]{:S(2)}, u32[]{:S(2)}) %collective-permute-start.5) | collective-permute-done | bytes 196640 | tf_op jit(solution)/shard_map/ppermute | solution.py:504
  24.2 9.4 %collective-permute-start.2 = (bf16[64,1536]{1,0:T(8,128)(2,1)S(1)}, bf16[64,1536]{1,0:T(8,128)(2,1)S(1)}, u32[]{:S(2)}, u32[]{:S(2)}) collective-permute-start(bf16[64,1536]{1,0:T(8,128)(2,1)S(1)} %get-tuple-element.60), channel_id=1, source_target_pairs={{0,6},{1,7},{2,4},{3,5},{4,2},{5,3},{6,0},{7,1},{8,14},{9,15},{10,... | collective-permute-start | bytes 589832 | tf_op jit(solution)/shard_map/ppermute | solution.py:504
  33.6 1.2 %collective-permute-start.3 = (bf16[64,1536]{1,0:T(8,128)(2,1)S(1)}, bf16[64,1536]{1,0:T(8,128)(2,1)S(1)}, u32[]{:S(2)}, u32[]{:S(2)}) collective-permute-start(bf16[64,1536]{1,0:T(8,128)(2,1)S(1)} %get-tuple-element.61), channel_id=1, source_target_pairs={{0,10},{1,11},{2,8},{3,9},{4,14},{5,15},{6,12},{7,13},{8,2},{9,3},... | collective-permute-start | bytes 589832 | tf_op jit(solution)/shard_map/ppermute | solution.py:504
  34.8 1.5 %collective-permute-start.4 = (bf16[64,1536]{1,0:T(8,128)(2,1)S(1)}, bf16[64,1536]{1,0:T(8,128)(2,1)S(1)}, u32[]{:S(2)}, u32[]{:S(2)}) collective-permute-start(bf16[64,1536]{1,0:T(8,128)(2,1)S(1)} %get-tuple-element.62), channel_id=1, source_target_pairs={{0,14},{1,15},{2,12},{3,13},{4,10},{5,11},{6,8},{7,9},{8,6},{9,7},... | collective-permute-start | bytes 589832 | tf_op jit(solution)/shard_map/ppermute | solution.py:504
  36.3 18.7 %ffn.3 = (bf16[64,1536]{1,0:T(8,128)(2,1)S(1)}, bf16[64,1536]{1,0:T(8,128)(2,1)S(1)}, bf16[64,1536]{1,0:T(8,128)(2,1)S(1)}, bf16[64,1536]{1,0:T(8,128)(2,1)S(1)}) custom-call(bf16[64,1536]{1,0:T(8,128)(2,1)S(1)} %collective-permute-done.5.refs_0_, bf16[64,1536]{1,0:T(8,128)(2,1)S(1)} %collective-permute-done.6.refs_1_, ...), custom_call_target="tpu_custom_call" | custom-call | flops 14495514624 | bytes 56623104 | tf_op jit(solution)/shard_map/ffn/pallas_call | solution.py:251
  55.0 2.4 %collective-permute-start.10 = (bf16[64,1536]{1,0:T(8,128)(2,1)S(1)}, bf16[64,1536]{1,0:T(8,128)(2,1)S(1)}, u32[]{:S(2)}, u32[]{:S(2)}) collective-permute-start(bf16[64,1536]{1,0:T(8,128)(2,1)S(1)} %get-tuple-element.86), channel_id=1, source_target_pairs={{0,12},{1,13},{2,14},{3,15},{4,8},{5,9},{6,10},{7,11},{8,4},{9,5},... | collective-permute-start | bytes 589832 | tf_op jit(solution)/shard_map/ppermute | solution.py:504
  57.4 1.2 %collective-permute-start.11 = (bf16[64,1536]{1,0:T(8,128)(2,1)S(1)}, bf16[64,1536]{1,0:T(8,128)(2,1)S(1)}, u32[]{:S(2)}, u32[]{:S(2)}) collective-permute-start(bf16[64,1536]{1,0:T(8,128)(2,1)S(1)} %get-tuple-element.87), channel_id=1, source_target_pairs={{0,4},{1,5},{2,6},{3,7},{4,0},{5,1},{6,2},{7,3},{8,12},{9,13},{10,... | collective-permute-start | bytes 589832 | tf_op jit(solution)/shard_map/ppermute | solution.py:504
  59.1 1.9 %collective-permute-start.9 = (bf16[64,1536]{1,0:T(8,128)(2,1)S(1)}, bf16[64,1536]{1,0:T(8,128)(2,1)S(1)}, u32[]{:S(2)}, u32[]{:S(2)}) collective-permute-start(bf16[64,1536]{1,0:T(8,128)(2,1)S(1)} %get-tuple-element.85), channel_id=1, source_target_pairs={{0,8},{1,9},{2,10},{3,11},{4,12},{5,13},{6,14},{7,15},{8,0},{9,1},... | collective-permute-start | bytes 589832 | tf_op jit(solution)/shard_map/ppermute | solution.py:504
  61.0 18.9 %ffn.2 = (bf16[64,1536]{1,0:T(8,128)(2,1)S(1)}, bf16[64,1536]{1,0:T(8,128)(2,1)S(1)}, bf16[64,1536]{1,0:T(8,128)(2,1)S(1)}, bf16[64,1536]{1,0:T(8,128)(2,1)S(1)}) custom-call(bf16[64,1536]{1,0:T(8,128)(2,1)S(1)} %collective-permute-done.2.refs_0_, bf16[64,1536]{1,0:T(8,128)(2,1)S(1)} %collective-permute-done.3.refs_1_, ...), custom_call_target="tpu_custom_call" | custom-call | flops 14495514624 | bytes 56623104 | tf_op jit(solution)/shard_map/ffn/pallas_call | solution.py:251
  80.8 3.0 %collective-permute-start.16 = (bf16[64,1536]{1,0:T(8,128)(2,1)S(1)}, bf16[64,1536]{1,0:T(8,128)(2,1)S(1)}, u32[]{:S(2)}, u32[]{:S(2)}) collective-permute-start(bf16[64,1536]{1,0:T(8,128)(2,1)S(1)} %get-tuple-element.93), channel_id=1, source_target_pairs={{0,10},{1,11},{2,8},{3,9},{4,14},{5,15},{6,12},{7,13},{8,2},{9,3},... | collective-permute-start | bytes 589832 | tf_op jit(solution)/shard_map/ppermute | solution.py:504
  83.8 1.5 %collective-permute-start.17 = (bf16[64,1536]{1,0:T(8,128)(2,1)S(1)}, bf16[64,1536]{1,0:T(8,128)(2,1)S(1)}, u32[]{:S(2)}, u32[]{:S(2)}) collective-permute-start(bf16[64,1536]{1,0:T(8,128)(2,1)S(1)} %get-tuple-element.94), channel_id=1, source_target_pairs={{0,14},{1,15},{2,12},{3,13},{4,10},{5,11},{6,8},{7,9},{8,6},{9,7},... | collective-permute-start | bytes 589832 | tf_op jit(solution)/shard_map/ppermute | solution.py:504
  85.3 1.5 %route_table.1.routes_ref = f32[256,8]{1,0:T(8,128)S(1)} custom-call(bf16[256,1536]{1,0:T(8,128)(2,1)S(1)} %get-tuple-element.90.rows_ref, f32[16,1536]{1,0:T(8,128)S(1)} %bitcast.13, s32[1,2,128]{2,1,0:T(2,128)S(1)} %get-tuple-element.57.own_ids.own_ids_ref, s32[1,2,128]{2,1,0:T(2,128)S(1)} %collective-permute-done.other_ids.other_ids_ref, ...), custom_call_target="tpu_custom_call" | custom-call | flops 75497472 | bytes 786432 | tf_op jit(solution)/shard_map/route_table/pallas_call | solution.py:299
  86.8 1.7 %combine.2 = (f32[128,1536]{1,0:T(8,128)S(1)}, f32[128,1536]{1,0:T(8,128)S(1)}) custom-call(f32[256,8]{1,0:T(8,128)S(1)} %route_table.1.routes_ref, bf16[64,1536]{1,0:T(8,128)(2,1)S(1)} %collective-permute-done.9.refs_0_, bf16[64,1536]{1,0:T(8,128)(2,1)S(1)} %collective-permute-done.10.refs_1_, bf16[64,1536]{1,0:T(8,128)(2,1)S(1)} %collective-permute-done.11.refs_2_, ...), custom_call_target="tpu_custom_call" | custom-call | flops 402653184 | bytes 786432 | tf_op jit(solution)/shard_map/combine/pallas_call | solution.py:432
  89.3 8.5 %collective-permute-done.16.refs_1_ = bf16[64,1536]{1,0:T(8,128)(2,1)S(1)} collective-permute-done((bf16[64,1536]{1,0:T(8,128)(2,1)S(1)}, bf16[64,1536]{1,0:T(8,128)(2,1)S(1)}, u32[]{:S(2)}, u32[]{:S(2)}) %collective-permute-start.16) | collective-permute-done | bytes 196640 | tf_op jit(solution)/shard_map/ppermute | solution.py:504
  98.7 2.7 %collective-permute-start.19 = (bf16[3,128,256]{2,1,0:T(8,128)(2,1)S(1)}, bf16[3,128,256]{2,1,0:T(8,128)(2,1)S(1)}, u32[]{:S(2)}, u32[]{:S(2)}) collective-permute-start(bf16[3,128,256]{2,1,0:T(8,128)(2,1)S(1)} %collective-permute-done.13.refs_2_), channel_id=1, source_target_pairs={{0,4},{1,5},{2,6},{3,7},{4,0},{5,1},{6,2},{7,3},{8,12},{9,13},{10,... | collective-permute-start | bytes 589832 | tf_op jit(solution)/shard_map/ppermute | solution.py:504
  101.4 5.5 %collective-permute-done.19.refs_3_ = bf16[3,128,256]{2,1,0:T(8,128)(2,1)S(1)} collective-permute-done((bf16[3,128,256]{2,1,0:T(8,128)(2,1)S(1)}, bf16[3,128,256]{2,1,0:T(8,128)(2,1)S(1)}, u32[]{:S(2)}, u32[]{:S(2)}) %collective-permute-start.19) | collective-permute-done | bytes 196640 | tf_op jit(solution)/shard_map/ppermute | solution.py:504
  106.9 2.2 %attend.1 = (f32[128,384]{1,0:T(8,128)S(1)}, bf16[128,384]{1,0:T(8,128)(2,1)S(1)}) custom-call(s32[1]{0:T(128)} %bitcast.7.head_ref, bf16[3,64,256]{2,1,0:T(8,128)(2,1)S(1)} %get-tuple-element.104.q_ref, bf16[3,128,256]{2,1,0:T(8,128)(2,1)S(1)} %get-tuple-element.64.refs_0_, bf16[3,128,256]{2,1,0:T(8,128)(2,1)S(1)} %collective-permute-done.14.refs_1_, ...), custom_call_target="tpu_custom_call" | custom-call | flops 201326592 | bytes 786432 | tf_op jit(solution)/shard_map/attend/pallas_call | solution.py:380
  110.5 1.2 %finish.1 = f32[1,16,128]{2,1,0:T(8,128)} custom-call(f32[128,1536]{1,0:T(8,128)S(1)} %get-tuple-element.102.keep_moe_ref, bf16[128,1536]{1,0:T(8,128)(2,1)S(1)} %collective-permute-done.18.got_moe_ref, bf16[1,128,1536]{2,1,0:T(8,128)(2,1)S(1)} %copy-done.1, f32[3,1,1536]{2,1,0:T(1,128)S(1)} %bitcast.15, bf16[16,1536]{1,0:T(8,128)(2,1)S(1)} %bitcast.16, ...), custom_call_target="tpu_custom_call" | custom-call | flops 12582912 | bytes 1572864 | tf_op jit(solution)/shard_map/finish/pallas_call | solution.py:476
  (51 shorter events, 8.3 us)
Async XLA Ops:
  0.0 3.5 %collective-permute-start.1 = (bf16[1,128,1536]{2,1,0:T(8,128)(2,1)}, bf16[1,128,1536]{2,1,0:T(8,128)(2,1)S(1)}, u32[]{:S(2)}, u32[]{:S(2)}) collective-permute-start(bf16[1,128,1536]{2,1,0:T(8,128)(2,1)} %hidden_ref.1), channel_id=1, source_target_pairs={{0,1},{1,0},{2,3},{3,2},{4,5},{5,4},{6,7},{7,6},{8,9},{9,8},{10,11... | collective-permute-start | bytes 1179656 | tf_op jit(solution)/shard_map/ppermute | solution.py:504
  0.5 3.0 %collective-permute-start = (s32[1,2,128]{2,1,0:T(2,128)}, s32[1,2,128]{2,1,0:T(2,128)S(1)}, u32[]{:S(2)}, u32[]{:S(2)}) collective-permute-start(s32[1,2,128]{2,1,0:T(2,128)} %bitcast.19), channel_id=1, source_target_pairs={{0,1},{1,0},{2,3},{3,2},{4,5},{5,4},{6,7},{7,6},{8,9},{9,8},{10,11... | collective-permute-start | bytes 3080 | tf_op jit(solution)/shard_map/ppermute | solution.py:504
  5.0 18.9 %collective-permute-start.5 = (bf16[64,1536]{1,0:T(8,128)(2,1)S(1)}, bf16[64,1536]{1,0:T(8,128)(2,1)S(1)}, u32[]{:S(2)}, u32[]{:S(2)}) collective-permute-start(bf16[64,1536]{1,0:T(8,128)(2,1)S(1)} %get-tuple-element.75), channel_id=1, source_target_pairs={{0,8},{1,9},{2,10},{3,11},{4,12},{5,13},{6,14},{7,15},{8,0},{9,1},... | collective-permute-start | bytes 589832 | tf_op jit(solution)/shard_map/ppermute | solution.py:504
  9.1 15.0 %collective-permute-start.6 = (bf16[64,1536]{1,0:T(8,128)(2,1)S(1)}, bf16[64,1536]{1,0:T(8,128)(2,1)S(1)}, u32[]{:S(2)}, u32[]{:S(2)}) collective-permute-start(bf16[64,1536]{1,0:T(8,128)(2,1)S(1)} %get-tuple-element.76), channel_id=1, source_target_pairs={{0,12},{1,13},{2,14},{3,15},{4,8},{5,9},{6,10},{7,11},{8,4},{9,5},... | collective-permute-start | bytes 589832 | tf_op jit(solution)/shard_map/ppermute | solution.py:504
  10.5 23.1 %collective-permute-start.7 = (bf16[64,1536]{1,0:T(8,128)(2,1)S(1)}, bf16[64,1536]{1,0:T(8,128)(2,1)S(1)}, u32[]{:S(2)}, u32[]{:S(2)}) collective-permute-start(bf16[64,1536]{1,0:T(8,128)(2,1)S(1)} %get-tuple-element.77), channel_id=1, source_target_pairs={{0,4},{1,5},{2,6},{3,7},{4,0},{5,1},{6,2},{7,3},{8,12},{9,13},{10,... | collective-permute-start | bytes 589832 | tf_op jit(solution)/shard_map/ppermute | solution.py:504
  10.7 24.1 %collective-permute-start.8 = (bf16[64,1536]{1,0:T(8,128)(2,1)S(1)}, bf16[64,1536]{1,0:T(8,128)(2,1)S(1)}, u32[]{:S(2)}, u32[]{:S(2)}) collective-permute-start(bf16[64,1536]{1,0:T(8,128)(2,1)S(1)} %get-tuple-element.78), channel_id=1, source_target_pairs={{0,2},{1,3},{2,0},{3,1},{4,6},{5,7},{6,4},{7,5},{8,10},{9,11},{10,... | collective-permute-start | bytes 589832 | tf_op jit(solution)/shard_map/ppermute | solution.py:504
  13.3 41.7 %collective-permute-start.13 = (bf16[3,128,256]{2,1,0:T(8,128)(2,1)S(1)}, bf16[3,128,256]{2,1,0:T(8,128)(2,1)S(1)}, u32[]{:S(2)}, u32[]{:S(2)}) collective-permute-start(bf16[3,128,256]{2,1,0:T(8,128)(2,1)S(1)} %get-tuple-element.64.refs_0_), channel_id=1, source_target_pairs={{0,8},{1,9},{2,10},{3,11},{4,12},{5,13},{6,14},{7,15},{8,0},{9,1},... | collective-permute-start | bytes 589832 | tf_op jit(solution)/shard_map/ppermute | solution.py:504
  23.9 56.0 %collective-permute-start.14 = (bf16[3,128,256]{2,1,0:T(8,128)(2,1)S(1)}, bf16[3,128,256]{2,1,0:T(8,128)(2,1)S(1)}, u32[]{:S(2)}, u32[]{:S(2)}) collective-permute-start(bf16[3,128,256]{2,1,0:T(8,128)(2,1)S(1)} %get-tuple-element.64.refs_0_), channel_id=1, source_target_pairs={{0,4},{1,5},{2,6},{3,7},{4,0},{5,1},{6,2},{7,3},{8,12},{9,13},{10,... | collective-permute-start | bytes 589832 | tf_op jit(solution)/shard_map/ppermute | solution.py:504
  24.2 33.2 %collective-permute-start.2 = (bf16[64,1536]{1,0:T(8,128)(2,1)S(1)}, bf16[64,1536]{1,0:T(8,128)(2,1)S(1)}, u32[]{:S(2)}, u32[]{:S(2)}) collective-permute-start(bf16[64,1536]{1,0:T(8,128)(2,1)S(1)} %get-tuple-element.60), channel_id=1, source_target_pairs={{0,6},{1,7},{2,4},{3,5},{4,2},{5,3},{6,0},{7,1},{8,14},{9,15},{10,... | collective-permute-start | bytes 589832 | tf_op jit(solution)/shard_map/ppermute | solution.py:504
  33.6 24.9 %collective-permute-start.3 = (bf16[64,1536]{1,0:T(8,128)(2,1)S(1)}, bf16[64,1536]{1,0:T(8,128)(2,1)S(1)}, u32[]{:S(2)}, u32[]{:S(2)}) collective-permute-start(bf16[64,1536]{1,0:T(8,128)(2,1)S(1)} %get-tuple-element.61), channel_id=1, source_target_pairs={{0,10},{1,11},{2,8},{3,9},{4,14},{5,15},{6,12},{7,13},{8,2},{9,3},... | collective-permute-start | bytes 589832 | tf_op jit(solution)/shard_map/ppermute | solution.py:504
  34.8 24.3 %collective-permute-start.4 = (bf16[64,1536]{1,0:T(8,128)(2,1)S(1)}, bf16[64,1536]{1,0:T(8,128)(2,1)S(1)}, u32[]{:S(2)}, u32[]{:S(2)}) collective-permute-start(bf16[64,1536]{1,0:T(8,128)(2,1)S(1)} %get-tuple-element.62), channel_id=1, source_target_pairs={{0,14},{1,15},{2,12},{3,13},{4,10},{5,11},{6,8},{7,9},{8,6},{9,7},... | collective-permute-start | bytes 589832 | tf_op jit(solution)/shard_map/ppermute | solution.py:504
  55.0 24.9 %collective-permute-start.10 = (bf16[64,1536]{1,0:T(8,128)(2,1)S(1)}, bf16[64,1536]{1,0:T(8,128)(2,1)S(1)}, u32[]{:S(2)}, u32[]{:S(2)}) collective-permute-start(bf16[64,1536]{1,0:T(8,128)(2,1)S(1)} %get-tuple-element.86), channel_id=1, source_target_pairs={{0,12},{1,13},{2,14},{3,15},{4,8},{5,9},{6,10},{7,11},{8,4},{9,5},... | collective-permute-start | bytes 589832 | tf_op jit(solution)/shard_map/ppermute | solution.py:504
  57.4 22.6 %collective-permute-start.11 = (bf16[64,1536]{1,0:T(8,128)(2,1)S(1)}, bf16[64,1536]{1,0:T(8,128)(2,1)S(1)}, u32[]{:S(2)}, u32[]{:S(2)}) collective-permute-start(bf16[64,1536]{1,0:T(8,128)(2,1)S(1)} %get-tuple-element.87), channel_id=1, source_target_pairs={{0,4},{1,5},{2,6},{3,7},{4,0},{5,1},{6,2},{7,3},{8,12},{9,13},{10,... | collective-permute-start | bytes 589832 | tf_op jit(solution)/shard_map/ppermute | solution.py:504
  58.5 21.4 %collective-permute-start.12 = (bf16[64,1536]{1,0:T(8,128)(2,1)S(1)}, bf16[64,1536]{1,0:T(8,128)(2,1)S(1)}, u32[]{:S(2)}, u32[]{:S(2)}) collective-permute-start(bf16[64,1536]{1,0:T(8,128)(2,1)S(1)} %get-tuple-element.88), channel_id=1, source_target_pairs={{0,2},{1,3},{2,0},{3,1},{4,6},{5,7},{6,4},{7,5},{8,10},{9,11},{10,... | collective-permute-start | bytes 589832 | tf_op jit(solution)/shard_map/ppermute | solution.py:504
  59.1 20.9 %collective-permute-start.9 = (bf16[64,1536]{1,0:T(8,128)(2,1)S(1)}, bf16[64,1536]{1,0:T(8,128)(2,1)S(1)}, u32[]{:S(2)}, u32[]{:S(2)}) collective-permute-start(bf16[64,1536]{1,0:T(8,128)(2,1)S(1)} %get-tuple-element.85), channel_id=1, source_target_pairs={{0,8},{1,9},{2,10},{3,11},{4,12},{5,13},{6,14},{7,15},{8,0},{9,1},... | collective-permute-start | bytes 589832 | tf_op jit(solution)/shard_map/ppermute | solution.py:504
  61.0 49.5 %copy-start.6 = (bf16[1536,16]{0,1:T(8,128)(2,1)S(1)}, bf16[1536,16]{0,1:T(8,128)(2,1)}, u32[]{:S(2)}) copy-start(bf16[1536,16]{0,1:T(8,128)(2,1)} %param.21) | copy-start | bytes 147460
  61.0 49.5 %copy-start.7 = (bf16[384,16]{0,1:T(8,128)(2,1)S(1)}, bf16[384,16]{0,1:T(8,128)(2,1)}, u32[]{:S(2)}) copy-start(bf16[384,16]{0,1:T(8,128)(2,1)} %param.24) | copy-start | bytes 36868
  61.0 49.5 %copy-start.8 = (f32[1,128,16]{1,2,0:T(8,128)S(1)}, f32[1,128,16]{1,2,0:T(8,128)}, u32[]{:S(2)}) copy-start(f32[1,128,16]{1,2,0:T(8,128)} %param.25) | copy-start | bytes 24580
  80.0 9.4 %collective-permute-start.15 = (bf16[64,1536]{1,0:T(8,128)(2,1)S(1)}, bf16[64,1536]{1,0:T(8,128)(2,1)S(1)}, u32[]{:S(2)}, u32[]{:S(2)}) collective-permute-start(bf16[64,1536]{1,0:T(8,128)(2,1)S(1)} %get-tuple-element.92), channel_id=1, source_target_pairs={{0,6},{1,7},{2,4},{3,5},{4,2},{5,3},{6,0},{7,1},{8,14},{9,15},{10,... | collective-permute-start | bytes 589832 | tf_op jit(solution)/shard_map/ppermute | solution.py:504
  80.8 17.0 %collective-permute-start.16 = (bf16[64,1536]{1,0:T(8,128)(2,1)S(1)}, bf16[64,1536]{1,0:T(8,128)(2,1)S(1)}, u32[]{:S(2)}, u32[]{:S(2)}) collective-permute-start(bf16[64,1536]{1,0:T(8,128)(2,1)S(1)} %get-tuple-element.93), channel_id=1, source_target_pairs={{0,10},{1,11},{2,8},{3,9},{4,14},{5,15},{6,12},{7,13},{8,2},{9,3},... | collective-permute-start | bytes 589832 | tf_op jit(solution)/shard_map/ppermute | solution.py:504
  83.8 14.1 %collective-permute-start.17 = (bf16[64,1536]{1,0:T(8,128)(2,1)S(1)}, bf16[64,1536]{1,0:T(8,128)(2,1)S(1)}, u32[]{:S(2)}, u32[]{:S(2)}) collective-permute-start(bf16[64,1536]{1,0:T(8,128)(2,1)S(1)} %get-tuple-element.94), channel_id=1, source_target_pairs={{0,14},{1,15},{2,12},{3,13},{4,10},{5,11},{6,8},{7,9},{8,6},{9,7},... | collective-permute-start | bytes 589832 | tf_op jit(solution)/shard_map/ppermute | solution.py:504
  98.6 11.9 %collective-permute-start.18 = (bf16[128,1536]{1,0:T(8,128)(2,1)S(1)}, bf16[128,1536]{1,0:T(8,128)(2,1)S(1)}, u32[]{:S(2)}, u32[]{:S(2)}) collective-permute-start(bf16[128,1536]{1,0:T(8,128)(2,1)S(1)} %get-tuple-element.103), channel_id=1, source_target_pairs={{0,1},{1,0},{2,3},{3,2},{4,5},{5,4},{6,7},{7,6},{8,9},{9,8},{10,11... | collective-permute-start | bytes 1179656 | tf_op jit(solution)/shard_map/ppermute | solution.py:504
  98.7 8.2 %collective-permute-start.19 = (bf16[3,128,256]{2,1,0:T(8,128)(2,1)S(1)}, bf16[3,128,256]{2,1,0:T(8,128)(2,1)S(1)}, u32[]{:S(2)}, u32[]{:S(2)}) collective-permute-start(bf16[3,128,256]{2,1,0:T(8,128)(2,1)S(1)} %collective-permute-done.13.refs_2_), channel_id=1, source_target_pairs={{0,4},{1,5},{2,6},{3,7},{4,0},{5,1},{6,2},{7,3},{8,12},{9,13},{10,... | collective-permute-start | bytes 589832 | tf_op jit(solution)/shard_map/ppermute | solution.py:504
  109.1 1.4 %collective-permute-start.20 = (bf16[128,384]{1,0:T(8,128)(2,1)S(1)}, bf16[128,384]{1,0:T(8,128)(2,1)S(1)}, u32[]{:S(2)}, u32[]{:S(2)}) collective-permute-start(bf16[128,384]{1,0:T(8,128)(2,1)S(1)} %get-tuple-element.108), channel_id=1, source_target_pairs={{0,1},{1,0},{2,3},{3,2},{4,5},{5,4},{6,7},{7,6},{8,9},{9,8},{10,11... | collective-permute-start | bytes 294920 | tf_op jit(solution)/shard_map/ppermute | solution.py:504
  (8 other events, 172.6 us)

commit v5 on v4

--- a/solution.py
+++ b/solution.py
@@ -21,6 +21,7 @@
 MEMBERS = ("expert", "dp", "head")
 CHUNK_A = [8, 12, 4, 2]
 CHUNK_B = [6, 10, 14, 0]
+BACK_A = [8, 12, 4]
 
 
 def layer_norm(values):
@@ -521,20 +522,25 @@
     rows_a, queries = lax.optimization_barrier((rows_a, queries))
 
     done_a = ffn(rows_a, kept, gate_weight, up_weight, down_weight)
-    back_a = [swap(block, k) for block, k in zip(done_a, CHUNK_A)]
 
     done_b = ffn(rows_b, kept, gate_weight, up_weight, down_weight)
+    back_a = [swap(block, k) if k in BACK_A else block for block, k in zip(done_a, CHUNK_A)]
     done_b, queries, back_a, far, near, rows = lax.optimization_barrier(
         (done_b, queries, back_a, far, near, rows)
     )
+    back_a = [block if k in BACK_A else swap(block, k) for block, k in zip(back_a, CHUNK_A)]
     back_b = [swap(block, k) for block, k in zip(done_b, CHUNK_B)]
     relayed = swap(far, 4)
 
     keep, send = attend(head, queries, [kv, near, far, relayed], guide_out)
     got = swap(send, 1)
     routes = route_table(rows, router_weight.T, near_ids, other_ids, code)
-    sums = combine(back_a, [k // 2 for k in CHUNK_A], routes, (), jnp.float32)
-    keep_moe, send_moe = combine(back_b, [k // 2 for k in CHUNK_B], routes, sums, jnp.bfloat16)
+    back = dict(zip(CHUNK_A + CHUNK_B, back_a + back_b))
+    late = [k for k in CHUNK_A + CHUNK_B if k not in BACK_A]
+    sums = combine([back[k] for k in BACK_A], [k // 2 for k in BACK_A], routes, (), jnp.float32)
+    keep_moe, send_moe = combine(
+        [back[k] for k in late], [k // 2 for k in late], routes, sums, jnp.bfloat16
+    )
     got_moe = swap(send_moe, 1)
     result = finish(
         keep_moe, got_moe, hidden, modulation, main_final.T, keep, got, guide_final.T,

time: 112 us -> 112 us (level)
  transfers between devices with their start and end apart: 21 -> 21, of which waited for: 4 -> 4; matrix products, arithmetic and copies ran while one was open for 0% -> 0% of each run, Pallas kernels for 42% -> 41%
where the time goes in v5:
time: 112 us
  Pallas kernels  50.4 us (45%)
  starting transfers between devices  37.1 us (33%)
  waiting for transfers between devices  19.8 us (18%)
  local copies, waits for them, and re-layouts  3.39 us (3%)
  between operations  1.55 us (1%)
    pallas_call x2, Pallas kernels, ffn(): pl.pallas_call(functools.partial(ffn_kernel, blocks, units // tile), in_s...  37.6 us
    ppermute x21, starting transfers between devices, swap(): return lax.ppermute(block, MEMBERS, [(i, i ^ k) for i in range(devices)])  37.1 us
    ppermute x21, waiting for transfers between devices, swap(): return lax.ppermute(block, MEMBERS, [(i, i ^ k) for i in range(devices)])  19.8 us
    unnamed x22, local copies, waits for them, and re-layouts  3.39 us
    pallas_call x1, Pallas kernels, resident(): pl.pallas_call(resident_kernel, in_specs=[hbm] * 3, out_specs=[vmem] * 3,...  3.14 us
    pallas_call x2, Pallas kernels, combine(): pl.pallas_call(functools.partial(combine_kernel, chips), in_specs=[vmem]...  2.5 us
  transfers between devices with their start and end apart: 21, of which 4 were waited for; matrix products, arithmetic and copies ran while one was open for 0% of the time, Pallas kernels for 41%

profile of v5, /device:TPU:0, one launch (start us, length us, event | category | flops | bytes accessed | tf_op | source)
XLA Modules:
  0.0 112.2 jit_solution(11289927999678771985)
XLA Ops:
  3.5 1.5 %prep.1 = (bf16[256,1536]{1,0:T(8,128)(2,1)S(1)}, s32[2,256]{1,0:T(2,128)S(1)}, bf16[64,1536]{1,0:T(8,128)(2,1)S(1)}, bf16[64,1536]{1,0:T(8,128)(2,1)S(1)}, bf16...) custom-call(s32[1]{0:T(128)} %bitcast.me_ref, ...), custom_call_target="tpu_custom_call" | custom-call | flops 402653184 | bytes 1572864 | tf_op jit(solution)/shard_map/prep/pallas_call | solution.py:112
  5.0 4.1 %collective-permute-start.5 = (bf16[64,1536]{1,0:T(8,128)(2,1)S(1)}, bf16[64,1536]{1,0:T(8,128)(2,1)S(1)}, u32[]{:S(2)}, u32[]{:S(2)}) collective-permute-start(bf16[64,1536]{1,0:T(8,128)(2,1)S(1)} %get-tuple-element.75), channel_id=1, source_target_pairs={{0,8},{1,9},{2,10},{3,11},{4,12},{5,13},{6,14},{7,15},{8,0},{9,1},... | collective-permute-start | bytes 589832 | tf_op jit(solution)/shard_map/ppermute | solution.py:505
  9.1 1.3 %collective-permute-start.6 = (bf16[64,1536]{1,0:T(8,128)(2,1)S(1)}, bf16[64,1536]{1,0:T(8,128)(2,1)S(1)}, u32[]{:S(2)}, u32[]{:S(2)}) collective-permute-start(bf16[64,1536]{1,0:T(8,128)(2,1)S(1)} %get-tuple-element.76), channel_id=1, source_target_pairs={{0,12},{1,13},{2,14},{3,15},{4,8},{5,9},{6,10},{7,11},{8,4},{9,5},... | collective-permute-start | bytes 589832 | tf_op jit(solution)/shard_map/ppermute | solution.py:505
  10.7 1.5 %collective-permute-start.8 = (bf16[64,1536]{1,0:T(8,128)(2,1)S(1)}, bf16[64,1536]{1,0:T(8,128)(2,1)S(1)}, u32[]{:S(2)}, u32[]{:S(2)}) collective-permute-start(bf16[64,1536]{1,0:T(8,128)(2,1)S(1)} %get-tuple-element.78), channel_id=1, source_target_pairs={{0,2},{1,3},{2,0},{3,1},{4,6},{5,7},{6,4},{7,5},{8,10},{9,11},{10,... | collective-permute-start | bytes 589832 | tf_op jit(solution)/shard_map/ppermute | solution.py:505
  13.3 2.9 %collective-permute-start.12 = (bf16[3,128,256]{2,1,0:T(8,128)(2,1)S(1)}, bf16[3,128,256]{2,1,0:T(8,128)(2,1)S(1)}, u32[]{:S(2)}, u32[]{:S(2)}) collective-permute-start(bf16[3,128,256]{2,1,0:T(8,128)(2,1)S(1)} %get-tuple-element.64.refs_0_), channel_id=1, source_target_pairs={{0,8},{1,9},{2,10},{3,11},{4,12},{5,13},{6,14},{7,15},{8,0},{9,1},... | collective-permute-start | bytes 589832 | tf_op jit(solution)/shard_map/ppermute | solution.py:505
  16.2 3.1 %resident.1 = (bf16[1536,768]{1,0:T(8,128)(2,1)S(1)}, bf16[1536,768]{1,0:T(8,128)(2,1)S(1)}, bf16[768,1536]{1,0:T(8,128)(2,1)S(1)}) custom-call(bf16[1536,6144]{1,0:T(8,128)(2,1)} %refs_7_.3, bf16[1536,6144]{1,0:T(8,128)(2,1)} %refs_8_.3, bf16[6144,1536]{1,0:T(8,128)(2,1)} %refs_9_.3), custom_call_target="tpu_custom_call" | custom-call | bytes 7077888 | tf_op jit(solution)/shard_map/resident/pallas_call | solution.py:149
  19.4 4.5 %collective-permute-done.5.refs_0_ = bf16[64,1536]{1,0:T(8,128)(2,1)S(1)} collective-permute-done((bf16[64,1536]{1,0:T(8,128)(2,1)S(1)}, bf16[64,1536]{1,0:T(8,128)(2,1)S(1)}, u32[]{:S(2)}, u32[]{:S(2)}) %collective-permute-start.5) | collective-permute-done | bytes 196640 | tf_op jit(solution)/shard_map/ppermute | solution.py:505
  24.2 9.4 %collective-permute-start.2 = (bf16[64,1536]{1,0:T(8,128)(2,1)S(1)}, bf16[64,1536]{1,0:T(8,128)(2,1)S(1)}, u32[]{:S(2)}, u32[]{:S(2)}) collective-permute-start(bf16[64,1536]{1,0:T(8,128)(2,1)S(1)} %get-tuple-element.60), channel_id=1, source_target_pairs={{0,6},{1,7},{2,4},{3,5},{4,2},{5,3},{6,0},{7,1},{8,14},{9,15},{10,... | collective-permute-start | bytes 589832 | tf_op jit(solution)/shard_map/ppermute | solution.py:505
  33.6 1.2 %collective-permute-start.3 = (bf16[64,1536]{1,0:T(8,128)(2,1)S(1)}, bf16[64,1536]{1,0:T(8,128)(2,1)S(1)}, u32[]{:S(2)}, u32[]{:S(2)}) collective-permute-start(bf16[64,1536]{1,0:T(8,128)(2,1)S(1)} %get-tuple-element.61), channel_id=1, source_target_pairs={{0,10},{1,11},{2,8},{3,9},{4,14},{5,15},{6,12},{7,13},{8,2},{9,3},... | collective-permute-start | bytes 589832 | tf_op jit(solution)/shard_map/ppermute | solution.py:505
  34.8 1.5 %collective-permute-start.4 = (bf16[64,1536]{1,0:T(8,128)(2,1)S(1)}, bf16[64,1536]{1,0:T(8,128)(2,1)S(1)}, u32[]{:S(2)}, u32[]{:S(2)}) collective-permute-start(bf16[64,1536]{1,0:T(8,128)(2,1)S(1)} %get-tuple-element.62), channel_id=1, source_target_pairs={{0,14},{1,15},{2,12},{3,13},{4,10},{5,11},{6,8},{7,9},{8,6},{9,7},... | collective-permute-start | bytes 589832 | tf_op jit(solution)/shard_map/ppermute | solution.py:505
  36.3 18.7 %ffn.3 = (bf16[64,1536]{1,0:T(8,128)(2,1)S(1)}, bf16[64,1536]{1,0:T(8,128)(2,1)S(1)}, bf16[64,1536]{1,0:T(8,128)(2,1)S(1)}, bf16[64,1536]{1,0:T(8,128)(2,1)S(1)}) custom-call(bf16[64,1536]{1,0:T(8,128)(2,1)S(1)} %collective-permute-done.5.refs_0_, bf16[64,1536]{1,0:T(8,128)(2,1)S(1)} %collective-permute-done.6.refs_1_, ...), custom_call_target="tpu_custom_call" | custom-call | flops 14495514624 | bytes 56623104 | tf_op jit(solution)/shard_map/ffn/pallas_call | solution.py:252
  55.0 2.4 %collective-permute-start.10 = (bf16[64,1536]{1,0:T(8,128)(2,1)S(1)}, bf16[64,1536]{1,0:T(8,128)(2,1)S(1)}, u32[]{:S(2)}, u32[]{:S(2)}) collective-permute-start(bf16[64,1536]{1,0:T(8,128)(2,1)S(1)} %get-tuple-element.86), channel_id=1, source_target_pairs={{0,12},{1,13},{2,14},{3,15},{4,8},{5,9},{6,10},{7,11},{8,4},{9,5},... | collective-permute-start | bytes 589832 | tf_op jit(solution)/shard_map/ppermute | solution.py:505
  59.5 18.9 %ffn.2 = (bf16[64,1536]{1,0:T(8,128)(2,1)S(1)}, bf16[64,1536]{1,0:T(8,128)(2,1)S(1)}, bf16[64,1536]{1,0:T(8,128)(2,1)S(1)}, bf16[64,1536]{1,0:T(8,128)(2,1)S(1)}) custom-call(bf16[64,1536]{1,0:T(8,128)(2,1)S(1)} %collective-permute-done.2.refs_0_, bf16[64,1536]{1,0:T(8,128)(2,1)S(1)} %collective-permute-done.3.refs_1_, ...), custom_call_target="tpu_custom_call" | custom-call | flops 14495514624 | bytes 56623104 | tf_op jit(solution)/shard_map/ffn/pallas_call | solution.py:252
  78.5 1.6 %collective-permute-start.14 = (bf16[64,1536]{1,0:T(8,128)(2,1)S(1)}, bf16[64,1536]{1,0:T(8,128)(2,1)S(1)}, u32[]{:S(2)}, u32[]{:S(2)}) collective-permute-start(bf16[64,1536]{1,0:T(8,128)(2,1)S(1)} %get-tuple-element.92), channel_id=1, source_target_pairs={{0,2},{1,3},{2,0},{3,1},{4,6},{5,7},{6,4},{7,5},{8,10},{9,11},{10,... | collective-permute-start | bytes 589832 | tf_op jit(solution)/shard_map/ppermute | solution.py:505
  80.8 3.0 %collective-permute-start.16 = (bf16[64,1536]{1,0:T(8,128)(2,1)S(1)}, bf16[64,1536]{1,0:T(8,128)(2,1)S(1)}, u32[]{:S(2)}, u32[]{:S(2)}) collective-permute-start(bf16[64,1536]{1,0:T(8,128)(2,1)S(1)} %get-tuple-element.94), channel_id=1, source_target_pairs={{0,10},{1,11},{2,8},{3,9},{4,14},{5,15},{6,12},{7,13},{8,2},{9,3},... | collective-permute-start | bytes 589832 | tf_op jit(solution)/shard_map/ppermute | solution.py:505
  83.8 1.5 %collective-permute-start.17 = (bf16[64,1536]{1,0:T(8,128)(2,1)S(1)}, bf16[64,1536]{1,0:T(8,128)(2,1)S(1)}, u32[]{:S(2)}, u32[]{:S(2)}) collective-permute-start(bf16[64,1536]{1,0:T(8,128)(2,1)S(1)} %get-tuple-element.95), channel_id=1, source_target_pairs={{0,14},{1,15},{2,12},{3,13},{4,10},{5,11},{6,8},{7,9},{8,6},{9,7},... | collective-permute-start | bytes 589832 | tf_op jit(solution)/shard_map/ppermute | solution.py:505
  85.3 1.5 %route_table.1.routes_ref = f32[256,8]{1,0:T(8,128)S(1)} custom-call(bf16[256,1536]{1,0:T(8,128)(2,1)S(1)} %get-tuple-element.90.rows_ref, f32[16,1536]{1,0:T(8,128)S(1)} %bitcast.13, s32[1,2,128]{2,1,0:T(2,128)S(1)} %get-tuple-element.57.own_ids.own_ids_ref, s32[1,2,128]{2,1,0:T(2,128)S(1)} %collective-permute-done.other_ids.other_ids_ref, ...), custom_call_target="tpu_custom_call" | custom-call | flops 75497472 | bytes 786432 | tf_op jit(solution)/shard_map/route_table/pallas_call | solution.py:300
  86.8 1.4 %combine.2 = (f32[128,1536]{1,0:T(8,128)S(1)}, f32[128,1536]{1,0:T(8,128)S(1)}) custom-call(f32[256,8]{1,0:T(8,128)S(1)} %route_table.1.routes_ref, bf16[64,1536]{1,0:T(8,128)(2,1)S(1)} %collective-permute-done.9.refs_0_, bf16[64,1536]{1,0:T(8,128)(2,1)S(1)} %collective-permute-done.10.refs_1_, bf16[64,1536]{1,0:T(8,128)(2,1)S(1)} %collective-permute-done.11.refs_2_), custom_call_target="tpu_custom_call" | custom-call | flops 301989888 | bytes 589824 | tf_op jit(solution)/shard_map/combine/pallas_call | solution.py:433
  88.2 6.7 %collective-permute-done.14.refs_0_ = bf16[64,1536]{1,0:T(8,128)(2,1)S(1)} collective-permute-done((bf16[64,1536]{1,0:T(8,128)(2,1)S(1)}, bf16[64,1536]{1,0:T(8,128)(2,1)S(1)}, u32[]{:S(2)}, u32[]{:S(2)}) %collective-permute-start.14) | collective-permute-done | bytes 196640 | tf_op jit(solution)/shard_map/ppermute | solution.py:505
  94.9 3.0 %collective-permute-done.16.refs_2_ = bf16[64,1536]{1,0:T(8,128)(2,1)S(1)} collective-permute-done((bf16[64,1536]{1,0:T(8,128)(2,1)S(1)}, bf16[64,1536]{1,0:T(8,128)(2,1)S(1)}, u32[]{:S(2)}, u32[]{:S(2)}) %collective-permute-start.16) | collective-permute-done | bytes 196640 | tf_op jit(solution)/shard_map/ppermute | solution.py:505
  99.1 2.7 %collective-permute-start.19 = (bf16[3,128,256]{2,1,0:T(8,128)(2,1)S(1)}, bf16[3,128,256]{2,1,0:T(8,128)(2,1)S(1)}, u32[]{:S(2)}, u32[]{:S(2)}) collective-permute-start(bf16[3,128,256]{2,1,0:T(8,128)(2,1)S(1)} %collective-permute-done.12.refs_2_), channel_id=1, source_target_pairs={{0,4},{1,5},{2,6},{3,7},{4,0},{5,1},{6,2},{7,3},{8,12},{9,13},{10,... | collective-permute-start | bytes 589832 | tf_op jit(solution)/shard_map/ppermute | solution.py:505
  101.8 5.5 %collective-permute-done.19.refs_3_ = bf16[3,128,256]{2,1,0:T(8,128)(2,1)S(1)} collective-permute-done((bf16[3,128,256]{2,1,0:T(8,128)(2,1)S(1)}, bf16[3,128,256]{2,1,0:T(8,128)(2,1)S(1)}, u32[]{:S(2)}, u32[]{:S(2)}) %collective-permute-start.19) | collective-permute-done | bytes 196640 | tf_op jit(solution)/shard_map/ppermute | solution.py:505
  107.3 2.2 %attend.1 = (f32[128,384]{1,0:T(8,128)S(1)}, bf16[128,384]{1,0:T(8,128)(2,1)S(1)}) custom-call(s32[1]{0:T(128)} %bitcast.7.head_ref, bf16[3,64,256]{2,1,0:T(8,128)(2,1)S(1)} %get-tuple-element.104.q_ref, bf16[3,128,256]{2,1,0:T(8,128)(2,1)S(1)} %get-tuple-element.64.refs_0_, bf16[3,128,256]{2,1,0:T(8,128)(2,1)S(1)} %collective-permute-done.13.refs_1_, ...), custom_call_target="tpu_custom_call" | custom-call | flops 201326592 | bytes 786432 | tf_op jit(solution)/shard_map/attend/pallas_call | solution.py:381
  111.0 1.2 %finish.1 = f32[1,16,128]{2,1,0:T(8,128)} custom-call(f32[128,1536]{1,0:T(8,128)S(1)} %get-tuple-element.102.keep_moe_ref, bf16[128,1536]{1,0:T(8,128)(2,1)S(1)} %collective-permute-done.18.got_moe_ref, bf16[1,128,1536]{2,1,0:T(8,128)(2,1)S(1)} %copy-done.1, f32[3,1,1536]{2,1,0:T(1,128)S(1)} %bitcast.15, bf16[16,1536]{1,0:T(8,128)(2,1)S(1)} %bitcast.16, ...), custom_call_target="tpu_custom_call" | custom-call | flops 12582912 | bytes 1572864 | tf_op jit(solution)/shard_map/finish/pallas_call | solution.py:477
  (51 shorter events, 9.3 us)
Async XLA Ops:
  0.0 3.5 %collective-permute-start.1 = (bf16[1,128,1536]{2,1,0:T(8,128)(2,1)}, bf16[1,128,1536]{2,1,0:T(8,128)(2,1)S(1)}, u32[]{:S(2)}, u32[]{:S(2)}) collective-permute-start(bf16[1,128,1536]{2,1,0:T(8,128)(2,1)} %hidden_ref.1), channel_id=1, source_target_pairs={{0,1},{1,0},{2,3},{3,2},{4,5},{5,4},{6,7},{7,6},{8,9},{9,8},{10,11... | collective-permute-start | bytes 1179656 | tf_op jit(solution)/shard_map/ppermute | solution.py:505
  0.5 3.0 %collective-permute-start = (s32[1,2,128]{2,1,0:T(2,128)}, s32[1,2,128]{2,1,0:T(2,128)S(1)}, u32[]{:S(2)}, u32[]{:S(2)}) collective-permute-start(s32[1,2,128]{2,1,0:T(2,128)} %bitcast.19), channel_id=1, source_target_pairs={{0,1},{1,0},{2,3},{3,2},{4,5},{5,4},{6,7},{7,6},{8,9},{9,8},{10,11... | collective-permute-start | bytes 3080 | tf_op jit(solution)/shard_map/ppermute | solution.py:505
  5.0 18.9 %collective-permute-start.5 = (bf16[64,1536]{1,0:T(8,128)(2,1)S(1)}, bf16[64,1536]{1,0:T(8,128)(2,1)S(1)}, u32[]{:S(2)}, u32[]{:S(2)}) collective-permute-start(bf16[64,1536]{1,0:T(8,128)(2,1)S(1)} %get-tuple-element.75), channel_id=1, source_target_pairs={{0,8},{1,9},{2,10},{3,11},{4,12},{5,13},{6,14},{7,15},{8,0},{9,1},... | collective-permute-start | bytes 589832 | tf_op jit(solution)/shard_map/ppermute | solution.py:505
  9.1 15.0 %collective-permute-start.6 = (bf16[64,1536]{1,0:T(8,128)(2,1)S(1)}, bf16[64,1536]{1,0:T(8,128)(2,1)S(1)}, u32[]{:S(2)}, u32[]{:S(2)}) collective-permute-start(bf16[64,1536]{1,0:T(8,128)(2,1)S(1)} %get-tuple-element.76), channel_id=1, source_target_pairs={{0,12},{1,13},{2,14},{3,15},{4,8},{5,9},{6,10},{7,11},{8,4},{9,5},... | collective-permute-start | bytes 589832 | tf_op jit(solution)/shard_map/ppermute | solution.py:505
  10.5 23.1 %collective-permute-start.7 = (bf16[64,1536]{1,0:T(8,128)(2,1)S(1)}, bf16[64,1536]{1,0:T(8,128)(2,1)S(1)}, u32[]{:S(2)}, u32[]{:S(2)}) collective-permute-start(bf16[64,1536]{1,0:T(8,128)(2,1)S(1)} %get-tuple-element.77), channel_id=1, source_target_pairs={{0,4},{1,5},{2,6},{3,7},{4,0},{5,1},{6,2},{7,3},{8,12},{9,13},{10,... | collective-permute-start | bytes 589832 | tf_op jit(solution)/shard_map/ppermute | solution.py:505
  10.7 24.1 %collective-permute-start.8 = (bf16[64,1536]{1,0:T(8,128)(2,1)S(1)}, bf16[64,1536]{1,0:T(8,128)(2,1)S(1)}, u32[]{:S(2)}, u32[]{:S(2)}) collective-permute-start(bf16[64,1536]{1,0:T(8,128)(2,1)S(1)} %get-tuple-element.78), channel_id=1, source_target_pairs={{0,2},{1,3},{2,0},{3,1},{4,6},{5,7},{6,4},{7,5},{8,10},{9,11},{10,... | collective-permute-start | bytes 589832 | tf_op jit(solution)/shard_map/ppermute | solution.py:505
  13.3 65.1 %collective-permute-start.12 = (bf16[3,128,256]{2,1,0:T(8,128)(2,1)S(1)}, bf16[3,128,256]{2,1,0:T(8,128)(2,1)S(1)}, u32[]{:S(2)}, u32[]{:S(2)}) collective-permute-start(bf16[3,128,256]{2,1,0:T(8,128)(2,1)S(1)} %get-tuple-element.64.refs_0_), channel_id=1, source_target_pairs={{0,8},{1,9},{2,10},{3,11},{4,12},{5,13},{6,14},{7,15},{8,0},{9,1},... | collective-permute-start | bytes 589832 | tf_op jit(solution)/shard_map/ppermute | solution.py:505
  23.9 54.5 %collective-permute-start.13 = (bf16[3,128,256]{2,1,0:T(8,128)(2,1)S(1)}, bf16[3,128,256]{2,1,0:T(8,128)(2,1)S(1)}, u32[]{:S(2)}, u32[]{:S(2)}) collective-permute-start(bf16[3,128,256]{2,1,0:T(8,128)(2,1)S(1)} %get-tuple-element.64.refs_0_), channel_id=1, source_target_pairs={{0,4},{1,5},{2,6},{3,7},{4,0},{5,1},{6,2},{7,3},{8,12},{9,13},{10,... | collective-permute-start | bytes 589832 | tf_op jit(solution)/shard_map/ppermute | solution.py:505
  24.2 30.8 %collective-permute-start.2 = (bf16[64,1536]{1,0:T(8,128)(2,1)S(1)}, bf16[64,1536]{1,0:T(8,128)(2,1)S(1)}, u32[]{:S(2)}, u32[]{:S(2)}) collective-permute-start(bf16[64,1536]{1,0:T(8,128)(2,1)S(1)} %get-tuple-element.60), channel_id=1, source_target_pairs={{0,6},{1,7},{2,4},{3,5},{4,2},{5,3},{6,0},{7,1},{8,14},{9,15},{10,... | collective-permute-start | bytes 589832 | tf_op jit(solution)/shard_map/ppermute | solution.py:505
  33.6 23.8 %collective-permute-start.3 = (bf16[64,1536]{1,0:T(8,128)(2,1)S(1)}, bf16[64,1536]{1,0:T(8,128)(2,1)S(1)}, u32[]{:S(2)}, u32[]{:S(2)}) collective-permute-start(bf16[64,1536]{1,0:T(8,128)(2,1)S(1)} %get-tuple-element.61), channel_id=1, source_target_pairs={{0,10},{1,11},{2,8},{3,9},{4,14},{5,15},{6,12},{7,13},{8,2},{9,3},... | collective-permute-start | bytes 589832 | tf_op jit(solution)/shard_map/ppermute | solution.py:505
  34.8 23.8 %collective-permute-start.4 = (bf16[64,1536]{1,0:T(8,128)(2,1)S(1)}, bf16[64,1536]{1,0:T(8,128)(2,1)S(1)}, u32[]{:S(2)}, u32[]{:S(2)}) collective-permute-start(bf16[64,1536]{1,0:T(8,128)(2,1)S(1)} %get-tuple-element.62), channel_id=1, source_target_pairs={{0,14},{1,15},{2,12},{3,13},{4,10},{5,11},{6,8},{7,9},{8,6},{9,7},... | collective-permute-start | bytes 589832 | tf_op jit(solution)/shard_map/ppermute | solution.py:505
  55.0 23.4 %collective-permute-start.10 = (bf16[64,1536]{1,0:T(8,128)(2,1)S(1)}, bf16[64,1536]{1,0:T(8,128)(2,1)S(1)}, u32[]{:S(2)}, u32[]{:S(2)}) collective-permute-start(bf16[64,1536]{1,0:T(8,128)(2,1)S(1)} %get-tuple-element.86), channel_id=1, source_target_pairs={{0,12},{1,13},{2,14},{3,15},{4,8},{5,9},{6,10},{7,11},{8,4},{9,5},... | collective-permute-start | bytes 589832 | tf_op jit(solution)/shard_map/ppermute | solution.py:505
  57.4 21.1 %collective-permute-start.11 = (bf16[64,1536]{1,0:T(8,128)(2,1)S(1)}, bf16[64,1536]{1,0:T(8,128)(2,1)S(1)}, u32[]{:S(2)}, u32[]{:S(2)}) collective-permute-start(bf16[64,1536]{1,0:T(8,128)(2,1)S(1)} %get-tuple-element.87), channel_id=1, source_target_pairs={{0,4},{1,5},{2,6},{3,7},{4,0},{5,1},{6,2},{7,3},{8,12},{9,13},{10,... | collective-permute-start | bytes 589832 | tf_op jit(solution)/shard_map/ppermute | solution.py:505
  58.5 19.9 %collective-permute-start.9 = (bf16[64,1536]{1,0:T(8,128)(2,1)S(1)}, bf16[64,1536]{1,0:T(8,128)(2,1)S(1)}, u32[]{:S(2)}, u32[]{:S(2)}) collective-permute-start(bf16[64,1536]{1,0:T(8,128)(2,1)S(1)} %get-tuple-element.85), channel_id=1, source_target_pairs={{0,8},{1,9},{2,10},{3,11},{4,12},{5,13},{6,14},{7,15},{8,0},{9,1},... | collective-permute-start | bytes 589832 | tf_op jit(solution)/shard_map/ppermute | solution.py:505
  59.5 51.4 %copy-start.6 = (bf16[1536,16]{0,1:T(8,128)(2,1)S(1)}, bf16[1536,16]{0,1:T(8,128)(2,1)}, u32[]{:S(2)}) copy-start(bf16[1536,16]{0,1:T(8,128)(2,1)} %param.21) | copy-start | bytes 147460
  59.5 51.4 %copy-start.7 = (bf16[384,16]{0,1:T(8,128)(2,1)S(1)}, bf16[384,16]{0,1:T(8,128)(2,1)}, u32[]{:S(2)}) copy-start(bf16[384,16]{0,1:T(8,128)(2,1)} %param.24) | copy-start | bytes 36868
  59.5 51.4 %copy-start.8 = (f32[1,128,16]{1,2,0:T(8,128)S(1)}, f32[1,128,16]{1,2,0:T(8,128)}, u32[]{:S(2)}) copy-start(f32[1,128,16]{1,2,0:T(8,128)} %param.25) | copy-start | bytes 24580
  78.5 16.4 %collective-permute-start.14 = (bf16[64,1536]{1,0:T(8,128)(2,1)S(1)}, bf16[64,1536]{1,0:T(8,128)(2,1)S(1)}, u32[]{:S(2)}, u32[]{:S(2)}) collective-permute-start(bf16[64,1536]{1,0:T(8,128)(2,1)S(1)} %get-tuple-element.92), channel_id=1, source_target_pairs={{0,2},{1,3},{2,0},{3,1},{4,6},{5,7},{6,4},{7,5},{8,10},{9,11},{10,... | collective-permute-start | bytes 589832 | tf_op jit(solution)/shard_map/ppermute | solution.py:505
  80.0 14.9 %collective-permute-start.15 = (bf16[64,1536]{1,0:T(8,128)(2,1)S(1)}, bf16[64,1536]{1,0:T(8,128)(2,1)S(1)}, u32[]{:S(2)}, u32[]{:S(2)}) collective-permute-start(bf16[64,1536]{1,0:T(8,128)(2,1)S(1)} %get-tuple-element.93), channel_id=1, source_target_pairs={{0,6},{1,7},{2,4},{3,5},{4,2},{5,3},{6,0},{7,1},{8,14},{9,15},{10,... | collective-permute-start | bytes 589832 | tf_op jit(solution)/shard_map/ppermute | solution.py:505
  80.8 17.1 %collective-permute-start.16 = (bf16[64,1536]{1,0:T(8,128)(2,1)S(1)}, bf16[64,1536]{1,0:T(8,128)(2,1)S(1)}, u32[]{:S(2)}, u32[]{:S(2)}) collective-permute-start(bf16[64,1536]{1,0:T(8,128)(2,1)S(1)} %get-tuple-element.94), channel_id=1, source_target_pairs={{0,10},{1,11},{2,8},{3,9},{4,14},{5,15},{6,12},{7,13},{8,2},{9,3},... | collective-permute-start | bytes 589832 | tf_op jit(solution)/shard_map/ppermute | solution.py:505
  83.8 14.1 %collective-permute-start.17 = (bf16[64,1536]{1,0:T(8,128)(2,1)S(1)}, bf16[64,1536]{1,0:T(8,128)(2,1)S(1)}, u32[]{:S(2)}, u32[]{:S(2)}) collective-permute-start(bf16[64,1536]{1,0:T(8,128)(2,1)S(1)} %get-tuple-element.95), channel_id=1, source_target_pairs={{0,14},{1,15},{2,12},{3,13},{4,10},{5,11},{6,8},{7,9},{8,6},{9,7},... | collective-permute-start | bytes 589832 | tf_op jit(solution)/shard_map/ppermute | solution.py:505
  99.0 11.9 %collective-permute-start.18 = (bf16[128,1536]{1,0:T(8,128)(2,1)S(1)}, bf16[128,1536]{1,0:T(8,128)(2,1)S(1)}, u32[]{:S(2)}, u32[]{:S(2)}) collective-permute-start(bf16[128,1536]{1,0:T(8,128)(2,1)S(1)} %get-tuple-element.103), channel_id=1, source_target_pairs={{0,1},{1,0},{2,3},{3,2},{4,5},{5,4},{6,7},{7,6},{8,9},{9,8},{10,11... | collective-permute-start | bytes 1179656 | tf_op jit(solution)/shard_map/ppermute | solution.py:505
  99.1 8.2 %collective-permute-start.19 = (bf16[3,128,256]{2,1,0:T(8,128)(2,1)S(1)}, bf16[3,128,256]{2,1,0:T(8,128)(2,1)S(1)}, u32[]{:S(2)}, u32[]{:S(2)}) collective-permute-start(bf16[3,128,256]{2,1,0:T(8,128)(2,1)S(1)} %collective-permute-done.12.refs_2_), channel_id=1, source_target_pairs={{0,4},{1,5},{2,6},{3,7},{4,0},{5,1},{6,2},{7,3},{8,12},{9,13},{10,... | collective-permute-start | bytes 589832 | tf_op jit(solution)/shard_map/ppermute | solution.py:505
  109.5 1.4 %collective-permute-start.20 = (bf16[128,384]{1,0:T(8,128)(2,1)S(1)}, bf16[128,384]{1,0:T(8,128)(2,1)S(1)}, u32[]{:S(2)}, u32[]{:S(2)}) collective-permute-start(bf16[128,384]{1,0:T(8,128)(2,1)S(1)} %get-tuple-element.108), channel_id=1, source_target_pairs={{0,1},{1,0},{2,3},{3,2},{4,5},{5,4},{6,7},{7,6},{8,9},{9,8},{10,11... | collective-permute-start | bytes 294920 | tf_op jit(solution)/shard_map/ppermute | solution.py:505
  (8 other events, 179.9 us)
